TPU v7x, 32 devices: a whole 2x2x4 slice. The times are simulated.
32 devices in a mesh: dp: 4 (over y, x), expert: 8 (over z, core).
Axes of the slice: x: 2, y: 2, z: 4, core: 2. Of those that a mesh axis runs over, the one named last changes fastest.
Arguments:
- inputs: bfloat16 [32768, 768], P(('dp', 'expert')), may hold values from -6 to 6
- cotangent: bfloat16 [32768, 768], P(('dp', 'expert')), may hold values from -6 to 6
- seq_group: int32 [32], P(('dp', 'expert')), may hold values from 0 to 7
- domain_counts: int32 [8], replicated, may hold values from 1 to 8
- sort_order: int32 [32, 1024], P(('dp', 'expert')), may hold values from 0 to 1023, each once within a row
- send_counts: int32 [32, 8], P(('dp', 'expert')), may hold values from 0 to 256, as said below
- gain_one: float32 [768], replicated, may hold values from 0.5 to 1.5
- shift_one: float32 [768], replicated, may hold values from -1.2 to 1.2
- gain_two: float32 [768], replicated, may hold values from 0.5 to 1.5
- shift_two: float32 [768], replicated, may hold values from -1.2 to 1.2
- w_query: bfloat16 [768, 768], replicated, may hold values from -0.3125 to 0.3125
- w_key: bfloat16 [768, 768], replicated, may hold values from -0.3125 to 0.3125
- w_value: bfloat16 [768, 768], replicated, may hold values from -0.21875 to 0.21875
- w_out: bfloat16 [768, 768], replicated, may hold values from -0.875 to 0.875
- router: bfloat16 [768, 8], replicated, may hold values from -0.15625 to 0.15625
- expert_in: bfloat16 [8, 768, 3072], P('expert'), may hold values from -0.21875 to 0.21875
- expert_out: bfloat16 [8, 3072, 768], P('expert'), may hold values from -0.3125 to 0.3125
Outputs:
- output: bfloat16 [32768, 768], P(('dp', 'expert'))
- grad_inputs: bfloat16 [32768, 768], P(('dp', 'expert'))
- grad_gain_one: float32 [768], replicated
- grad_shift_one: float32 [768], replicated
- grad_gain_two: float32 [768], replicated
- grad_shift_two: float32 [768], replicated
- grad_w_query: float32 [768, 768], replicated
- grad_w_key: float32 [768, 768], replicated
- grad_w_value: float32 [768, 768], replicated
- grad_w_out: float32 [768, 768], replicated
- grad_expert_in: float32 [8, 768, 3072], P('expert')
- grad_expert_out: float32 [8, 3072, 768], P('expert')
Inputs may be any that keep to these rules, and one draw needn't show every extreme that they name: `send_counts`: each row sums to 1024. One expert, the same in every row, gets exactly 256 tokens from every device; in each row one other expert gets none and the rest get between 64 and 192. `sort_order`: each row is a permutation of the local token indices.
All inputs are finite; a program needn't handle non-finite values.
Results may differ from a plain program's by a relative error of at most 0.015.
The roundings to bfloat16 on the way count: a program that leaves them out, or rounds other values in their place, can miss the bound.
Values may be sent and summed in bfloat16 or wider, within the bound.
A program may use at most 256 MiB of HBM per device.

v0:
```python
import jax
import jax.numpy as jnp
from jax import lax
from jax.sharding import PartitionSpec as P

HEADS = 12
HEAD_DIM = 64
LEN = 1024


epsilon = 1e-05


def layer_norm(values_in, scales, offsets):
    center = values_in - jnp.mean(values_in, axis=-1, keepdims=True)
    spread = jnp.mean(center * center, axis=-1, keepdims=True)
    return center * lax.rsqrt(spread + epsilon) * scales + offsets


def exact_gelu(pre_act):
    return jax.nn.gelu(pre_act, approximate=False)


def local(
    inputs,
    cotangent,
    seq_group,
    domain_counts,
    sort_order,
    send_counts,
    gain_one,
    shift_one,
    gain_two,
    shift_two,
    w_query,
    w_key,
    w_value,
    w_out,
    router,
    expert_in,
    expert_out,
):
    tok_rows, model_width = inputs.shape
    seq_count = tok_rows // LEN
    experts_total = send_counts.shape[1]
    capacity = 2 * tok_rows // experts_total
    senders = lax.axis_size("expert")
    scale_factor = HEAD_DIM ** (-0.5)
    counts_row = send_counts[0]
    count_ends = jnp.cumsum(counts_row)
    count_starts = count_ends - counts_row
    places = jnp.arange(tok_rows, dtype=jnp.int32)
    expert_ids = jnp.arange(experts_total, dtype=jnp.int32)
    expert_at = jnp.sum((places[:, None] >= count_ends[None, :]).astype(jnp.int32), axis=1)
    slot_at = places - jnp.sum(
        jnp.where(expert_at[:, None] == expert_ids[None, :], count_starts[None, :], 0), axis=1
    )
    dest_token = (
        jnp.zeros((tok_rows,), jnp.int32).at[sort_order[0]].set(expert_at * capacity + slot_at)
    )
    expert_token = jnp.zeros((tok_rows,), jnp.int32).at[sort_order[0]].set(expert_at)
    choose = (expert_token[:, None] == expert_ids[None, :]).astype(jnp.bfloat16)
    router_rows = jnp.einsum("te,de->td", choose, router, preferred_element_type=jnp.float32)
    inputs_f = inputs.astype(jnp.float32)
    normed_b = layer_norm(inputs_f, gain_one, shift_one).astype(jnp.bfloat16)
    query_rows = jnp.dot(normed_b, w_query, preferred_element_type=jnp.float32).astype(jnp.bfloat16)
    key_rows = jnp.dot(normed_b, w_key, preferred_element_type=jnp.float32).astype(jnp.bfloat16)
    value_rows = jnp.dot(normed_b, w_value, preferred_element_type=jnp.float32).astype(jnp.bfloat16)

    def heads_first(matrix):
        return matrix.reshape(seq_count, LEN, HEADS, HEAD_DIM).transpose(2, 0, 1, 3)

    def tokens_first(matrix):
        return matrix.transpose(1, 2, 0, 3).reshape(tok_rows, HEADS * HEAD_DIM)

    positions = jnp.arange(LEN, dtype=jnp.int32)
    causal = positions[:, None] >= positions[None, :]

    def head_scores(query_h, key_h):
        scores = (
            jnp.einsum("sqd,skd->sqk", query_h, key_h, preferred_element_type=jnp.float32)
            * scale_factor
        )
        return jnp.where(causal[None], scores, -1000000000.0)

    def head_forward(pieces):
        query_h, key_h, value_h = pieces
        scores = head_scores(query_h, key_h)
        row_peak = jnp.max(scores, axis=-1, keepdims=True)
        exp_scores = jnp.exp(scores - row_peak)
        row_total = jnp.sum(exp_scores, axis=-1, keepdims=True)
        attention = (exp_scores / row_total).astype(jnp.bfloat16)
        head_out = jnp.einsum(
            "sqk,skd->sqd", attention, value_h, preferred_element_type=jnp.float32
        )
        return (head_out.astype(jnp.bfloat16), (row_peak + jnp.log(row_total))[..., 0])

    query_heads = heads_first(query_rows)
    key_heads = heads_first(key_rows)
    value_heads = heads_first(value_rows)
    mixed_heads, log_totals = lax.map(head_forward, (query_heads, key_heads, value_heads))
    mixed_rows = tokens_first(mixed_heads)
    branch = jnp.dot(mixed_rows, w_out, preferred_element_type=jnp.float32)
    hidden = inputs_f + branch
    routed = layer_norm(hidden, gain_two, shift_two)
    routed_b = routed.astype(jnp.bfloat16)
    gate_vals = jax.nn.sigmoid(jnp.sum(routed * router_rows, axis=1))
    send_rows = (
        jnp.zeros((experts_total * capacity, model_width), jnp.bfloat16)
        .at[dest_token]
        .set(routed_b)
    )
    arrived = lax.all_to_all(
        send_rows.reshape(experts_total, capacity, model_width),
        "expert",
        split_axis=0,
        concat_axis=0,
        tiled=True,
    ).reshape(senders * capacity, model_width)
    first_weight = expert_in[0]
    second_weight = expert_out[0]
    pre_act = jnp.dot(arrived, first_weight, preferred_element_type=jnp.float32)
    act_rows = exact_gelu(pre_act).astype(jnp.bfloat16)
    expert_rows = jnp.dot(act_rows, second_weight, preferred_element_type=jnp.float32).astype(
        jnp.bfloat16
    )
    returned = lax.all_to_all(
        expert_rows.reshape(senders, capacity, model_width),
        "expert",
        split_axis=0,
        concat_axis=0,
        tiled=True,
    ).reshape(experts_total * capacity, model_width)
    back_rows = returned[dest_token].astype(jnp.float32)
    output = (hidden + gate_vals[:, None] * back_rows).astype(jnp.bfloat16)
    inverse = 1.0 / domain_counts.astype(jnp.float32)
    domain_weights = inverse / jnp.mean(inverse)
    domain_ids = jnp.arange(domain_counts.shape[0], dtype=jnp.int32)
    seq_weight = jnp.sum(
        jnp.where(seq_group[:, None] == domain_ids[None, :], domain_weights[None, :], 0.0), axis=1
    )
    grad_output = (
        cotangent.astype(jnp.float32).reshape(seq_count, LEN, model_width)
        * seq_weight[:, None, None]
    ).reshape(tok_rows, model_width)
    grad_back = (gate_vals[:, None] * grad_output).astype(jnp.bfloat16)
    grad_logit = jnp.sum(back_rows * grad_output, axis=1) * gate_vals * (1.0 - gate_vals)
    send_grads = (
        jnp.zeros((experts_total * capacity, model_width), jnp.bfloat16)
        .at[dest_token]
        .set(grad_back)
    )
    grad_arrived = lax.all_to_all(
        send_grads.reshape(experts_total, capacity, model_width),
        "expert",
        split_axis=0,
        concat_axis=0,
        tiled=True,
    ).reshape(senders * capacity, model_width)
    grad_act = jnp.einsum(
        "rd,fd->rf", grad_arrived, second_weight, preferred_element_type=jnp.float32
    )
    gelu_back = jax.vjp(exact_gelu, pre_act)[1]
    grad_pre = gelu_back(grad_act)[0].astype(jnp.bfloat16)
    grad_second = jnp.einsum(
        "rf,rd->fd", act_rows, grad_arrived, preferred_element_type=jnp.float32
    )
    grad_first = jnp.einsum("rd,rf->df", arrived, grad_pre, preferred_element_type=jnp.float32)
    grad_sent = jnp.einsum(
        "rf,df->rd", grad_pre, first_weight, preferred_element_type=jnp.float32
    ).astype(jnp.bfloat16)
    grad_returned = lax.all_to_all(
        grad_sent.reshape(senders, capacity, model_width),
        "expert",
        split_axis=0,
        concat_axis=0,
        tiled=True,
    ).reshape(experts_total * capacity, model_width)
    grad_routed = grad_returned[dest_token].astype(jnp.float32) + grad_logit[:, None] * router_rows
    norm_back_two = jax.vjp(layer_norm, hidden, gain_two, shift_two)[1]
    grad_hidden_norm, grad_gain_two, grad_shift_two = norm_back_two(grad_routed)
    grad_hidden = grad_output + grad_hidden_norm
    grad_branch = grad_hidden.astype(jnp.bfloat16)
    grad_w_out = jnp.einsum(
        "td,te->de", mixed_rows, grad_branch, preferred_element_type=jnp.float32
    )
    grad_mixed = jnp.einsum(
        "te,de->td", grad_branch, w_out, preferred_element_type=jnp.float32
    ).astype(jnp.bfloat16)

    def head_backward(pieces):
        query_h, key_h, value_h, grad_h, log_total = pieces
        attention = jnp.exp(head_scores(query_h, key_h) - log_total[..., None])
        attention_b = attention.astype(jnp.bfloat16)
        grad_value = jnp.einsum(
            "sqk,sqd->skd", attention_b, grad_h, preferred_element_type=jnp.float32
        )
        grad_attention = jnp.einsum(
            "sqd,skd->sqk", grad_h, value_h, preferred_element_type=jnp.float32
        )
        row_delta = jnp.sum(attention * grad_attention, axis=-1, keepdims=True)
        grad_scores = (attention * (grad_attention - row_delta)).astype(jnp.bfloat16)
        grad_query = (
            jnp.einsum("sqk,skd->sqd", grad_scores, key_h, preferred_element_type=jnp.float32)
            * scale_factor
        )
        grad_key = (
            jnp.einsum("sqk,sqd->skd", grad_scores, query_h, preferred_element_type=jnp.float32)
            * scale_factor
        )
        return (
            grad_query.astype(jnp.bfloat16),
            grad_key.astype(jnp.bfloat16),
            grad_value.astype(jnp.bfloat16),
        )

    grad_q_heads, grad_k_heads, grad_v_heads = lax.map(
        head_backward, (query_heads, key_heads, value_heads, heads_first(grad_mixed), log_totals)
    )
    grad_queries = tokens_first(grad_q_heads)
    grad_keys = tokens_first(grad_k_heads)
    grad_values = tokens_first(grad_v_heads)
    grad_w_query = jnp.einsum(
        "td,te->de", normed_b, grad_queries, preferred_element_type=jnp.float32
    )
    grad_w_key = jnp.einsum("td,te->de", normed_b, grad_keys, preferred_element_type=jnp.float32)
    grad_w_value = jnp.einsum(
        "td,te->de", normed_b, grad_values, preferred_element_type=jnp.float32
    )
    grad_normed = jnp.einsum("te,de->td", grad_queries, w_query, preferred_element_type=jnp.float32)
    grad_normed = grad_normed + jnp.einsum(
        "te,de->td", grad_keys, w_key, preferred_element_type=jnp.float32
    )
    grad_normed = grad_normed + jnp.einsum(
        "te,de->td", grad_values, w_value, preferred_element_type=jnp.float32
    )
    norm_back_one = jax.vjp(layer_norm, inputs_f, gain_one, shift_one)[1]
    grad_input_norm, grad_gain_one, grad_shift_one = norm_back_one(grad_normed)
    grad_inputs = (grad_hidden + grad_input_norm).astype(jnp.bfloat16)
    expert_sums = (
        lax.psum(grad_first.astype(jnp.bfloat16), "dp").astype(jnp.float32),
        lax.psum(grad_second.astype(jnp.bfloat16), "dp").astype(jnp.float32),
    )
    dense_sums = lax.psum(
        (
            grad_w_query,
            grad_w_key,
            grad_w_value,
            grad_w_out,
            grad_gain_one,
            grad_shift_one,
            grad_gain_two,
            grad_shift_two,
        ),
        ("dp", "expert"),
    )
    return (
        output,
        grad_inputs,
        dense_sums[4],
        dense_sums[5],
        dense_sums[6],
        dense_sums[7],
        dense_sums[0],
        dense_sums[1],
        dense_sums[2],
        dense_sums[3],
        expert_sums[0][None],
        expert_sums[1][None],
    )


def solution(mesh):
    return jax.shard_map(
        local,
        mesh=mesh,
        in_specs=(
            P(("dp", "expert"), None),
            P(("dp", "expert"), None),
            P(("dp", "expert")),
            P(),
            P(("dp", "expert"), None),
            P(("dp", "expert"), None),
            P(),
            P(),
            P(),
            P(),
            P(),
            P(),
            P(),
            P(),
            P(),
            P("expert", None, None),
            P("expert", None, None),
        ),
        out_specs=(
            P(("dp", "expert"), None),
            P(("dp", "expert"), None),
            P(),
            P(),
            P(),
            P(),
            P(),
            P(),
            P(),
            P(),
            P("expert", None, None),
            P("expert", None, None),
        ),
        check_vma=False,
    )
```

profile of v0, /device:TPU:0, one launch (start us, length us, event | category | flops | bytes accessed | tf_op | source)
XLA Modules:
  0.0 991.2 jit_solution(5724763379888539284)
XLA Ops:
  34.1 62.7 %while.28 = (s32[]{:T(128)}, bf16[12,1,1024,64]{2,3,1,0:T(8,128)(2,1)}, f32[12,1,1024]{2,1,0:T(1,128)}, bf16[12,1,1024,64]{3,2,1,0:T(8,128)(2,1)}, bf16[12,1,102...) while((s32[]{:T(128)}, bf16[12,1,1024,64]{2,3,1,0:T(8,128)(2,1)}, ...), condition=%wide.region_5.6_spmd.clone, body=%wide.region_2.5_spmd.clone.sunk | while | flops 284228608 | bytes 13544013 | solution.py:101
  103.0 4.5 scatter_custom_fusion
  107.5 5.1 multiply_reduce_fusion.3
  119.2 7.9 scatter_custom_fusion.2
  127.1 78.1 %all_to_all.20 = bf16[8,256,768]{2,1,0:T(8,128)(2,1)S(1)} all-to-all(bf16[8,256,768]{2,1,0:T(8,128)(2,1)} %bitcast.180), channel_id=1, replica_groups=mesh['dp'=4,'expert'=8] {'expert'}, dimensions={0} | all-to-all | bytes 6291456 | tf_op jit(solution)/shard_map/all_to_all | solution.py:113
  205.3 63.5 %multiply_convert_fusion.1 = (bf16[2048,3072]{1,0:T(8,128)(2,1)S(1)}, f32[2048,3072]{1,0:T(8,128)}, f32[2048,3072]{1,0:T(8,128)}) fusion(bf16[2048,768]{1,0:T(8,128)(2,1)S(1)} %bitcast.185, bf16[1,768,3072]{2,1,0:T(8,128)(2,1)} %param.36), kind=kOutput, calls=%fused_computation.72 | convolution fusion | flops 10072621056 | bytes 70778880 | tf_op jit(solution)/shard_map/dot_general | solution.py:122
  268.8 11.2 %fusion.82 = bf16[2048,768]{1,0:T(8,128)(2,1)} fusion(bf16[2048,3072]{1,0:T(8,128)(2,1)S(1)} %get-tuple-element.228, bf16[1,3072,768]{2,1,0:T(8,128)(2,1)S(1)} %copy-done.42), kind=kOutput, calls=%fused_computation.111 | convolution fusion | flops 9665249280 | bytes 20447232 | tf_op jit(solution)/shard_map/dot_general | solution.py:124
  280.0 4.9 all-to-all-start.1
  289.3 67.2 %all-to-all-done.1 = bf16[8,256,768]{2,1,0:T(8,128)(2,1)} async-done(((bf16[8,256,768]{2,1,0:T(8,128)(2,1)}), bf16[8,256,768]{2,1,0:T(8,128)(2,1)}, u32[]{:S(2)}, u32[]{:S(2)}) %all-to-all-start.1) | async-done | bytes 3145760 | tf_op jit(solution)/shard_map/all_to_all | solution.py:127
  356.5 7.9 gather_fusion
  373.5 7.9 scatter_custom_fusion.3
  381.3 76.2 %all_to_all.21 = bf16[8,256,768]{2,1,0:T(8,128)(2,1)} all-to-all(bf16[8,256,768]{2,1,0:T(8,128)(2,1)} %bitcast.179), channel_id=1, replica_groups=mesh['dp'=4,'expert'=8] {'expert'}, dimensions={0} | all-to-all | bytes 6291456 | tf_op jit(solution)/shard_map/all_to_all | solution.py:153
  457.5 32.8 %add_convert_fusion = bf16[2048,3072]{1,0:T(8,128)(2,1)} fusion(f32[2048,3072]{1,0:T(8,128)} %get-tuple-element.229, f32[2048,3072]{1,0:T(8,128)} %get-tuple-element.244, bf16[2048,768]{1,0:T(8,128)(2,1)} %bitcast.188, bf16[1,3072,768]{2,1,0:T(8,128)(2,1)} %param.37), kind=kOutput, calls=%fused_computation.71 | convolution fusion | flops 9751756800 | bytes 70778880 | tf_op jit(solution)/shard_map/rd,fd->rf/dot_general | solution.py:160
  490.3 15.4 %fusion.79 = bf16[2048,768]{1,0:T(8,128)(2,1)} fusion(bf16[2048,3072]{1,0:T(8,128)(2,1)} %add_convert_fusion, bf16[1,768,3072]{2,1,0:T(8,128)(2,1)} %param.36), kind=kOutput, calls=%fused_computation.110 | convolution fusion | flops 9665249280 | bytes 20447232 | tf_op jit(solution)/shard_map/rf,df->rd/dot_general | solution.py:169
  510.5 15.5 %fusion.76 = bf16[1,3072,768]{2,1,0:T(8,128)(2,1)} fusion(bf16[2048,3072]{1,0:T(8,128)(2,1)} %copy-done.49, bf16[2048,768]{1,0:T(8,128)(2,1)} %bitcast.189), kind=kOutput, calls=%fused_computation.105 | convolution fusion | flops 9666035712 | bytes 20447232 | tf_op jit(solution)/shard_map/rf,rd->fd/dot_general | solution.py:165
  526.1 14.5 %fusion.75 = bf16[1,768,3072]{2,1,0:T(8,128)(2,1)} fusion(bf16[2048,768]{1,0:T(8,128)(2,1)S(1)} %bitcast.186, bf16[2048,3072]{1,0:T(8,128)(2,1)} %add_convert_fusion), kind=kOutput, calls=%fused_computation.104 | convolution fusion | flops 9666035712 | bytes 20447232 | tf_op jit(solution)/shard_map/rd,rf->df/dot_general | solution.py:168
  541.0 40.7 %all-to-all-done.3 = bf16[8,256,768]{2,1,0:T(8,128)(2,1)} async-done(((bf16[8,256,768]{2,1,0:T(8,128)(2,1)}), bf16[8,256,768]{2,1,0:T(8,128)(2,1)}, u32[]{:S(2)}, u32[]{:S(2)}) %all-to-all-start.3) | async-done | bytes 3145760 | tf_op jit(solution)/shard_map/all_to_all | solution.py:172
  581.8 7.9 gather_fusion.1
  592.3 4.9 multiply_reduce_fusion.1
  612.4 151.4 %while.29 = (s32[]{:T(128)}, bf16[12,1,1024,64]{2,3,1,0:T(8,128)(2,1)}, bf16[12,1,1024,64]{2,3,1,0:T(8,128)(2,1)}, bf16[12,1,1024,64]{2,3,1,0:T(8,128)(2,1)}, bf...) while((s32[]{:T(128)}, ...), condition=%wide.region_23.24_spmd.clone, body=%wide.region_21.23_spmd.clone.sunk | while | flops 681901056 | bytes 33711208 | solution.py:217
  763.9 4.8 fusion.124
  801.9 40.2 %all-reduce = (f32[768]{0:T(1024)}, f32[768]{0:T(1024)}, f32[768]{0:T(1024)}, f32[768]{0:T(1024)}) all-reduce(f32[768]{0:T(1024)S(1)} %get-tuple-element.181, f32[768]{0:T(1024)S(1)} %get-tuple-element.184, f32[768]{0:T(1024)S(1)} %get-tuple-element.179, ...), channel_id=1, replica_groups=mesh['dp'=4,'expert'=8] {'dp','expert'}, use_global_device_ids=true, to_apply=%region_27.28 | all-reduce | flops 3072 | bytes 24576 | tf_op jit(solution)/shard_map/psum | solution.py:244
  842.0 7.5 broadcast_in_dim.122
  854.0 120.3 %all-reduce.6.cloned.1.call-done = (f32[768,768]{1,0:T(8,128)}, f32[768,768]{1,0:T(8,128)}, f32[768,768]{1,0:T(8,128)}, f32[768,768]{1,0:T(8,128)}) async-done(((f32[768,768]{1,0:T(8,128)}, f32[768,768]{1,0:T(8,128)}, f32[768,768]{1,0:T(8,128)}, f32[768,768]{1,0:T(8,128)}), (f32[768,768]{1,0:T(8,128)}, f32[768,768]{1,0:T(8,128)}, f32[768,768]{1,0:T(8,128)}, ...) | async-done | bytes 9437200 | tf_op jit(solution)/shard_map/psum | solution.py:244
  (311 shorter events, 335.6 us)
Async XLA Ops:
  7.2 10.6 %copy-start = (bf16[768,768]{1,0:T(8,128)(2,1)S(1)}, bf16[768,768]{1,0:T(8,128)(2,1)}, u32[]{:S(2)}) copy-start(bf16[768,768]{1,0:T(8,128)(2,1)} %param.33) | copy-start | bytes 3538948
  9.0 87.7 %copy-start.1 = (bf16[1024,768]{0,1:T(8,128)(2,1)}, bf16[1024,768]{0,1:T(8,128)(2,1)S(1)}, u32[]{:S(2)}) copy-start(bf16[1024,768]{0,1:T(8,128)(2,1)S(1)} %copy.57) | copy-start | bytes 4718596
  9.3 15.3 %copy-start.21 = (f32[1024]{0:T(1024)}, f32[1024]{0:T(1024)S(1)}, u32[]{:S(2)}) copy-start(f32[1024]{0:T(1024)S(1)} %broadcast_multiply_fusion.1) | copy-start | bytes 12292
  10.9 13.7 %copy-start.30 = (f32[1024]{0:T(1024)}, f32[1024]{0:T(1024)S(1)}, u32[]{:S(2)}) copy-start(f32[1024]{0:T(1024)S(1)} %fusion.102) | copy-start | bytes 12292
  100.0 7.5 copy-start.25
  100.1 7.5 copy-start.37
  100.1 7.5 copy-start.38
  100.1 12.6 %copy-start.19 = (f32[1024]{0:T(1024)}, f32[1024]{0:T(1024)S(1)}, u32[]{:S(2)}) copy-start(f32[1024]{0:T(1024)S(1)} %broadcast_multiply_fusion) | copy-start | bytes 12292
  102.7 10.0 %copy-start.23 = (f32[1024]{0:T(1024)}, f32[1024]{0:T(1024)S(1)}, u32[]{:S(2)}) copy-start(f32[1024]{0:T(1024)S(1)} %fusion.103) | copy-start | bytes 12292
  119.2 86.0 %copy-start.39 = (s32[1024]{0:T(1024)}, s32[1024]{0:T(1024)S(1)}, u32[]{:S(2)}) copy-start(s32[1024]{0:T(1024)S(1)} %get-tuple-element.240) | copy-start | bytes 12292
  205.3 63.5 %copy-start.13 = (bf16[8,256,768]{2,1,0:T(8,128)(2,1)}, bf16[8,256,768]{2,1,0:T(8,128)(2,1)S(1)}, u32[]{:S(2)}) copy-start(bf16[8,256,768]{2,1,0:T(8,128)(2,1)S(1)} %all_to_all.20) | copy-start | bytes 9437188
  205.3 63.5 %copy-start.42 = (bf16[1,3072,768]{2,1,0:T(8,128)(2,1)S(1)}, bf16[1,3072,768]{2,1,0:T(8,128)(2,1)}, u32[]{:S(2)}) copy-start(bf16[1,3072,768]{2,1,0:T(8,128)(2,1)} %param.37) | copy-start | bytes 14155780
  268.7 11.3 %copy-start.49 = (bf16[2048,3072]{1,0:T(8,128)(2,1)}, bf16[2048,3072]{1,0:T(8,128)(2,1)S(1)}, u32[]{:S(2)}) copy-start(bf16[2048,3072]{1,0:T(8,128)(2,1)S(1)} %get-tuple-element.228) | copy-start | bytes 37748740
  280.0 76.5 %all-to-all-start.1 = ((bf16[8,256,768]{2,1,0:T(8,128)(2,1)}), bf16[8,256,768]{2,1,0:T(8,128)(2,1)}, u32[]{:S(2)}, u32[]{:S(2)}) async-start(bf16[8,256,768]{2,1,0:T(8,128)(2,1)} %bitcast.190), calls=%async_computation.1 | async-start | bytes 6291456 | tf_op jit(solution)/shard_map/all_to_all | solution.py:127
  285.0 71.5 %copy-start.36 = (s32[1024]{0:T(1024)S(1)}, s32[1024]{0:T(1024)}, u32[]{:S(2)}) copy-start(s32[1024]{0:T(1024)} %get-tuple-element.239) | copy-start | bytes 12292
  286.7 315.2 %copy-start.8 = (bf16[1024,768]{0,1:T(8,128)(2,1)}, bf16[1024,768]{0,1:T(8,128)(2,1)S(1)}, u32[]{:S(2)}) copy-start(bf16[1024,768]{0,1:T(8,128)(2,1)S(1)} %copy.63) | copy-start | bytes 4718596
  505.8 76.0 %all-to-all-start.3 = ((bf16[8,256,768]{2,1,0:T(8,128)(2,1)}), bf16[8,256,768]{2,1,0:T(8,128)(2,1)}, u32[]{:S(2)}, u32[]{:S(2)}) async-start(bf16[8,256,768]{2,1,0:T(8,128)(2,1)} %bitcast.187), calls=%async_computation.3 | async-start | bytes 6291456 | tf_op jit(solution)/shard_map/all_to_all | solution.py:172
  510.2 331.8 %all-reduce.8.cloned.1.call-start = ((), (), s32[]{:S(2)}) async-start(), calls=%async_computation.5 | async-start | bytes 18874368 | tf_op jit(solution)/shard_map/psum | solution.py:241
  510.5 15.6 %copy-start.14 = (bf16[8,256,768]{2,1,0:T(8,128)(2,1)S(1)}, bf16[8,256,768]{2,1,0:T(8,128)(2,1)}, u32[]{:S(2)}) copy-start(bf16[8,256,768]{2,1,0:T(8,128)(2,1)} %copy-done.13) | copy-start | bytes 9437188
  540.6 433.7 %all-reduce.6.cloned.1.call-start = ((), (), s32[]{:S(2)}) async-start(), calls=%async_computation.4 | async-start | bytes 18874368 | tf_op jit(solution)/shard_map/psum | solution.py:244
  592.3 5.0 copy-start.4
  592.3 5.3 copy-start.5
  592.3 5.7 copy-start.10
  842.0 7.5 copy-start.12
  (30 other events, 88.2 us)
Sparse Core Ops, SparseCore 0:
  540.7 190.4 all-reduce.7
  782.2 192.0 all-reduce.5
where the time goes:
time: 1000 us; the launch traced here: 991 us
  matrix products  378 us (38%)
  waiting for transfers between devices  228 us (23%)
  blocking collectives  194 us (19%)
  local copies, waits for them, and re-layouts  109 us (11%)
  other arithmetic  54.5 us (5%)
  between operations  16.2 us (2%)
  starting transfers between devices  10.1 us (1%)
    psum x1, waiting for transfers between devices, local(): lax.psum((grad_w_query, grad_w_key, grad_w_value, grad_w_out, grad_gain_o...  120 us
    all_to_all x1, blocking collectives, local(): lax.all_to_all(send_rows.reshape(experts_total, capacity, model_width), '...  78.1 us
    all_to_all x1, blocking collectives, local(): lax.all_to_all(send_grads.reshape(experts_total, capacity, model_width),...  76.2 us
    all_to_all x1, waiting for transfers between devices, local(): lax.all_to_all(expert_rows.reshape(senders, capacity, model_width), 'expe...  67.2 us
    dot_general x1, matrix products, local(): pre_act = jnp.dot(arrived, first_weight, preferred_element_type=jnp.float32)  63.5 us
    dot_general x24, matrix products, head_scores(): jnp.einsum('sqd,skd->sqk', query_h, key_h, preferred_element_type=jnp.flo...  46.2 us
    all_to_all x1, waiting for transfers between devices, local(): lax.all_to_all(grad_sent.reshape(senders, capacity, model_width), 'expert...  40.7 us
    psum x1, blocking collectives, local(): lax.psum((grad_w_query, grad_w_key, grad_w_value, grad_w_out, grad_gain_o...  40.2 us
  transfers between devices with their start and end apart: 4, of which 3 were waited for; matrix products, arithmetic and copies ran while one was open for 26% of the time, Pallas kernels for 0%

commit v1 on v0

v1 whole, which is shorter than its diff:
```python
import functools

import jax
import jax.numpy as jnp
from jax import lax
from jax.experimental import pallas as pl
from jax.experimental.pallas import tpu as pltpu
from jax.sharding import PartitionSpec as P

HEADS = 12
HEAD_DIM = 64
LEN = 1024
EPS = 1e-05
F32 = jnp.float32
BF16 = jnp.bfloat16
BLK = 256
LIMIT = 60 * 1024 * 1024

VMEM = pl.BlockSpec(memory_space=pltpu.VMEM)
SMEM = pl.BlockSpec(memory_space=pltpu.SMEM)


def dot(left, right, contract):
    return lax.dot_general(left, right, ((contract[0:1], contract[1:2]), ((), ())), preferred_element_type=F32)


def nn(left, right):
    return dot(left, right, (1, 0))


def nt(left, right):
    return dot(left, right, (1, 1))


def tn(left, right):
    return dot(left, right, (0, 0))


def iota(shape, axis):
    return lax.broadcasted_iota(jnp.int32, shape, axis)


def norm_stats(rows):
    center = rows - jnp.mean(rows, axis=-1, keepdims=True)
    rstd = lax.rsqrt(jnp.mean(center * center, axis=-1, keepdims=True) + EPS)
    return center * rstd, rstd


def pack_rows(slot_row, rows_ref, send_ref):
    slots = send_ref.shape[0]
    tokens = rows_ref.shape[0]

    def step(block, carry):
        base = pl.multiple_of(block * BLK, BLK)
        slot = iota((BLK, tokens), 0) + base
        pick = jnp.where(slot == slot_row, 1.0, 0.0).astype(BF16)
        send_ref[pl.ds(base, BLK), :] = nn(pick, rows_ref[...]).astype(BF16)
        return carry

    lax.fori_loop(0, slots // BLK, step, 0)


def table_kernel(experts, capacity, counts_ref, weight_ref, sort_ref, cot_ref, send_ref, slot_col_ref, slot_row_ref, scaled):
    tokens = cot_ref.shape[0]
    place = iota((1, tokens), 1)
    expert_at = jnp.zeros((1, tokens), jnp.int32)
    start_at = jnp.zeros((1, tokens), jnp.int32)
    end = jnp.int32(0)
    for expert in range(experts):
        count = counts_ref[0, expert]
        end = end + count
        past = place >= end
        expert_at = expert_at + jnp.where(past, 1, 0)
        start_at = start_at + jnp.where(past, count, 0)
    dest = (expert_at * capacity + place - start_at).astype(F32)
    sort_row = sort_ref[...]
    scaled[...] = (cot_ref[...].astype(F32) * weight_ref[0, 0]).astype(BF16)
    for block in range(tokens // BLK):
        token = iota((BLK, tokens), 0) + block * BLK
        col = jnp.sum(jnp.where(token == sort_row, dest, 0.0), axis=1, keepdims=True)
        wide = jnp.broadcast_to(col, (BLK, 128))
        slot_col_ref[pl.ds(block * BLK, BLK), :] = wide.astype(jnp.int32)
        slot_row_ref[:, pl.ds(block * BLK, BLK)] = wide.T[0:8].astype(jnp.int32)
    pack_rows(slot_row_ref[0:1, :], scaled, send_ref)


def forward_kernel(
    capacity,
    x_ref,
    gain_one_ref,
    shift_one_ref,
    gain_two_ref,
    shift_two_ref,
    wq_ref,
    wk_ref,
    wv_ref,
    wo_ref,
    router_ref,
    slot_col_ref,
    slot_row_ref,
    normed_ref,
    q_ref,
    k_ref,
    v_ref,
    mixed_ref,
    lse_ref,
    hidden_ref,
    gate_ref,
    send_ref,
    routed,
):
    tokens, width = x_ref.shape
    blocks = tokens // BLK
    lane = iota((1, 128), 1)

    def project(block, carry):
        rows = pl.ds(pl.multiple_of(block * BLK, BLK), BLK)
        hat, _ = norm_stats(x_ref[rows, :].astype(F32))
        normed = (hat * gain_one_ref[...] + shift_one_ref[...]).astype(BF16)
        normed_ref[rows, :] = normed
        q_ref[rows, :] = (nn(normed, wq_ref[...]).astype(BF16) * (HEAD_DIM ** (-0.5))).astype(BF16)
        k_ref[rows, :] = nn(normed, wk_ref[...]).astype(BF16)
        v_ref[rows, :] = nn(normed, wv_ref[...]).astype(BF16)
        return carry

    lax.fori_loop(0, blocks, project, 0)

    keep = iota((BLK, BLK), 0) <= iota((BLK, BLK), 1)

    def attend(pair, carry):
        cols = pl.ds(pl.multiple_of(pair * 128, 128), 128)
        k_pair = k_ref[:, cols]
        v_t = v_ref[:, cols].astype(F32).T.astype(BF16)
        k_head = [jnp.where(lane < 64, k_pair, 0), jnp.where(lane >= 64, k_pair, 0)]
        for block in range(blocks):
            span = (block + 1) * BLK
            query = q_ref[pl.ds(block * BLK, BLK), cols]
            outs = []
            for half in range(2):
                scores = nt(k_head[half][:span], query)
                diag = jnp.where(keep, scores[block * BLK :], -1000000000.0)
                scores = jnp.concatenate([scores[: block * BLK], diag], axis=0) if block else diag
                peak = jnp.max(scores, axis=0, keepdims=True)
                exps = jnp.exp(scores - peak)
                total = jnp.sum(exps, axis=0, keepdims=True)
                out = nn(v_t[half * 64 : half * 64 + 64, :span], exps.astype(BF16))
                outs.append(out * (1.0 / total))
                lse_ref[pair, half : half + 1, pl.ds(block * BLK, BLK)] = peak + jnp.log(total)
            mixed_ref[pl.ds(block * BLK, BLK), cols] = jnp.concatenate(outs, axis=0).T.astype(BF16)
        return carry

    lax.fori_loop(0, HEADS // 2, attend, 0)

    experts = router_ref.shape[1]

    def finish(block, carry):
        rows = pl.ds(pl.multiple_of(block * BLK, BLK), BLK)
        hidden = x_ref[rows, :].astype(F32) + nn(mixed_ref[rows, :], wo_ref[...])
        hidden_ref[rows, :] = hidden
        hat, _ = norm_stats(hidden)
        low = (hat * gain_two_ref[...] + shift_two_ref[...]).astype(BF16)
        routed[rows, :] = low
        logits = nn(low, router_ref[...])
        slot = slot_col_ref[rows, 0:1]
        first = iota((BLK, experts), 1) * capacity
        mine = (slot >= first) & (slot < first + capacity)
        logit = jnp.sum(jnp.where(mine, logits, 0.0), axis=1, keepdims=True)
        gate_ref[rows, :] = jnp.broadcast_to(jax.nn.sigmoid(logit), (BLK, 128))
        return carry

    lax.fori_loop(0, blocks, finish, 0)
    pack_rows(slot_row_ref[0:1, :], routed, send_ref)


def gelu_parts(v):
    size = jnp.abs(v)
    t = 1.0 / (1.0 + (0.3275911 * 0.7071067811865476) * size)
    bell = jnp.exp(-0.5 * (v * v))
    poly = ((((1.061405429 * t - 1.453152027) * t + 1.421413741) * t - 0.284496736) * t + 0.254829592) * t
    tail = 0.5 * poly * bell
    return jnp.where(v >= 0.0, 1.0 - tail, tail), bell * 0.3989422804014327


def expert_kernel(
    chunk,
    x_ref,
    g_ref,
    router_ref,
    w1_ref,
    w2_ref,
    y_ref,
    dx_ref,
    gw1_ref,
    gw2_ref,
    acc1,
    acc2,
):
    step = pl.program_id(0)
    hidden = w1_ref.shape[1]
    width = w1_ref.shape[0]

    @pl.when(step == 0)
    def _():
        acc1[...] = jnp.zeros_like(acc1)
        acc2[...] = jnp.zeros_like(acc2)

    x = x_ref[...]
    router = router_ref[...]
    logit = jnp.sum(x.astype(F32) * router, axis=1, keepdims=True)
    gate = jax.nn.sigmoid(logit)
    go = g_ref[...].astype(F32)
    g = (gate * go).astype(BF16)
    x_t = x.astype(F32).T.astype(BF16)
    y = jnp.zeros(x.shape, F32)
    dx = jnp.zeros(x.shape, F32)
    for first in range(0, hidden, chunk):
        cols = pl.ds(first, chunk)
        w1 = w1_ref[:, cols]
        w2 = w2_ref[cols, :]
        pre = nn(x, w1)
        cdf, pdf = gelu_parts(pre)
        act = (pre * cdf).astype(BF16)
        slope = cdf + pre * pdf
        y = y + nn(act, w2)
        grad = (nt(g, w2) * slope).astype(BF16)
        dx = dx + nt(grad, w1)
        acc1[:, cols] += nn(x_t, grad)
        acc2[cols, :] += tn(act, g)
    y_low = y.astype(BF16)
    y_ref[...] = y_low
    dlogit = jnp.sum(y_low.astype(F32) * go, axis=1, keepdims=True) * gate * (1.0 - gate)
    dx_ref[...] = (dx + dlogit * router).astype(BF16)

    @pl.when(step == pl.num_programs(0) - 1)
    def _():
        gw1_ref[...] = acc1[...].astype(BF16)
        gw2_ref[...] = acc2[...].astype(BF16)


def backward_kernel(
    weight_ref,
    x_ref,
    cot_ref,
    gain_one_ref,
    gain_two_ref,
    wq_ref,
    wk_ref,
    wv_ref,
    wo_ref,
    slot_col_ref,
    normed_ref,
    q_ref,
    k_ref,
    v_ref,
    mixed_ref,
    lse_ref,
    hidden_ref,
    dx_ref,
    grad_ref,
    dense_ref,
    ghid,
    gmix,
    branch,
    normed_t,
    dqkv,
    sums,
):
    tokens, width = x_ref.shape
    slots = dx_ref.shape[0]
    blocks = tokens // BLK
    lane = iota((1, 128), 1)
    sums[...] = jnp.zeros_like(sums)

    def open_block(block, carry):
        rows = pl.ds(pl.multiple_of(block * BLK, BLK), BLK)
        slot = slot_col_ref[rows, 0:1]
        pick = jnp.where(iota((BLK, slots), 1) == slot, 1.0, 0.0).astype(BF16)
        grad = nn(pick, dx_ref[...])
        hat, rstd = norm_stats(hidden_ref[rows, :])
        sums[2:3, :] += jnp.sum(grad * hat, axis=0, keepdims=True)
        sums[3:4, :] += jnp.sum(grad, axis=0, keepdims=True)
        gg = grad * gain_two_ref[...]
        inner = gg - jnp.mean(gg, axis=1, keepdims=True) - hat * jnp.mean(gg * hat, axis=1, keepdims=True)
        total = cot_ref[rows, :].astype(F32) * weight_ref[0, 0] + rstd * inner
        ghid[rows, :] = total
        low = total.astype(BF16)
        branch[rows, :] = low
        gmix[rows, :] = nt(low, wo_ref[...]).astype(BF16)
        normed_t[:, rows] = normed_ref[rows, :].astype(F32).T.astype(BF16)
        return carry

    lax.fori_loop(0, blocks, open_block, 0)
    dense_ref[pl.ds(3 * width, width), :] = tn(mixed_ref[...], branch[...]).astype(BF16)

    keep = iota((BLK, BLK), 0) <= iota((BLK, BLK), 1)

    def attend(pair, carry):
        base = pl.multiple_of(pair * 128, 128)
        cols = pl.ds(base, 128)
        q_pair = q_ref[:, cols]
        k_pair = k_ref[:, cols]
        v_pair = v_ref[:, cols]
        o_pair = gmix[:, cols]
        low = lane < 64
        q_head = [jnp.where(low, q_pair, 0), jnp.where(low, 0, q_pair)]
        k_head = [jnp.where(low, k_pair, 0), jnp.where(low, 0, k_pair)]
        v_head = [jnp.where(low, v_pair, 0), jnp.where(low, 0, v_pair)]
        o_head = [jnp.where(low, o_pair, 0), jnp.where(low, 0, o_pair)]
        k_t = k_pair.astype(F32).T.astype(BF16)
        prod_t = (o_pair.astype(F32) * mixed_ref[:, cols].astype(F32)).T
        delta = [jnp.sum(prod_t[:64], axis=0, keepdims=True), jnp.sum(prod_t[64:], axis=0, keepdims=True)]
        dq_t = [[None] * blocks, [None] * blocks]
        for block in range(blocks):
            start = block * BLK
            dk = None
            dv = None
            for half in range(2):
                scores = nt(k_head[half][start : start + BLK], q_pair[start:])
                diag = jnp.where(keep, scores[:, :BLK], -1000000000.0)
                scores = jnp.concatenate([diag, scores[:, BLK:]], axis=1) if block < blocks - 1 else diag
                probs = jnp.exp(scores - lse_ref[pair, half : half + 1, pl.ds(start, tokens - start)])
                grad_p = nt(v_head[half][start : start + BLK], o_pair[start:])
                grad_s = (probs * (grad_p - delta[half][:, start:])).astype(BF16)
                dv_part = nn(probs.astype(BF16), o_head[half][start:])
                dk_part = nn(grad_s, q_head[half][start:])
                dv = dv_part if dv is None else dv + dv_part
                dk = dk_part if dk is None else dk + dk_part
                dq_part = nn(k_t[half * 64 : half * 64 + 64, start : start + BLK], grad_s)
                for later in range(block, blocks):
                    piece = dq_part[:, (later - block) * BLK : (later - block + 1) * BLK]
                    dq_t[half][later] = piece if dq_t[half][later] is None else dq_t[half][later] + piece
            rows = pl.ds(start, BLK)
            dqkv[rows, pl.ds(pl.multiple_of(base + width, 128), 128)] = dk.astype(BF16)
            dqkv[rows, pl.ds(pl.multiple_of(base + 2 * width, 128), 128)] = dv.astype(BF16)
        for block in range(blocks):
            both = jnp.concatenate([dq_t[0][block], dq_t[1][block]], axis=0) * (HEAD_DIM ** (-0.5))
            dqkv[pl.ds(block * BLK, BLK), cols] = both.T.astype(BF16)
        return carry

    lax.fori_loop(0, HEADS // 2, attend, 0)

    for part in range(3):
        dense_ref[pl.ds(part * width, width), :] = nn(normed_t[...], dqkv[:, pl.ds(part * width, width)]).astype(BF16)

    def close_block(block, carry):
        rows = pl.ds(pl.multiple_of(block * BLK, BLK), BLK)
        grad = nt(dqkv[rows, 0:width], wq_ref[...])
        grad = grad + nt(dqkv[rows, width : 2 * width], wk_ref[...])
        grad = grad + nt(dqkv[rows, 2 * width : 3 * width], wv_ref[...])
        hat, rstd = norm_stats(x_ref[rows, :].astype(F32))
        sums[0:1, :] += jnp.sum(grad * hat, axis=0, keepdims=True)
        sums[1:2, :] += jnp.sum(grad, axis=0, keepdims=True)
        gg = grad * gain_one_ref[...]
        inner = gg - jnp.mean(gg, axis=1, keepdims=True) - hat * jnp.mean(gg * hat, axis=1, keepdims=True)
        grad_ref[rows, :] = (ghid[rows, :] + rstd * inner).astype(BF16)
        return carry

    lax.fori_loop(0, blocks, close_block, 0)
    dense_ref[pl.ds(4 * width, 16), :] = sums[...].astype(BF16)


def output_kernel(slot_col_ref, hidden_ref, gate_ref, y_ref, out_ref):
    tokens, _ = hidden_ref.shape
    slots = y_ref.shape[0]

    def step(block, carry):
        rows = pl.ds(pl.multiple_of(block * BLK, BLK), BLK)
        slot = slot_col_ref[rows, 0:1]
        pick = jnp.where(iota((BLK, slots), 1) == slot, 1.0, 0.0).astype(BF16)
        back = nn(pick, y_ref[...])
        out_ref[rows, :] = (hidden_ref[rows, :] + gate_ref[rows, 0:1] * back).astype(BF16)
        return carry

    lax.fori_loop(0, tokens // BLK, step, 0)


def call(kernel, outs, in_specs, scratch, name):
    return pl.pallas_call(
        kernel,
        out_shape=outs,
        in_specs=in_specs,
        out_specs=[VMEM] * len(outs),
        scratch_shapes=scratch,
        compiler_params=pltpu.CompilerParams(vmem_limit_bytes=LIMIT),
        name=name,
    )


def shape(dims, kind):
    return jax.ShapeDtypeStruct(dims, kind)


def tables(experts, capacity, counts, weight, sort_order, cotangent):
    tokens, width = cotangent.shape
    slots = experts * capacity
    return call(
        functools.partial(table_kernel, experts, capacity),
        [shape((slots, width), BF16), shape((tokens, 128), jnp.int32), shape((8, tokens), jnp.int32)],
        [SMEM, SMEM, VMEM, VMEM],
        [pltpu.VMEM((tokens, width), BF16)],
        "tables",
    )(counts, weight, sort_order, cotangent)


def forward(capacity, slots, inputs, g1, s1, g2, s2, wq, wk, wv, wo, router, slot_col, slot_row):
    tokens, width = inputs.shape
    rows_low = shape((tokens, width), BF16)
    return call(
        functools.partial(forward_kernel, capacity),
        [
            rows_low,
            rows_low,
            rows_low,
            rows_low,
            rows_low,
            shape((HEADS // 2, 8, tokens), F32),
            shape((tokens, width), F32),
            shape((tokens, 128), F32),
            shape((slots, width), BF16),
        ],
        [VMEM] * 12,
        [pltpu.VMEM((tokens, width), BF16)],
        "dense_forward",
    )(inputs, g1, s1, g2, s2, wq, wk, wv, wo, router, slot_col, slot_row)


def expert_block(x, g, router_row, w1, w2, rows=BLK, chunk=768):
    slots, width = x.shape
    hidden = w1.shape[1]
    row_spec = pl.BlockSpec((rows, width), lambda i: (i, 0))
    one = pl.Buffered(1)

    def whole(dims):
        return pl.BlockSpec(dims, lambda i: (0, 0), pipeline_mode=one)

    return pl.pallas_call(
        functools.partial(expert_kernel, chunk),
        out_shape=[
            shape((slots, width), BF16),
            shape((slots, width), BF16),
            shape((width, hidden), BF16),
            shape((hidden, width), BF16),
        ],
        grid=(slots // rows,),
        in_specs=[row_spec, row_spec, whole((1, width)), whole((width, hidden)), whole((hidden, width))],
        out_specs=[row_spec, row_spec, whole((width, hidden)), whole((hidden, width))],
        scratch_shapes=[pltpu.VMEM((width, hidden), F32), pltpu.VMEM((hidden, width), F32)],
        compiler_params=pltpu.CompilerParams(vmem_limit_bytes=LIMIT),
        name="expert",
    )(x, g, router_row, w1, w2)


def backward(weight, inputs, cotangent, g1, g2, wq, wk, wv, wo, slot_col, normed, q, k, v, mixed, lse, hidden, dx):
    tokens, width = inputs.shape
    return call(
        backward_kernel,
        [shape((tokens, width), BF16), shape((4 * width + 16, width), BF16)],
        [SMEM] + [VMEM] * 17,
        [
            pltpu.VMEM((tokens, width), F32),
            pltpu.VMEM((tokens, width), BF16),
            pltpu.VMEM((tokens, width), BF16),
            pltpu.VMEM((width, tokens), BF16),
            pltpu.VMEM((tokens, 3 * width), BF16),
            pltpu.VMEM((16, width), F32),
        ],
        "dense_backward",
    )(weight, inputs, cotangent, g1, g2, wq, wk, wv, wo, slot_col, normed, q, k, v, mixed, lse, hidden, dx)


def combine(slot_col, hidden, gate, y):
    return call(output_kernel, [shape(hidden.shape, BF16)], [VMEM] * 4, [], "combine")(slot_col, hidden, gate, y)[0]


def local(
    inputs,
    cotangent,
    seq_group,
    domain_counts,
    sort_order,
    send_counts,
    gain_one,
    shift_one,
    gain_two,
    shift_two,
    w_query,
    w_key,
    w_value,
    w_out,
    router,
    expert_in,
    expert_out,
):
    tokens, width = inputs.shape
    experts = send_counts.shape[1]
    capacity = 2 * tokens // experts
    slots = experts * capacity
    inverse = 1.0 / domain_counts.astype(F32)
    domain_weights = inverse / jnp.mean(inverse)
    ids = jnp.arange(domain_counts.shape[0], dtype=jnp.int32)
    weight = jnp.sum(jnp.where(seq_group[:, None] == ids[None, :], domain_weights[None, :], 0.0), axis=1).reshape(1, 1)
    mine = lax.axis_index("expert")
    router_row = lax.dynamic_slice_in_dim(router.T, mine, 1, axis=0).astype(F32)

    def exchange(rows):
        return lax.all_to_all(
            rows.reshape(experts, capacity, width), "expert", split_axis=0, concat_axis=0, tiled=True
        ).reshape(slots, width)

    g1, s1, g2, s2 = (v.reshape(1, width) for v in (gain_one, shift_one, gain_two, shift_two))
    cot_send, slot_col, slot_row = tables(experts, capacity, send_counts, weight, sort_order, cotangent)
    cot_rows = exchange(cot_send)
    normed, q, k, v, mixed, lse, hidden, gate, send = forward(
        capacity, slots, inputs, g1, s1, g2, s2, w_query, w_key, w_value, w_out, router, slot_col, slot_row
    )
    arrived = exchange(send)
    y_rows, dx_rows, grad_first, grad_second = expert_block(arrived, cot_rows, router_row, expert_in[0], expert_out[0])
    dx_back = exchange(dx_rows)
    y_back = exchange(y_rows)
    expert_sums = (lax.psum(grad_first, "dp").astype(F32), lax.psum(grad_second, "dp").astype(F32))
    grad_inputs, dense = backward(
        weight, inputs, cotangent, g1, g2, w_query, w_key, w_value, w_out, slot_col, normed, q, k, v, mixed, lse, hidden, dx_back
    )
    output = combine(slot_col, hidden, gate, y_back)
    dense = lax.psum(dense, ("dp", "expert")).astype(F32)
    parts = [dense[i * width : (i + 1) * width] for i in range(4)]
    vecs = [dense[4 * width + i] for i in range(4)]
    return (
        output,
        grad_inputs,
        *vecs,
        *parts,
        expert_sums[0][None],
        expert_sums[1][None],
    )


def solution(mesh):
    rows = P(("dp", "expert"), None)
    split = P("expert", None, None)
    return jax.shard_map(
        local,
        mesh=mesh,
        in_specs=(rows, rows, P(("dp", "expert")), P(), rows, rows) + (P(),) * 9 + (split, split),
        out_specs=(rows, rows) + (P(),) * 8 + (split, split),
        check_vma=False,
    )
```

time: 1000 us -> 851 us (0.85)
  matrix products: 378 us -> 0 us
  Pallas kernels: 0 us -> 204 us
  waiting for transfers between devices: 228 us -> 339 us
  local copies, waits for them, and re-layouts: 109 us -> 13.9 us
  blocking collectives: 194 us -> 255 us
  other arithmetic: 54.5 us -> 19.1 us
    dot_general x103 -> x0, matrix products: 378 us -> none  [the longest x1 63.5 us: local(): pre_act = jnp.dot(arrived, first_weight, preferred_element_type=jnp.float32)]
    pallas_call x0 -> x5, Pallas kernels: none -> 204 us  [the longest x1 84.4 us: expert_block(): pl.pallas_call(functools.partial(expert_kernel, chunk), out_shape=[shape(...]
    psum x2, waiting for transfers between devices: 120 us -> 269 us  [the longest x1 185 us: local(): lax.psum(grad_first, 'dp').astype(F32)]
    all_to_all x2 -> x3, blocking collectives: 154 us -> 255 us  [exchange(): lax.all_to_all(rows.reshape(experts, capacity, width), 'expert', split_ax...]
    psum x1 -> x0, blocking collectives: 40.2 us -> none  [local(): lax.psum((grad_w_query, grad_w_key, grad_w_value, grad_w_out, grad_gain_o...]
    all_to_all x2 -> x1, waiting for transfers between devices: 108 us -> 69.9 us  [exchange(): lax.all_to_all(rows.reshape(experts, capacity, width), 'expert', split_ax...]
    scatter x4 -> x0, local copies, waits for them, and re-layouts: 24.6 us -> none  [the longest x1 7.89 us: local(): send_rows = jnp.zeros((experts_total * capacity, model_width), jnp.bfloat...]
    gather x4 -> x0, local copies, waits for them, and re-layouts: 20.9 us -> none  [the longest x2 10.5 us: local(): grad_returned[dest_token].astype(jnp.float32)]
  transfers between devices with their start and end apart: 4 -> 3, of which waited for: 3 -> 3; matrix products, arithmetic and copies ran while one was open for 26% -> 1% of each run, Pallas kernels for 0% -> 1%
where the time goes in v1:
time: 851 us; the launch traced here: 850 us
  waiting for transfers between devices  339 us (40%)
  blocking collectives  255 us (30%)
  Pallas kernels  204 us (24%)
  other arithmetic  19.1 us (2%)
  between operations  15.4 us (2%)
  local copies, waits for them, and re-layouts  13.9 us (2%)
    all_to_all x3, blocking collectives, exchange(): lax.all_to_all(rows.reshape(experts, capacity, width), 'expert', split_ax...  255 us
    psum x1, waiting for transfers between devices, local(): lax.psum(grad_first, 'dp').astype(F32)  185 us
    pallas_call x1, Pallas kernels, expert_block(): pl.pallas_call(functools.partial(expert_kernel, chunk), out_shape=[shape(...  84.4 us
    psum x1, waiting for transfers between devices, local(): dense = lax.psum(dense, ('dp', 'expert')).astype(F32)  83.7 us
    all_to_all x1, waiting for transfers between devices, exchange(): lax.all_to_all(rows.reshape(experts, capacity, width), 'expert', split_ax...  69.9 us
    pallas_call x1, Pallas kernels, backward(): call(backward_kernel, [shape((tokens, width), BF16), shape((4 * width + 1...  55.6 us
    pallas_call x1, Pallas kernels, forward(): call(functools.partial(forward_kernel, capacity), [rows_low, rows_low, ro...  45.9 us
  transfers between devices with their start and end apart: 3, of which 3 were waited for; matrix products, arithmetic and copies ran while one was open for 1% of the time, Pallas kernels for 1%

profile of v1, /device:TPU:0, one launch (start us, length us, event | category | flops | bytes accessed | tf_op | source)
XLA Modules:
  0.0 850.1 jit_solution(16421776439349761651)
XLA Ops:
  7.2 1.3 divide_reduce_fusion
  9.1 1.3 reshape.84.gain_one_ref
  10.4 1.3 reshape.86.gain_two_ref
  11.6 1.5 copy.29.router_ref
  13.2 1.3 reshape.85.shift_one_ref
  16.3 1.3 fusion
  17.7 9.5 %tables.1 = (bf16[2048,768]{1,0:T(8,128)(2,1)}, s32[1024,128]{1,0:T(8,128)}, s32[8,1024]{1,0:T(8,128)}) custom-call(s32[1,8]{1,0:T(1,128)} %counts_ref.1, f32[1,1]{1,0:T(1,128)} %bitcast.1.weight_ref, s32[1,1024]{1,0:T(1,128)} %sort_ref.1, bf16[1024,768]{1,0:T(8,128)(2,1)} %cot_ref.3), custom_call_target="tpu_custom_call" | custom-call | tf_op jit(solution)/shard_map/tables/pallas_call | solution.py:396
  27.2 45.9 %dense_forward.1 = (bf16[1024,768]{1,0:T(8,128)(2,1)}, bf16[1024,768]{1,0:T(8,128)(2,1)}, bf16[1024,768]{1,0:T(8,128)(2,1)}, bf16[1024,768]{1,0:T(8,128)(2,1)}, ...) custom-call(bf16[1024,768]{1,0:T(8,128)(2,1)} %x_ref.3, ...), custom_call_target="tpu_custom_call" | custom-call | tf_op jit(solution)/shard_map/dense_forward/pallas_call | solution.py:408
  73.0 78.0 %all_to_all.20 = bf16[8,256,768]{2,1,0:T(8,128)(2,1)} all-to-all(bf16[8,256,768]{2,1,0:T(8,128)(2,1)} %bitcast.28), channel_id=1, replica_groups=mesh['dp'=4,'expert'=8] {'expert'}, dimensions={0} | all-to-all | bytes 6291456 | tf_op jit(solution)/shard_map/all_to_all | solution.py:506
  151.0 3.7 all-to-all-start.1
  154.9 1.3 bitcast_convert_fusion.router_ref
  156.2 69.9 %all-to-all-done.1 = bf16[8,256,768]{2,1,0:T(8,128)(2,1)S(1)} async-done(((bf16[8,256,768]{2,1,0:T(8,128)(2,1)}), bf16[8,256,768]{2,1,0:T(8,128)(2,1)S(1)}, u32[]{:S(2)}, u32[]{:S(2)}) %all-to-all-start.1) | async-done | bytes 3145760 | tf_op jit(solution)/shard_map/all_to_all | solution.py:506
  226.1 1.7 copy-done.1
  227.8 84.4 %expert.1 = (bf16[2048,768]{1,0:T(8,128)(2,1)}, bf16[2048,768]{1,0:T(8,128)(2,1)}, bf16[768,3072]{1,0:T(8,128)(2,1)}, bf16[3072,768]{1,0:T(8,128)(2,1)}) custom-call(bf16[2048,768]{1,0:T(8,128)(2,1)} %bitcast.19, bf16[2048,768]{1,0:T(8,128)(2,1)} %bitcast.20, f32[1,768]{1,0:T(1,128)} %bitcast_convert_fusion.router_ref, bf16[768,3072]{1,0:T(8,128)(2,1)} %bitcast.24, ...), custom_call_target="tpu_custom_call" | custom-call | tf_op jit(solution)/shard_map/expert/pallas_call | solution.py:436
  312.1 76.0 %all_to_all.21 = bf16[8,256,768]{2,1,0:T(8,128)(2,1)} all-to-all(bf16[8,256,768]{2,1,0:T(8,128)(2,1)} %bitcast.29), channel_id=1, replica_groups=mesh['dp'=4,'expert'=8] {'expert'}, dimensions={0} | all-to-all | bytes 6291456 | tf_op jit(solution)/shard_map/all_to_all | solution.py:506
  388.1 55.6 %dense_backward.1 = (bf16[1024,768]{1,0:T(8,128)(2,1)}, bf16[3088,768]{1,0:T(8,128)(2,1)}) custom-call(f32[1,1]{1,0:T(1,128)} %bitcast.1.weight_ref, bf16[1024,768]{1,0:T(8,128)(2,1)} %x_ref.3, bf16[1024,768]{1,0:T(8,128)(2,1)} %cot_ref.3, f32[1,768]{1,0:T(1,128)} %reshape.84.gain_one_ref, f32[1,768]{1,0:T(1,128)} %reshape.86.gain_two_ref, ...), custom_call_target="tpu_custom_call" | custom-call | tf_op jit(solution)/shard_map/dense_backward/pallas_call | solution.py:455
  445.7 100.6 %all_to_all.22 = bf16[8,256,768]{2,1,0:T(8,128)(2,1)} all-to-all(bf16[8,256,768]{2,1,0:T(8,128)(2,1)S(1)} %bitcast.26), channel_id=1, replica_groups=mesh['dp'=4,'expert'=8] {'expert'}, dimensions={0} | all-to-all | bytes 6291456 | tf_op jit(solution)/shard_map/all_to_all | solution.py:506
  546.3 8.5 combine.1
  554.8 83.7 %all-reduce.4.cloned.1.call-done = bf16[3088,768]{1,0:T(8,128)(2,1)} async-done(((bf16[3088,768]{1,0:T(8,128)(2,1)}), bf16[3088,768]{1,0:T(8,128)(2,1)}) %all-reduce.4.cloned.1.call-update) | async-done | bytes 4743184 | tf_op jit(solution)/shard_map/psum | solution.py:525
  638.5 3.2 convert_element_type.16
  642.3 3.8 fusion.1
  646.2 185.1 %all-reduce.6.cloned.1.call-done = (bf16[1,768,3072]{2,1,0:T(8,128)(2,1)}, bf16[1,3072,768]{2,1,0:T(8,128)(2,1)}) async-done(((bf16[1,768,3072]{2,1,0:T(8,128)(2,1)}, bf16[1,3072,768]{2,1,0:T(8,128)(2,1)}), (bf16[1,768,3072]{2,1,0:T(8,128)(2,1)}, bf16[1,3072,768]{2,1,0:T(8,128)(2,1)})) %all-reduce.6.cloned.1.call-update) | async-done | bytes 9437200 | tf_op jit(solution)/shard_map/psum | solution.py:520
  831.2 7.5 broadcast_in_dim.21
  838.8 4.5 broadcast_in_dim.23
  (13 shorter events, 4.1 us)
Async XLA Ops:
  151.0 75.1 %all-to-all-start.1 = ((bf16[8,256,768]{2,1,0:T(8,128)(2,1)}), bf16[8,256,768]{2,1,0:T(8,128)(2,1)S(1)}, u32[]{:S(2)}, u32[]{:S(2)}) async-start(bf16[8,256,768]{2,1,0:T(8,128)(2,1)} %bitcast.27), calls=%async_computation.1 | async-start | bytes 6291456 | tf_op jit(solution)/shard_map/all_to_all | solution.py:506
  154.7 483.8 %all-reduce.4.cloned.1.call-start = ((), (), s32[]{:S(2)}) async-start(), calls=%async_computation.4 | async-start | bytes 9486336 | tf_op jit(solution)/shard_map/psum | solution.py:525
  226.1 1.7 copy-start.1
  443.7 387.5 %all-reduce.6.cloned.1.call-start = ((), (), s32[]{:S(2)}) async-start(), calls=%async_computation.5 | async-start | bytes 18874368 | tf_op jit(solution)/shard_map/psum | solution.py:520
  443.8 1.9 copy-start.3
  638.5 3.9 copy-start
  831.2 7.5 copy-start.2
Sparse Core Ops, SparseCore 0:
  443.9 194.5 all-reduce.3
  642.7 188.4 all-reduce.5

commit v2 on v1

--- a/solution.py
+++ b/solution.py
@@ -18,6 +18,8 @@
 
 VMEM = pl.BlockSpec(memory_space=pltpu.VMEM)
 SMEM = pl.BlockSpec(memory_space=pltpu.SMEM)
+ANY = pl.BlockSpec(memory_space=pl.ANY)
+MESH = pl.DeviceIdType.MESH
 
 
 def dot(left, right, contract):
@@ -38,6 +40,44 @@
 
 def iota(shape, axis):
     return lax.broadcasted_iota(jnp.int32, shape, axis)
+
+
+def flip(index, mask, count):
+    bit, out = 1, 0
+    while bit < count:
+        out = out + ((index // bit + mask // bit) % 2) * bit
+        bit *= 2
+    return out
+
+
+def greet(axis, me, count):
+    barrier = pltpu.get_barrier_semaphore()
+    for mask in range(1, count):
+        pl.semaphore_signal(barrier, inc=1, device_id={axis: flip(me, mask, count)}, device_id_type=MESH)
+    pl.semaphore_wait(barrier, count - 1)
+
+
+def send_block(me, count, capacity, mask, source, target, sends, recvs):
+    peer = flip(me, mask, count)
+    return pltpu.make_async_remote_copy(
+        src_ref=source.at[pl.ds(pl.multiple_of(peer * capacity, capacity), capacity)],
+        dst_ref=target.at[pl.ds(pl.multiple_of(mask * capacity, capacity), capacity)],
+        send_sem=sends.at[mask],
+        recv_sem=recvs.at[mask],
+        device_id={"expert": peer},
+        device_id_type=MESH,
+    )
+
+
+def return_block(me, count, capacity, mask, source, target, sends, recvs):
+    return pltpu.make_async_remote_copy(
+        src_ref=source.at[pl.ds(pl.multiple_of(mask * capacity, capacity), capacity)],
+        dst_ref=target.at[pl.ds(pl.multiple_of(me * capacity, capacity), capacity)],
+        send_sem=sends.at[mask],
+        recv_sem=recvs.at[mask],
+        device_id={"expert": flip(me, mask, count)},
+        device_id_type=MESH,
+    )
 
 
 def norm_stats(rows):
@@ -85,6 +125,7 @@
 
 
 def forward_kernel(
+    count,
     capacity,
     x_ref,
     gain_one_ref,
@@ -98,6 +139,7 @@
     router_ref,
     slot_col_ref,
     slot_row_ref,
+    cot_send_ref,
     normed_ref,
     q_ref,
     k_ref,
@@ -107,10 +149,23 @@
     hidden_ref,
     gate_ref,
     send_ref,
+    cot_rows_ref,
     routed,
+    sends,
+    recvs,
+    own,
 ):
     tokens, width = x_ref.shape
     blocks = tokens // BLK
+    me = lax.axis_index("expert")
+    greet("expert", me, count)
+    copies = [send_block(me, count, capacity, mask, cot_send_ref, cot_rows_ref, sends, recvs) for mask in range(1, count)]
+    for copy in reversed(copies):
+        copy.start()
+    mine = pltpu.make_async_copy(
+        cot_send_ref.at[pl.ds(pl.multiple_of(me * capacity, capacity), capacity)], cot_rows_ref.at[pl.ds(0, capacity)], own
+    )
+    mine.start()
     lane = iota((1, 128), 1)
 
     def project(block, carry):
@@ -170,6 +225,9 @@
 
     lax.fori_loop(0, blocks, finish, 0)
     pack_rows(slot_row_ref[0:1, :], routed, send_ref)
+    mine.wait()
+    for copy in copies:
+        copy.wait()
 
 
 def gelu_parts(v):
@@ -182,62 +240,146 @@
 
 
 def expert_kernel(
+    count,
+    capacity,
     chunk,
-    x_ref,
+    send_ref,
     g_ref,
     router_ref,
+    w1_hbm,
+    w2_hbm,
+    y_ref,
+    back_ref,
+    gw1_ref,
+    gw2_ref,
     w1_ref,
     w2_ref,
-    y_ref,
-    dx_ref,
-    gw1_ref,
-    gw2_ref,
     acc1,
     acc2,
+    x_rows,
+    dx_rows,
+    y_rows,
+    stage,
+    load_sems,
+    sends,
+    recvs,
+    back_sends,
+    back_recvs,
+    own,
+    y_sems,
+    stage_sems,
 ):
-    step = pl.program_id(0)
-    hidden = w1_ref.shape[1]
-    width = w1_ref.shape[0]
-
-    @pl.when(step == 0)
-    def _():
-        acc1[...] = jnp.zeros_like(acc1)
-        acc2[...] = jnp.zeros_like(acc2)
-
-    x = x_ref[...]
+    width, hidden = w1_ref.shape
+    slots = x_rows.shape[0]
+    group = BLK // capacity
+    me = lax.axis_index("expert")
+    loads = [pltpu.make_async_copy(w1_hbm, w1_ref, load_sems.at[0]), pltpu.make_async_copy(w2_hbm, w2_ref, load_sems.at[1])]
+    for load in loads:
+        load.start()
+    greet("expert", me, count)
+    mine_in = pltpu.make_async_copy(
+        send_ref.at[pl.ds(pl.multiple_of(me * capacity, capacity), capacity)], x_rows.at[pl.ds(0, capacity)], own.at[0]
+    )
+    mine_in.start()
+    for mask in range(1, count):
+        send_block(me, count, capacity, mask, send_ref, x_rows, sends, recvs).start()
+    acc1[...] = jnp.zeros_like(acc1)
+    acc2[...] = jnp.zeros_like(acc2)
+    for load in loads:
+        load.wait()
+    mine_in.wait()
     router = router_ref[...]
-    logit = jnp.sum(x.astype(F32) * router, axis=1, keepdims=True)
-    gate = jax.nn.sigmoid(logit)
-    go = g_ref[...].astype(F32)
-    g = (gate * go).astype(BF16)
-    x_t = x.astype(F32).T.astype(BF16)
-    y = jnp.zeros(x.shape, F32)
-    dx = jnp.zeros(x.shape, F32)
-    for first in range(0, hidden, chunk):
-        cols = pl.ds(first, chunk)
-        w1 = w1_ref[:, cols]
-        w2 = w2_ref[cols, :]
-        pre = nn(x, w1)
-        cdf, pdf = gelu_parts(pre)
-        act = (pre * cdf).astype(BF16)
-        slope = cdf + pre * pdf
-        y = y + nn(act, w2)
-        grad = (nt(g, w2) * slope).astype(BF16)
-        dx = dx + nt(grad, w1)
-        acc1[:, cols] += nn(x_t, grad)
-        acc2[cols, :] += tn(act, g)
-    y_low = y.astype(BF16)
-    y_ref[...] = y_low
-    dlogit = jnp.sum(y_low.astype(F32) * go, axis=1, keepdims=True) * gate * (1.0 - gate)
-    dx_ref[...] = (dx + dlogit * router).astype(BF16)
-
-    @pl.when(step == pl.num_programs(0) - 1)
-    def _():
-        gw1_ref[...] = acc1[...].astype(BF16)
-        gw2_ref[...] = acc2[...].astype(BF16)
+
+    def store_y(block):
+        rows = pl.ds(pl.multiple_of(block * BLK, BLK), BLK)
+        return pltpu.make_async_copy(y_rows.at[rows], y_ref.at[rows], y_sems.at[block])
+
+    def mine_out():
+        return pltpu.make_async_copy(
+            dx_rows.at[pl.ds(0, capacity)], back_ref.at[pl.ds(pl.multiple_of(me * capacity, capacity), capacity)], own.at[1]
+        )
+
+    def run(block, carry):
+        for item in range(group):
+            mask = block * group + item
+
+            @pl.when(mask > 0)
+            def _():
+                send_block(me, count, capacity, mask, send_ref, x_rows, sends, recvs).wait_recv()
+
+        rows = pl.ds(pl.multiple_of(block * BLK, BLK), BLK)
+        x = x_rows[rows, :]
+        logit = jnp.sum(x.astype(F32) * router, axis=1, keepdims=True)
+        gate = jax.nn.sigmoid(logit)
+        go = g_ref[rows, :].astype(F32)
+        g = (gate * go).astype(BF16)
+        x_t = x.astype(F32).T.astype(BF16)
+        y = jnp.zeros(x.shape, F32)
+        dx = jnp.zeros(x.shape, F32)
+        for first in range(0, hidden, chunk):
+            cols = pl.ds(first, chunk)
+            w1 = w1_ref[:, cols]
+            w2 = w2_ref[cols, :]
+            pre = nn(x, w1)
+            cdf, pdf = gelu_parts(pre)
+            act = (pre * cdf).astype(BF16)
+            slope = cdf + pre * pdf
+            y = y + nn(act, w2)
+            grad = (nt(g, w2) * slope).astype(BF16)
+            dx = dx + nt(grad, w1)
+            acc1[:, cols] += nn(x_t, grad)
+            acc2[cols, :] += tn(act, g)
+        y_low = y.astype(BF16)
+        y_rows[rows, :] = y_low
+        dlogit = jnp.sum(y_low.astype(F32) * go, axis=1, keepdims=True) * gate * (1.0 - gate)
+        dx_rows[rows, :] = (dx + dlogit * router).astype(BF16)
+        store_y(block).start()
+        for item in range(group):
+            mask = block * group + item
+
+            @pl.when(mask > 0)
+            def _():
+                return_block(me, count, capacity, mask, dx_rows, back_ref, back_sends, back_recvs).start()
+
+            @pl.when(mask == 0)
+            def _():
+                mine_out().start()
+
+        return carry
+
+    lax.fori_loop(0, slots // BLK, run, 0)
+
+    pieces = []
+    for first in range(0, hidden, stage.shape[1]):
+        pieces.append((acc1.at[:, pl.ds(first, stage.shape[1])], gw1_ref.at[:, pl.ds(first, stage.shape[1])]))
+    for first in range(0, hidden, stage.shape[1]):
+        pieces.append((acc2.at[pl.ds(first, stage.shape[1]), :], gw2_ref.at[pl.ds(first, stage.shape[1]), :]))
+    writes = []
+    for index, (piece, target) in enumerate(pieces):
+        slot = index % 2
+        if index >= 2:
+            writes[index - 2].wait()
+        stage[slot] = piece[...].astype(BF16)
+        write = pltpu.make_async_copy(stage.at[slot], target, stage_sems.at[slot])
+        write.start()
+        writes.append(write)
+    for write in writes[-2:]:
+        write.wait()
+    mine_out().wait()
+
+    def settle(block, carry):
+        store_y(block).wait()
+        return carry
+
+    lax.fori_loop(0, slots // BLK, settle, 0)
+    for mask in range(1, count):
+        send_block(me, count, capacity, mask, send_ref, x_rows, sends, recvs).wait_send()
+        return_block(me, count, capacity, mask, dx_rows, back_ref, back_sends, back_recvs).wait()
 
 
 def backward_kernel(
+    count,
+    capacity,
     weight_ref,
     x_ref,
     cot_ref,
@@ -256,16 +398,30 @@
     lse_ref,
     hidden_ref,
     dx_ref,
+    y_ref,
     grad_ref,
     dense_ref,
+    y_back_ref,
     ghid,
     gmix,
     branch,
     normed_t,
     dqkv,
     sums,
+    sends,
+    recvs,
+    own,
 ):
     tokens, width = x_ref.shape
+    me = lax.axis_index("expert")
+    greet("expert", me, count)
+    copies = [return_block(me, count, capacity, mask, y_ref, y_back_ref, sends, recvs) for mask in range(1, count)]
+    for copy in reversed(copies):
+        copy.start()
+    mine = pltpu.make_async_copy(
+        y_ref.at[pl.ds(0, capacity)], y_back_ref.at[pl.ds(pl.multiple_of(me * capacity, capacity), capacity)], own
+    )
+    mine.start()
     slots = dx_ref.shape[0]
     blocks = tokens // BLK
     lane = iota((1, 128), 1)
@@ -357,6 +513,9 @@
 
     lax.fori_loop(0, blocks, close_block, 0)
     dense_ref[pl.ds(4 * width, 16), :] = sums[...].astype(BF16)
+    mine.wait()
+    for copy in copies:
+        copy.wait()
 
 
 def output_kernel(slot_col_ref, hidden_ref, gate_ref, y_ref, out_ref):
@@ -374,16 +533,22 @@
     lax.fori_loop(0, tokens // BLK, step, 0)
 
 
-def call(kernel, outs, in_specs, scratch, name):
+def call(kernel, outs, in_specs, scratch, name, out_specs=None, collective=None, flops=10**9):
+    remote = {} if collective is None else {"collective_id": collective, "has_side_effects": True}
     return pl.pallas_call(
         kernel,
         out_shape=outs,
         in_specs=in_specs,
-        out_specs=[VMEM] * len(outs),
+        out_specs=out_specs or [VMEM] * len(outs),
         scratch_shapes=scratch,
-        compiler_params=pltpu.CompilerParams(vmem_limit_bytes=LIMIT),
+        compiler_params=pltpu.CompilerParams(vmem_limit_bytes=LIMIT, **remote),
+        cost_estimate=pl.CostEstimate(flops=flops, bytes_accessed=10**7, transcendentals=0),
         name=name,
     )
+
+
+def dma(*dims):
+    return pltpu.SemaphoreType.DMA(dims)
 
 
 def shape(dims, kind):
@@ -402,11 +567,11 @@
     )(counts, weight, sort_order, cotangent)
 
 
-def forward(capacity, slots, inputs, g1, s1, g2, s2, wq, wk, wv, wo, router, slot_col, slot_row):
+def forward(count, capacity, slots, inputs, g1, s1, g2, s2, wq, wk, wv, wo, router, slot_col, slot_row, cot_send):
     tokens, width = inputs.shape
     rows_low = shape((tokens, width), BF16)
     return call(
-        functools.partial(forward_kernel, capacity),
+        functools.partial(forward_kernel, count, capacity),
         [
             rows_low,
             rows_low,
@@ -417,45 +582,57 @@
             shape((tokens, width), F32),
             shape((tokens, 128), F32),
             shape((slots, width), BF16),
+            shape((slots, width), BF16),
         ],
-        [VMEM] * 12,
-        [pltpu.VMEM((tokens, width), BF16)],
+        [VMEM] * 12 + [ANY],
+        [pltpu.VMEM((tokens, width), BF16), dma(count), dma(count), dma()],
         "dense_forward",
-    )(inputs, g1, s1, g2, s2, wq, wk, wv, wo, router, slot_col, slot_row)
-
-
-def expert_block(x, g, router_row, w1, w2, rows=BLK, chunk=768):
-    slots, width = x.shape
+        [VMEM] * 9 + [ANY],
+        1,
+    )(inputs, g1, s1, g2, s2, wq, wk, wv, wo, router, slot_col, slot_row, cot_send)
+
+
+def expert_block(count, capacity, send, g, router_row, w1, w2, chunk=768):
+    slots, width = send.shape
     hidden = w1.shape[1]
-    row_spec = pl.BlockSpec((rows, width), lambda i: (i, 0))
-    one = pl.Buffered(1)
-
-    def whole(dims):
-        return pl.BlockSpec(dims, lambda i: (0, 0), pipeline_mode=one)
-
-    return pl.pallas_call(
-        functools.partial(expert_kernel, chunk),
-        out_shape=[
-            shape((slots, width), BF16),
-            shape((slots, width), BF16),
-            shape((width, hidden), BF16),
-            shape((hidden, width), BF16),
+    rows = shape((slots, width), BF16)
+    keep = pltpu.VMEM((slots, width), BF16)
+    return call(
+        functools.partial(expert_kernel, count, capacity, chunk),
+        [rows, rows, shape((width, hidden), BF16), shape((hidden, width), BF16)],
+        [ANY, VMEM, VMEM, ANY, ANY],
+        [
+            pltpu.VMEM((width, hidden), BF16),
+            pltpu.VMEM((hidden, width), BF16),
+            pltpu.VMEM((width, hidden), F32),
+            pltpu.VMEM((hidden, width), F32),
+            keep,
+            keep,
+            keep,
+            pltpu.VMEM((2, width, width), BF16),
+            dma(2),
+            dma(count),
+            dma(count),
+            dma(count),
+            dma(count),
+            dma(2),
+            dma(slots // BLK),
+            dma(2),
         ],
-        grid=(slots // rows,),
-        in_specs=[row_spec, row_spec, whole((1, width)), whole((width, hidden)), whole((hidden, width))],
-        out_specs=[row_spec, row_spec, whole((width, hidden)), whole((hidden, width))],
-        scratch_shapes=[pltpu.VMEM((width, hidden), F32), pltpu.VMEM((hidden, width), F32)],
-        compiler_params=pltpu.CompilerParams(vmem_limit_bytes=LIMIT),
-        name="expert",
-    )(x, g, router_row, w1, w2)
-
-
-def backward(weight, inputs, cotangent, g1, g2, wq, wk, wv, wo, slot_col, normed, q, k, v, mixed, lse, hidden, dx):
+        "expert",
+        [ANY] * 4,
+        2,
+    )(send, g, router_row, w1, w2)
+
+
+def backward(
+    count, capacity, weight, inputs, cotangent, g1, g2, wq, wk, wv, wo, slot_col, normed, q, k, v, mixed, lse, hidden, dx, y
+):
     tokens, width = inputs.shape
     return call(
-        backward_kernel,
-        [shape((tokens, width), BF16), shape((4 * width + 16, width), BF16)],
-        [SMEM] + [VMEM] * 17,
+        functools.partial(backward_kernel, count, capacity),
+        [shape((tokens, width), BF16), shape((4 * width + 16, width), BF16), shape(y.shape, BF16)],
+        [SMEM] + [VMEM] * 17 + [ANY],
         [
             pltpu.VMEM((tokens, width), F32),
             pltpu.VMEM((tokens, width), BF16),
@@ -463,9 +640,15 @@
             pltpu.VMEM((width, tokens), BF16),
             pltpu.VMEM((tokens, 3 * width), BF16),
             pltpu.VMEM((16, width), F32),
+            dma(count),
+            dma(count),
+            dma(),
         ],
         "dense_backward",
-    )(weight, inputs, cotangent, g1, g2, wq, wk, wv, wo, slot_col, normed, q, k, v, mixed, lse, hidden, dx)
+        [VMEM, VMEM, ANY],
+        3,
+        5 * 10**10,
+    )(weight, inputs, cotangent, g1, g2, wq, wk, wv, wo, slot_col, normed, q, k, v, mixed, lse, hidden, dx, y)
 
 
 def combine(slot_col, hidden, gate, y):
@@ -502,24 +685,19 @@
     mine = lax.axis_index("expert")
     router_row = lax.dynamic_slice_in_dim(router.T, mine, 1, axis=0).astype(F32)
 
-    def exchange(rows):
-        return lax.all_to_all(
-            rows.reshape(experts, capacity, width), "expert", split_axis=0, concat_axis=0, tiled=True
-        ).reshape(slots, width)
-
+    count = lax.axis_size("expert")
     g1, s1, g2, s2 = (v.reshape(1, width) for v in (gain_one, shift_one, gain_two, shift_two))
     cot_send, slot_col, slot_row = tables(experts, capacity, send_counts, weight, sort_order, cotangent)
-    cot_rows = exchange(cot_send)
-    normed, q, k, v, mixed, lse, hidden, gate, send = forward(
-        capacity, slots, inputs, g1, s1, g2, s2, w_query, w_key, w_value, w_out, router, slot_col, slot_row
-    )
-    arrived = exchange(send)
-    y_rows, dx_rows, grad_first, grad_second = expert_block(arrived, cot_rows, router_row, expert_in[0], expert_out[0])
-    dx_back = exchange(dx_rows)
-    y_back = exchange(y_rows)
+    normed, q, k, v, mixed, lse, hidden, gate, send, cot_rows = forward(
+        count, capacity, slots, inputs, g1, s1, g2, s2, w_query, w_key, w_value, w_out, router, slot_col, slot_row, cot_send
+    )
+    y_rows, dx_back, grad_first, grad_second = expert_block(
+        count, capacity, send, cot_rows, router_row, expert_in[0], expert_out[0]
+    )
     expert_sums = (lax.psum(grad_first, "dp").astype(F32), lax.psum(grad_second, "dp").astype(F32))
-    grad_inputs, dense = backward(
-        weight, inputs, cotangent, g1, g2, w_query, w_key, w_value, w_out, slot_col, normed, q, k, v, mixed, lse, hidden, dx_back
+    grad_inputs, dense, y_back = backward(
+        count, capacity, weight, inputs, cotangent, g1, g2, w_query, w_key, w_value, w_out, slot_col,
+        normed, q, k, v, mixed, lse, hidden, dx_back, y_rows,
     )
     output = combine(slot_col, hidden, gate, y_back)
     dense = lax.psum(dense, ("dp", "expert")).astype(F32)

time: 851 us -> 692 us (0.81)
  blocking collectives: 255 us -> 0 us
  Pallas kernels: 204 us -> 324 us
  waiting for transfers between devices: 339 us -> 321 us
    all_to_all x3 -> x0, blocking collectives: 255 us -> none  [exchange(): lax.all_to_all(rows.reshape(experts, capacity, width), 'expert', split_ax...]
    pallas_call x3, Pallas kernels: 186 us -> 306 us  [the longest x1 124 us: expert_block(): call(functools.partial(expert_kernel, count, capacity, chunk), [rows, row...]
    all_to_all x1 -> x0, waiting for transfers between devices: 69.9 us -> none  [exchange(): lax.all_to_all(rows.reshape(experts, capacity, width), 'expert', split_ax...]
    psum x1, waiting for transfers between devices: 83.7 us -> 136 us  [local(): dense = lax.psum(dense, ('dp', 'expert')).astype(F32)]
  transfers between devices with their start and end apart: 3 -> 2, of which waited for: 3 -> 2; matrix products, arithmetic and copies ran while one was open for 1% -> 1% of each run, Pallas kernels for 1% -> 1%
where the time goes in v2:
time: 692 us; the launch traced here: 691 us
  Pallas kernels  324 us (47%)
  waiting for transfers between devices  321 us (46%)
  other arithmetic  19.1 us (3%)
  between operations  15.4 us (2%)
  local copies, waits for them, and re-layouts  12.2 us (2%)
    psum x1, waiting for transfers between devices, local(): lax.psum(grad_first, 'dp').astype(F32)  185 us
    psum x1, waiting for transfers between devices, local(): dense = lax.psum(dense, ('dp', 'expert')).astype(F32)  136 us
    pallas_call x1, Pallas kernels, expert_block(): call(functools.partial(expert_kernel, count, capacity, chunk), [rows, row...  124 us
    pallas_call x1, Pallas kernels, backward(): call(functools.partial(backward_kernel, count, capacity), [shape((tokens,...  98.7 us
    pallas_call x1, Pallas kernels, forward(): call(functools.partial(forward_kernel, count, capacity), [rows_low, rows_...  82.7 us
  transfers between devices with their start and end apart: 2, of which 2 were waited for; matrix products, arithmetic and copies ran while one was open for 1% of the time, Pallas kernels for 1%

profile of v2, /device:TPU:0, one launch (start us, length us, event | category | flops | bytes accessed | tf_op | source)
XLA Modules:
  0.0 691.4 jit_solution(1470098010095846367)
XLA Ops:
  7.2 0.0 all-reduce.4.cloned.1.call-start
  7.2 1.3 divide_reduce_fusion
  9.1 1.3 reshape.60.gain_one_ref
  10.4 1.3 reshape.61.shift_one_ref
  11.7 1.3 reshape.62.gain_two_ref
  13.0 1.3 reshape.63.shift_two_ref
  14.2 1.5 copy.29.router_ref
  15.7 1.3 bitcast_convert_fusion.router_ref
  17.7 1.3 fusion
  18.9 9.5 %tables.1 = (bf16[2048,768]{1,0:T(8,128)(2,1)}, s32[1024,128]{1,0:T(8,128)}, s32[8,1024]{1,0:T(8,128)}) custom-call(s32[1,8]{1,0:T(1,128)} %counts_ref.1, f32[1,1]{1,0:T(1,128)} %bitcast.1.weight_ref, s32[1,1024]{1,0:T(1,128)} %sort_ref.1, bf16[1024,768]{1,0:T(8,128)(2,1)} %cot_ref.3), custom_call_target="tpu_custom_call" | custom-call | flops 1000000000 | bytes 10000000 | tf_op jit(solution)/shard_map/tables/pallas_call | solution.py:561
  28.5 82.7 %dense_forward.1 = (bf16[1024,768]{1,0:T(8,128)(2,1)}, bf16[1024,768]{1,0:T(8,128)(2,1)}, bf16[1024,768]{1,0:T(8,128)(2,1)}, bf16[1024,768]{1,0:T(8,128)(2,1)}, ...) custom-call(bf16[1024,768]{1,0:T(8,128)(2,1)} %x_ref.3, ...), custom_call_target="tpu_custom_call" | custom-call | flops 1000000000 | bytes 10000000 | tf_op jit(solution)/shard_map/dense_forward/pallas_call | solution.py:573
  111.1 124.2 %expert.1 = (bf16[2048,768]{1,0:T(8,128)(2,1)}, bf16[2048,768]{1,0:T(8,128)(2,1)}, bf16[768,3072]{1,0:T(8,128)(2,1)}, bf16[3072,768]{1,0:T(8,128)(2,1)}) custom-call(bf16[2048,768]{1,0:T(8,128)(2,1)} %get-tuple-element.43.send_ref, bf16[2048,768]{1,0:T(8,128)(2,1)} %get-tuple-element.44.g_ref, f32[1,768]{1,0:T(1,128)} %bitcast_convert_fusion.router_ref, ...), custom_call_target="tpu_custom_call" | custom-call | flops 1000000000 | bytes 10000000 | tf_op jit(solution)/shard_map/expert/pallas_call | solution.py:600
  235.4 98.7 %dense_backward.1 = (bf16[1024,768]{1,0:T(8,128)(2,1)}, bf16[3088,768]{1,0:T(8,128)(2,1)}, bf16[2048,768]{1,0:T(8,128)(2,1)}) custom-call(f32[1,1]{1,0:T(1,128)} %bitcast.1.weight_ref, bf16[1024,768]{1,0:T(8,128)(2,1)} %x_ref.3, bf16[1024,768]{1,0:T(8,128)(2,1)} %cot_ref.3, f32[1,768]{1,0:T(1,128)} %reshape.60.gain_one_ref, f32[1,768]{1,0:T(1,128)} %reshape.62.gain_two_ref, ...), custom_call_target="tpu_custom_call" | custom-call | flops 49999998976 | bytes 10000000 | tf_op jit(solution)/shard_map/dense_backward/pallas_call | solution.py:632
  334.1 0.0 all-reduce.6.cloned.1.call-start
  334.1 0.7 all-reduce.6.cloned.1.call-update
  334.8 8.4 %combine.1 = bf16[1024,768]{1,0:T(8,128)(2,1)} custom-call(s32[1024,128]{1,0:T(8,128)} %get-tuple-element.32.slot_col_ref, f32[1024,768]{1,0:T(8,128)} %get-tuple-element.35.hidden_ref, f32[1024,128]{1,0:T(8,128)} %get-tuple-element.36.gate_ref, bf16[2048,768]{1,0:T(8,128)(2,1)} %get-tuple-element.47.y_ref), custom_call_target="tpu_custom_call" | custom-call | flops 1000000000 | bytes 10000000 | tf_op jit(solution)/shard_map/combine/pallas_call | solution.py:655
  343.3 135.8 %all-reduce.4.cloned.1.call-done = bf16[3088,768]{1,0:T(8,128)(2,1)} async-done(((bf16[3088,768]{1,0:T(8,128)(2,1)}), bf16[3088,768]{1,0:T(8,128)(2,1)}) %all-reduce.4.cloned.1.call-update) | async-done | bytes 4743184 | tf_op jit(solution)/shard_map/psum | solution.py:703
  479.1 3.2 convert_element_type.16
  482.3 0.6 slice_reduce_fusion
  483.0 3.8 fusion.1
  486.8 184.6 %all-reduce.6.cloned.1.call-done = (bf16[1,768,3072]{2,1,0:T(8,128)(2,1)}, bf16[1,3072,768]{2,1,0:T(8,128)(2,1)}) async-done(((bf16[1,768,3072]{2,1,0:T(8,128)(2,1)}, bf16[1,3072,768]{2,1,0:T(8,128)(2,1)}), (bf16[1,768,3072]{2,1,0:T(8,128)(2,1)}, bf16[1,3072,768]{2,1,0:T(8,128)(2,1)})) %all-reduce.6.cloned.1.call-update) | async-done | bytes 9437200 | tf_op jit(solution)/shard_map/psum | solution.py:697
  671.4 7.5 %broadcast_in_dim.21 = f32[1,768,3072]{2,1,0:T(8,128)} convert(bf16[1,768,3072]{2,1,0:T(8,128)(2,1)} %get-tuple-element.56) | non-fusion elementwise | flops 2359296 | bytes 14155776 | tf_op jit(solution)/shard_map/broadcast_in_dim | solution.py:711
  678.9 4.5 broadcast_in_dim.23
  683.4 1.1 copy.35
  (7 shorter events, 0.0 us)
Async XLA Ops:
  7.2 471.9 %all-reduce.4.cloned.1.call-start = ((), (), s32[]{:S(2)}) async-start(), calls=%async_computation | async-start | bytes 9486336 | tf_op jit(solution)/shard_map/psum | solution.py:703
  334.1 337.3 %all-reduce.6.cloned.1.call-start = ((), (), s32[]{:S(2)}) async-start(), calls=%async_computation.1 | async-start | bytes 18874368 | tf_op jit(solution)/shard_map/psum | solution.py:697
  479.1 3.9 copy-start
  671.4 7.5 %copy-start.1 = (bf16[1,3072,768]{2,1,0:T(8,128)(2,1)S(1)}, bf16[1,3072,768]{2,1,0:T(8,128)(2,1)}, u32[]{:S(2)}) copy-start(bf16[1,3072,768]{2,1,0:T(8,128)(2,1)} %get-tuple-element.57) | copy-start | bytes 14155780
  678.9 4.5 copy-start.2
Sparse Core Ops, SparseCore 0:
  334.2 144.8 all-reduce.3
  482.8 188.5 all-reduce.5

commit v3 on v2

--- a/solution.py
+++ b/solution.py
@@ -69,9 +69,9 @@
     )
 
 
-def return_block(me, count, capacity, mask, source, target, sends, recvs):
+def return_block(me, count, capacity, mask, source, target, sends, recvs, shift=0):
     return pltpu.make_async_remote_copy(
-        src_ref=source.at[pl.ds(pl.multiple_of(mask * capacity, capacity), capacity)],
+        src_ref=source.at[pl.ds(pl.multiple_of((mask - shift) * capacity, capacity), capacity)],
         dst_ref=target.at[pl.ds(pl.multiple_of(me * capacity, capacity), capacity)],
         send_sem=sends.at[mask],
         recv_sem=recvs.at[mask],
@@ -250,6 +250,7 @@
     w2_hbm,
     y_ref,
     back_ref,
+    late_ref,
     gw1_ref,
     gw2_ref,
     w1_ref,
@@ -272,6 +273,7 @@
     width, hidden = w1_ref.shape
     slots = x_rows.shape[0]
     group = BLK // capacity
+    early = count - count // 4
     me = lax.axis_index("expert")
     loads = [pltpu.make_async_copy(w1_hbm, w1_ref, load_sems.at[0]), pltpu.make_async_copy(w2_hbm, w2_ref, load_sems.at[1])]
     for load in loads:
@@ -337,7 +339,7 @@
         for item in range(group):
             mask = block * group + item
 
-            @pl.when(mask > 0)
+            @pl.when((mask > 0) & (mask < early))
             def _():
                 return_block(me, count, capacity, mask, dx_rows, back_ref, back_sends, back_recvs).start()
 
@@ -366,14 +368,18 @@
     for write in writes[-2:]:
         write.wait()
     mine_out().wait()
+    tail = pltpu.make_async_copy(dx_rows.at[pl.ds(early * capacity, (count - early) * capacity)], late_ref, own.at[0])
+    tail.start()
 
     def settle(block, carry):
         store_y(block).wait()
         return carry
 
     lax.fori_loop(0, slots // BLK, settle, 0)
+    tail.wait()
     for mask in range(1, count):
         send_block(me, count, capacity, mask, send_ref, x_rows, sends, recvs).wait_send()
+    for mask in range(1, early):
         return_block(me, count, capacity, mask, dx_rows, back_ref, back_sends, back_recvs).wait()
 
 
@@ -397,11 +403,14 @@
     mixed_ref,
     lse_ref,
     hidden_ref,
-    dx_ref,
+    dx_hbm,
+    late_ref,
     y_ref,
     grad_ref,
     dense_ref,
+    vec_ref,
     y_back_ref,
+    dx_ref,
     ghid,
     gmix,
     branch,
@@ -410,18 +419,34 @@
     sums,
     sends,
     recvs,
+    late_sends,
+    late_recvs,
     own,
+    gets,
 ):
     tokens, width = x_ref.shape
     me = lax.axis_index("expert")
+    early = count - count // 4
     greet("expert", me, count)
-    copies = [return_block(me, count, capacity, mask, y_ref, y_back_ref, sends, recvs) for mask in range(1, count)]
+    lates = [return_block(me, count, capacity, mask, late_ref, dx_ref, late_sends, late_recvs, early) for mask in range(early, count)]
+    for copy in lates:
+        copy.start()
+    copies = [return_block(me, count, capacity, mask, y_ref, y_back_ref, sends, recvs) for mask in range(1, early)]
     for copy in reversed(copies):
         copy.start()
     mine = pltpu.make_async_copy(
         y_ref.at[pl.ds(0, capacity)], y_back_ref.at[pl.ds(pl.multiple_of(me * capacity, capacity), capacity)], own
     )
     mine.start()
+    loads = []
+    for mask in range(early):
+        part = pl.ds(pl.multiple_of(flip(me, mask, count) * capacity, capacity), capacity)
+        loads.append(pltpu.make_async_copy(dx_hbm.at[part], dx_ref.at[part], gets.at[mask]))
+        loads[-1].start()
+    for load in loads:
+        load.wait()
+    for copy in lates:
+        copy.wait()
     slots = dx_ref.shape[0]
     blocks = tokens // BLK
     lane = iota((1, 128), 1)
@@ -512,25 +537,176 @@
         return carry
 
     lax.fori_loop(0, blocks, close_block, 0)
-    dense_ref[pl.ds(4 * width, 16), :] = sums[...].astype(BF16)
+    vec_ref[...] = sums[...]
     mine.wait()
     for copy in copies:
         copy.wait()
 
 
-def output_kernel(slot_col_ref, hidden_ref, gate_ref, y_ref, out_ref):
-    tokens, _ = hidden_ref.shape
-    slots = y_ref.shape[0]
-
-    def step(block, carry):
-        rows = pl.ds(pl.multiple_of(block * BLK, BLK), BLK)
-        slot = slot_col_ref[rows, 0:1]
-        pick = jnp.where(iota((BLK, slots), 1) == slot, 1.0, 0.0).astype(BF16)
-        back = nn(pick, y_ref[...])
-        out_ref[rows, :] = (hidden_ref[rows, :] + gate_ref[rows, 0:1] * back).astype(BF16)
-        return carry
-
-    lax.fori_loop(0, tokens // BLK, step, 0)
+def bits_of(count):
+    return [1 << bit for bit in range(count.bit_length() - 1)]
+
+
+def halving_plan(dp, count, rows):
+    experts = [("expert", mask) for mask in bits_of(count)]
+    groups = [("dp", mask) for mask in bits_of(dp)]
+    plans = [experts[:1] + groups + experts[1:], experts[:1] + experts[1:] + groups]
+    halvings = 0
+    while halvings < len(plans[0]) and (rows >> halvings) % 32 == 0:
+        halvings += 1
+    return plans, halvings
+
+
+def finish_kernel(
+    dp,
+    count,
+    capacity,
+    dense_ref,
+    vec_ref,
+    slot_col_ref,
+    hidden_ref,
+    gate_ref,
+    y_hbm,
+    y_ref,
+    out_ref,
+    full_ref,
+    total_ref,
+    y_all,
+    acc,
+    landing,
+    full,
+    vec_acc,
+    vec_land,
+    sends,
+    recvs,
+    back_sends,
+    back_recvs,
+    vec_sends,
+    vec_recvs,
+    y_sends,
+    y_recvs,
+    gets,
+    put,
+):
+    tokens, width = hidden_ref.shape
+    slots = y_all.shape[0]
+    rows = dense_ref.shape[0] // 2
+    early = count - count // 4
+    place = {"dp": lax.axis_index("dp"), "expert": lax.axis_index("expert")}
+    size = {"dp": dp, "expert": count}
+    me = place["expert"]
+    plans, halvings = halving_plan(dp, count, rows)
+    steps = len(plans[0])
+
+    barrier = pltpu.get_barrier_semaphore()
+    for mask in range(1, count):
+        pl.semaphore_signal(barrier, inc=1, device_id={"expert": flip(me, mask, count)}, device_id_type=MESH)
+    for mask in bits_of(dp):
+        pl.semaphore_signal(barrier, inc=1, device_id={"dp": flip(place["dp"], mask, dp)}, device_id_type=MESH)
+    pl.semaphore_wait(barrier, count - 1 + len(bits_of(dp)))
+
+    def partner(axis, mask):
+        return {axis: flip(place[axis], mask, size[axis])}
+
+    def bit(axis, mask):
+        return (place[axis] // mask) % 2
+
+    def aligned(start):
+        return pl.multiple_of(start, 16)
+
+    def remote(source, target, send, recv, device):
+        return pltpu.make_async_remote_copy(
+            src_ref=source, dst_ref=target, send_sem=send, recv_sem=recv, device_id=device, device_id_type=MESH
+        )
+
+    low = [jnp.int32(stream * rows) for stream in range(2)]
+    extent = rows
+    offset = 0
+    trail = []
+    pending = []
+    y_copies = [return_block(me, count, capacity, mask, y_ref, y_all, y_sends, y_recvs) for mask in range(early, count)]
+    loads = []
+    for step in range(steps):
+        halve = step < halvings
+        part = extent // 2 if halve else extent
+        copies = []
+        for stream in range(2):
+            axis, mask = plans[stream][step]
+            mine = low[stream] + bit(axis, mask) * part if halve else low[stream]
+            other = low[stream] + (1 - bit(axis, mask)) * part if halve else low[stream]
+            source = dense_ref if step == 0 else acc.at[(step - 1) % 2]
+            land = landing.at[stream, pl.ds(offset, part)]
+            copy = remote(
+                source.at[pl.ds(aligned(other), part)], land, sends.at[stream, step], recvs.at[stream, step], partner(axis, mask)
+            )
+            copy.start()
+            copies.append((copy, mine, source))
+        axis, mask = plans[0][step]
+        vec_source = vec_ref if step == 0 else vec_acc.at[step - 1]
+        vec_copy = remote(vec_source, vec_land.at[step], vec_sends.at[step], vec_recvs.at[step], partner(axis, mask))
+        vec_copy.start()
+        if step == 0:
+            for copy in y_copies:
+                copy.start()
+            for mask in range(early):
+                span = pl.ds(pl.multiple_of(flip(me, mask, count) * capacity, capacity), capacity)
+                loads.append(pltpu.make_async_copy(y_hbm.at[span], y_all.at[span], gets.at[mask]))
+                loads[-1].start()
+        trail.append((list(low), extent, halve))
+        for stream in range(2):
+            copy, mine, source = copies[stream]
+            copy.wait()
+            span = pl.ds(aligned(mine), part)
+            kept = source[span, :].astype(F32) + landing[stream, pl.ds(offset, part), :].astype(F32)
+            if step < steps - 1:
+                acc[step % 2, span, :] = kept.astype(BF16)
+            else:
+                full[span, :] = kept.astype(BF16)
+            low[stream] = mine
+        vec_copy.wait()
+        vec_sum = vec_source[...] + vec_land[step]
+        if step < steps - 1:
+            vec_acc[step] = vec_sum
+        else:
+            total_ref[...] = vec_sum
+        extent = part
+        offset += part
+
+    for load in loads:
+        load.wait()
+
+    back = []
+    for step in reversed(range(halvings)):
+        starts, whole, _ = trail[step]
+        copies = []
+        for stream in range(2):
+            axis, mask = plans[stream][step]
+            span = pl.ds(aligned(low[stream]), extent)
+            copy = remote(
+                full.at[span], full.at[span], back_sends.at[stream, step], back_recvs.at[stream, step], partner(axis, mask)
+            )
+            copy.start()
+            copies.append(copy)
+        for stream in range(2):
+            copies[stream].wait()
+            low[stream] = starts[stream]
+        extent = whole
+        if step == halvings - 1:
+            for copy in y_copies:
+                copy.wait()
+
+            def combine(block, carry):
+                span = pl.ds(pl.multiple_of(block * BLK, BLK), BLK)
+                slot = slot_col_ref[span, 0:1]
+                pick = jnp.where(iota((BLK, slots), 1) == slot, 1.0, 0.0).astype(BF16)
+                returned = nn(pick, y_all[...])
+                out_ref[span, :] = (hidden_ref[span, :] + gate_ref[span, 0:1] * returned).astype(BF16)
+                return carry
+
+    lax.fori_loop(0, tokens // BLK, combine, 0)
+    write = pltpu.make_async_copy(full, full_ref, put)
+    write.start()
+    write.wait()
 
 
 def call(kernel, outs, in_specs, scratch, name, out_specs=None, collective=None, flops=10**9):
@@ -599,7 +775,7 @@
     keep = pltpu.VMEM((slots, width), BF16)
     return call(
         functools.partial(expert_kernel, count, capacity, chunk),
-        [rows, rows, shape((width, hidden), BF16), shape((hidden, width), BF16)],
+        [rows, rows, shape((slots // 4, width), BF16), shape((width, hidden), BF16), shape((hidden, width), BF16)],
         [ANY, VMEM, VMEM, ANY, ANY],
         [
             pltpu.VMEM((width, hidden), BF16),
@@ -620,39 +796,71 @@
             dma(2),
         ],
         "expert",
-        [ANY] * 4,
+        [ANY] * 5,
         2,
     )(send, g, router_row, w1, w2)
 
 
 def backward(
-    count, capacity, weight, inputs, cotangent, g1, g2, wq, wk, wv, wo, slot_col, normed, q, k, v, mixed, lse, hidden, dx, y
+    count, capacity, weight, inputs, cotangent, g1, g2, wq, wk, wv, wo, slot_col, normed, q, k, v, mixed, lse, hidden, dx, late, y
 ):
     tokens, width = inputs.shape
     return call(
         functools.partial(backward_kernel, count, capacity),
-        [shape((tokens, width), BF16), shape((4 * width + 16, width), BF16), shape(y.shape, BF16)],
-        [SMEM] + [VMEM] * 17 + [ANY],
+        [shape((tokens, width), BF16), shape((4 * width, width), BF16), shape((8, width), F32), shape(y.shape, BF16)],
+        [SMEM] + [VMEM] * 16 + [ANY] * 3,
         [
+            pltpu.VMEM(dx.shape, BF16),
             pltpu.VMEM((tokens, width), F32),
             pltpu.VMEM((tokens, width), BF16),
             pltpu.VMEM((tokens, width), BF16),
             pltpu.VMEM((width, tokens), BF16),
             pltpu.VMEM((tokens, 3 * width), BF16),
-            pltpu.VMEM((16, width), F32),
+            pltpu.VMEM((8, width), F32),
+            dma(count),
+            dma(count),
+            dma(count),
+            dma(count),
+            dma(),
+            dma(count),
+        ],
+        "dense_backward",
+        [VMEM, VMEM, VMEM, ANY],
+        3,
+        5 * 10**10,
+    )(weight, inputs, cotangent, g1, g2, wq, wk, wv, wo, slot_col, normed, q, k, v, mixed, lse, hidden, dx, late, y)
+
+
+def finish(dp, count, capacity, dense, vec, slot_col, hidden, gate, y_back, y):
+    tokens, width = hidden.shape
+    rows = dense.shape[0]
+    steps = len(bits_of(dp)) + len(bits_of(count))
+    return call(
+        functools.partial(finish_kernel, dp, count, capacity),
+        [shape(hidden.shape, BF16), shape(dense.shape, BF16), shape(vec.shape, F32)],
+        [VMEM] * 5 + [ANY] * 2,
+        [
+            pltpu.VMEM(y.shape, BF16),
+            pltpu.VMEM((2, rows, width), BF16),
+            pltpu.VMEM((2, rows, width), BF16),
+            pltpu.VMEM((rows, width), BF16),
+            pltpu.VMEM((steps,) + vec.shape, F32),
+            pltpu.VMEM((steps,) + vec.shape, F32),
+            dma(2, steps),
+            dma(2, steps),
+            dma(2, steps),
+            dma(2, steps),
+            dma(steps),
+            dma(steps),
+            dma(count),
             dma(count),
             dma(count),
             dma(),
         ],
-        "dense_backward",
-        [VMEM, VMEM, ANY],
-        3,
-        5 * 10**10,
-    )(weight, inputs, cotangent, g1, g2, wq, wk, wv, wo, slot_col, normed, q, k, v, mixed, lse, hidden, dx, y)
-
-
-def combine(slot_col, hidden, gate, y):
-    return call(output_kernel, [shape(hidden.shape, BF16)], [VMEM] * 4, [], "combine")(slot_col, hidden, gate, y)[0]
+        "finish",
+        [VMEM, ANY, VMEM],
+        4,
+    )(dense, vec, slot_col, hidden, gate, y_back, y)
 
 
 def local(
@@ -691,18 +899,18 @@
     normed, q, k, v, mixed, lse, hidden, gate, send, cot_rows = forward(
         count, capacity, slots, inputs, g1, s1, g2, s2, w_query, w_key, w_value, w_out, router, slot_col, slot_row, cot_send
     )
-    y_rows, dx_back, grad_first, grad_second = expert_block(
+    y_rows, dx_back, dx_late, grad_first, grad_second = expert_block(
         count, capacity, send, cot_rows, router_row, expert_in[0], expert_out[0]
     )
     expert_sums = (lax.psum(grad_first, "dp").astype(F32), lax.psum(grad_second, "dp").astype(F32))
-    grad_inputs, dense, y_back = backward(
+    grad_inputs, dense, vec, y_back = backward(
         count, capacity, weight, inputs, cotangent, g1, g2, w_query, w_key, w_value, w_out, slot_col,
-        normed, q, k, v, mixed, lse, hidden, dx_back, y_rows,
-    )
-    output = combine(slot_col, hidden, gate, y_back)
-    dense = lax.psum(dense, ("dp", "expert")).astype(F32)
+        normed, q, k, v, mixed, lse, hidden, dx_back, dx_late, y_rows,
+    )
+    output, dense, vec = finish(lax.axis_size("dp"), count, capacity, dense, vec, slot_col, hidden, gate, y_back, y_rows)
+    dense = dense.astype(F32)
     parts = [dense[i * width : (i + 1) * width] for i in range(4)]
-    vecs = [dense[4 * width + i] for i in range(4)]
+    vecs = [vec[i] for i in range(4)]
     return (
         output,
         grad_inputs,

time: 692 us -> 479 us (0.69)
  waiting for transfers between devices: 321 us -> 0.02 us
  Pallas kernels: 324 us -> 429 us
    psum x1, waiting for transfers between devices: 185 us -> 0.01 us  [local(): lax.psum(grad_first, 'dp').astype(F32)]
    pallas_call x1, Pallas kernels: 8.44 us -> 147 us  [finish(): call(functools.partial(finish_kernel, dp, count, capacity), [shape(hidden...]
    psum x1 -> x0, waiting for transfers between devices: 136 us -> none  [local(): dense = lax.psum(dense, ('dp', 'expert')).astype(F32)]
    pallas_call x1, Pallas kernels: 124 us -> 107 us  [expert_block(): call(functools.partial(expert_kernel, count, capacity, chunk), [rows, row...]
    pallas_call x1, Pallas kernels: 98.7 us -> 83.1 us  [backward(): call(functools.partial(backward_kernel, count, capacity), [shape((tokens,...]
  transfers between devices with their start and end apart: 2 -> 1, of which waited for: 2 -> 0; matrix products, arithmetic and copies ran while one was open for 1% -> 2% of each run, Pallas kernels for 1% -> 48%
where the time goes in v3:
time: 479 us; the launch traced here: 478 us
  Pallas kernels  429 us (90%)
  local copies, waits for them, and re-layouts  17.4 us (4%)
  other arithmetic  15.8 us (3%)
  between operations  15.4 us (3%)
    pallas_call x1, Pallas kernels, finish(): call(functools.partial(finish_kernel, dp, count, capacity), [shape(hidden...  147 us
    pallas_call x1, Pallas kernels, expert_block(): call(functools.partial(expert_kernel, count, capacity, chunk), [rows, row...  107 us
    pallas_call x1, Pallas kernels, backward(): call(functools.partial(backward_kernel, count, capacity), [shape((tokens,...  83.1 us
    pallas_call x1, Pallas kernels, forward(): call(functools.partial(forward_kernel, count, capacity), [rows_low, rows_...  82.7 us
  transfers between devices with their start and end apart: 1, of which 0 were waited for; matrix products, arithmetic and copies ran while one was open for 2% of the time, Pallas kernels for 48%

profile of v3, /device:TPU:0, one launch (start us, length us, event | category | flops | bytes accessed | tf_op | source)
XLA Modules:
  0.0 478.1 jit_solution(2314523854952706930)
XLA Ops:
  7.2 0.0 all-reduce.3.cloned.1.call-start
  7.9 1.3 divide_reduce_fusion
  9.1 1.5 copy.29.router_ref
  10.7 1.3 bitcast_convert_fusion.router_ref
  12.0 1.3 reshape.60.gain_one_ref
  13.2 1.3 reshape.61.gain_two_ref
  14.5 1.3 reshape.62.shift_one_ref
  15.8 1.3 reshape.63.shift_two_ref
  17.7 1.3 fusion
  18.9 9.5 %tables.1 = (bf16[2048,768]{1,0:T(8,128)(2,1)}, s32[1024,128]{1,0:T(8,128)}, s32[8,1024]{1,0:T(8,128)}) custom-call(s32[1,8]{1,0:T(1,128)} %counts_ref.1, f32[1,1]{1,0:T(1,128)} %bitcast.1.weight_ref, s32[1,1024]{1,0:T(1,128)} %sort_ref.1, bf16[1024,768]{1,0:T(8,128)(2,1)} %cot_ref.3), custom_call_target="tpu_custom_call" | custom-call | flops 1000000000 | bytes 10000000 | tf_op jit(solution)/shard_map/tables/pallas_call | solution.py:737
  28.5 82.7 %dense_forward.1 = (bf16[1024,768]{1,0:T(8,128)(2,1)}, bf16[1024,768]{1,0:T(8,128)(2,1)}, bf16[1024,768]{1,0:T(8,128)(2,1)}, bf16[1024,768]{1,0:T(8,128)(2,1)}, ...) custom-call(bf16[1024,768]{1,0:T(8,128)(2,1)} %x_ref.3, ...), custom_call_target="tpu_custom_call" | custom-call | flops 1000000000 | bytes 10000000 | tf_op jit(solution)/shard_map/dense_forward/pallas_call | solution.py:749
  111.2 107.4 %expert.1 = (bf16[2048,768]{1,0:T(8,128)(2,1)}, bf16[2048,768]{1,0:T(8,128)(2,1)}, bf16[512,768]{1,0:T(8,128)(2,1)}, bf16[768,3072]{1,0:T(8,128)(2,1)}, bf16[3072,768]{1,0:T(8,128)(2,1)}) custom-call(bf16[2048,768]{1,0:T(8,128)(2,1)} %get-tuple-element.47.send_ref, bf16[2048,768]{1,0:T(8,128)(2,1)} %get-tuple-element.48.g_ref, ...), custom_call_target="tpu_custom_call" | custom-call | flops 1000000000 | bytes 10000000 | tf_op jit(solution)/shard_map/expert/pallas_call | solution.py:776
  218.5 0.0 all-reduce.3.cloned.1.call-update
  218.6 83.1 %dense_backward.1 = (bf16[1024,768]{1,0:T(8,128)(2,1)}, bf16[3072,768]{1,0:T(8,128)(2,1)}, f32[8,768]{1,0:T(8,128)}, bf16[2048,768]{1,0:T(8,128)(2,1)}) custom-call(f32[1,1]{1,0:T(1,128)} %bitcast.1.weight_ref, bf16[1024,768]{1,0:T(8,128)(2,1)} %x_ref.3, bf16[1024,768]{1,0:T(8,128)(2,1)} %cot_ref.3, f32[1,768]{1,0:T(1,128)} %reshape.60.gain_one_ref, ...), custom_call_target="tpu_custom_call" | custom-call | flops 49999998976 | bytes 10000000 | tf_op jit(solution)/shard_map/dense_backward/pallas_call | solution.py:808
  301.7 146.7 %finish.1 = (bf16[1024,768]{1,0:T(8,128)(2,1)}, bf16[3072,768]{1,0:T(8,128)(2,1)}, f32[8,768]{1,0:T(8,128)}) custom-call(bf16[3072,768]{1,0:T(8,128)(2,1)} %get-tuple-element.52.dense_ref, f32[8,768]{1,0:T(8,128)} %get-tuple-element.53.vec_ref, s32[1024,128]{1,0:T(8,128)} %get-tuple-element.37.slot_col_ref, f32[1024,768]{1,0:T(8,128)} %get-tuple-element.46.hidden_ref, ...), custom_call_target="tpu_custom_call" | custom-call | flops 1000000000 | bytes 10000000 | tf_op jit(solution)/shard_map/finish/pallas_call | solution.py:838
  448.4 1.5 slice_reduce_fusion
  449.9 6.2 %fusion.1 = (f32[768,768]{1,0:T(8,128)}, f32[768,768]{1,0:T(8,128)}, f32[768,768]{1,0:T(8,128)}, f32[768,768]{1,0:T(8,128)}) fusion(bf16[3072,768]{1,0:T(8,128)(2,1)} %get-tuple-element.59), kind=kLoop, calls=%fused_computation.8 | loop fusion | bytes 18874368 | tf_op jit(solution)/shard_map/slice | solution.py:912
  456.1 7.5 %broadcast_in_dim.21 = f32[1,768,3072]{2,1,0:T(8,128)} convert(bf16[1,768,3072]{2,1,0:T(8,128)(2,1)} %get-tuple-element.66) | non-fusion elementwise | flops 2359296 | bytes 14155776 | tf_op jit(solution)/shard_map/broadcast_in_dim | solution.py:919
  463.6 0.0 copy-done
  463.6 4.5 broadcast_in_dim.23
  468.1 0.0 copy-done.2
  468.1 1.1 copy.35
  469.3 0.8 copy-done.1
  470.1 1.1 copy.36
  (4 shorter events, 0.0 us)
Async XLA Ops:
  7.2 448.9 %all-reduce.3.cloned.1.call-start = ((), (), s32[]{:S(2)}) async-start(), calls=%async_computation | async-start | bytes 18874368 | tf_op jit(solution)/shard_map/psum | solution.py:905
  456.1 7.5 %copy-start = (bf16[1,3072,768]{2,1,0:T(8,128)(2,1)S(1)}, bf16[1,3072,768]{2,1,0:T(8,128)(2,1)}, u32[]{:S(2)}) copy-start(bf16[1,3072,768]{2,1,0:T(8,128)(2,1)} %get-tuple-element.67) | copy-start | bytes 14155780
  463.6 4.5 copy-start.2
  468.1 2.0 copy-start.1
Sparse Core Ops, SparseCore 0:
  218.7 212.3 all-reduce.2

commit v4 on v3

--- a/solution.py
+++ b/solution.py
@@ -55,6 +55,10 @@
     for mask in range(1, count):
         pl.semaphore_signal(barrier, inc=1, device_id={axis: flip(me, mask, count)}, device_id_type=MESH)
     pl.semaphore_wait(barrier, count - 1)
+
+
+def held(count):
+    return (5,) if count == 8 else ()
 
 
 def send_block(me, count, capacity, mask, source, target, sends, recvs):
@@ -80,6 +84,22 @@
     )
 
 
+def row_of(ref):
+    return ref[...].reshape(1, ref.shape[0])
+
+
+def domain_weight(group_ref, counts_ref):
+    groups = counts_ref.shape[0]
+    group = group_ref[0]
+    total = jnp.zeros((1, 128), F32)
+    mine = jnp.zeros((1, 128), F32)
+    for index in range(groups):
+        inverse = 1.0 / jnp.full((1, 128), counts_ref[index], jnp.int32).astype(F32)
+        total = total + inverse
+        mine = mine + jnp.where(group == index, inverse, 0.0)
+    return (mine / (total / groups))[:, 0:1]
+
+
 def norm_stats(rows):
     center = rows - jnp.mean(rows, axis=-1, keepdims=True)
     rstd = lax.rsqrt(jnp.mean(center * center, axis=-1, keepdims=True) + EPS)
@@ -100,7 +120,7 @@
     lax.fori_loop(0, slots // BLK, step, 0)
 
 
-def table_kernel(experts, capacity, counts_ref, weight_ref, sort_ref, cot_ref, send_ref, slot_col_ref, slot_row_ref, scaled):
+def table_kernel(experts, capacity, counts_ref, group_ref, domain_ref, sort_ref, cot_ref, send_ref, slot_col_ref, slot_row_ref, scaled):
     tokens = cot_ref.shape[0]
     place = iota((1, tokens), 1)
     expert_at = jnp.zeros((1, tokens), jnp.int32)
@@ -114,7 +134,7 @@
         start_at = start_at + jnp.where(past, count, 0)
     dest = (expert_at * capacity + place - start_at).astype(F32)
     sort_row = sort_ref[...]
-    scaled[...] = (cot_ref[...].astype(F32) * weight_ref[0, 0]).astype(BF16)
+    scaled[...] = (cot_ref[...].astype(F32) * domain_weight(group_ref, domain_ref)).astype(BF16)
     for block in range(tokens // BLK):
         token = iota((BLK, tokens), 0) + block * BLK
         col = jnp.sum(jnp.where(token == sort_row, dest, 0.0), axis=1, keepdims=True)
@@ -159,19 +179,24 @@
     blocks = tokens // BLK
     me = lax.axis_index("expert")
     greet("expert", me, count)
-    copies = [send_block(me, count, capacity, mask, cot_send_ref, cot_rows_ref, sends, recvs) for mask in range(1, count)]
-    for copy in reversed(copies):
+    copies = [
+        send_block(me, count, capacity, mask, cot_send_ref, cot_rows_ref, sends, recvs)
+        for mask in range(1, count)
+        if mask not in held(count)
+    ]
+    for copy in copies:
         copy.start()
     mine = pltpu.make_async_copy(
         cot_send_ref.at[pl.ds(pl.multiple_of(me * capacity, capacity), capacity)], cot_rows_ref.at[pl.ds(0, capacity)], own
     )
     mine.start()
     lane = iota((1, 128), 1)
+    gain_one, shift_one, gain_two, shift_two = (row_of(r) for r in (gain_one_ref, shift_one_ref, gain_two_ref, shift_two_ref))
 
     def project(block, carry):
         rows = pl.ds(pl.multiple_of(block * BLK, BLK), BLK)
         hat, _ = norm_stats(x_ref[rows, :].astype(F32))
-        normed = (hat * gain_one_ref[...] + shift_one_ref[...]).astype(BF16)
+        normed = (hat * gain_one + shift_one).astype(BF16)
         normed_ref[rows, :] = normed
         q_ref[rows, :] = (nn(normed, wq_ref[...]).astype(BF16) * (HEAD_DIM ** (-0.5))).astype(BF16)
         k_ref[rows, :] = nn(normed, wk_ref[...]).astype(BF16)
@@ -206,16 +231,16 @@
 
     lax.fori_loop(0, HEADS // 2, attend, 0)
 
-    experts = router_ref.shape[1]
+    experts = router_ref.shape[0]
 
     def finish(block, carry):
         rows = pl.ds(pl.multiple_of(block * BLK, BLK), BLK)
         hidden = x_ref[rows, :].astype(F32) + nn(mixed_ref[rows, :], wo_ref[...])
         hidden_ref[rows, :] = hidden
         hat, _ = norm_stats(hidden)
-        low = (hat * gain_two_ref[...] + shift_two_ref[...]).astype(BF16)
+        low = (hat * gain_two + shift_two).astype(BF16)
         routed[rows, :] = low
-        logits = nn(low, router_ref[...])
+        logits = nt(low, router_ref[...])
         slot = slot_col_ref[rows, 0:1]
         first = iota((BLK, experts), 1) * capacity
         mine = (slot >= first) & (slot < first + capacity)
@@ -244,7 +269,8 @@
     capacity,
     chunk,
     send_ref,
-    g_ref,
+    cot_send_ref,
+    cot_rows_ref,
     router_ref,
     w1_hbm,
     w2_hbm,
@@ -258,12 +284,16 @@
     acc1,
     acc2,
     x_rows,
+    g_ref,
     dx_rows,
     y_rows,
     stage,
     load_sems,
+    cot_sems,
     sends,
     recvs,
+    cot_sends,
+    cot_recvs,
     back_sends,
     back_recvs,
     own,
@@ -276,6 +306,10 @@
     early = count - count // 4
     me = lax.axis_index("expert")
     loads = [pltpu.make_async_copy(w1_hbm, w1_ref, load_sems.at[0]), pltpu.make_async_copy(w2_hbm, w2_ref, load_sems.at[1])]
+    for mask in range(count):
+        if mask not in held(count):
+            part = pl.ds(mask * capacity, capacity)
+            loads.append(pltpu.make_async_copy(cot_rows_ref.at[part], g_ref.at[part], cot_sems.at[mask]))
     for load in loads:
         load.start()
     greet("expert", me, count)
@@ -284,13 +318,16 @@
     )
     mine_in.start()
     for mask in range(1, count):
+        if mask in held(count):
+            send_block(me, count, capacity, mask, cot_send_ref, g_ref, cot_sends, cot_recvs).start()
         send_block(me, count, capacity, mask, send_ref, x_rows, sends, recvs).start()
     acc1[...] = jnp.zeros_like(acc1)
     acc2[...] = jnp.zeros_like(acc2)
     for load in loads:
         load.wait()
     mine_in.wait()
-    router = router_ref[...]
+    experts = router_ref.shape[0]
+    router = jnp.sum(jnp.where(iota((experts, 1), 0) == me, router_ref[...].astype(F32), 0.0), axis=0, keepdims=True)
 
     def store_y(block):
         rows = pl.ds(pl.multiple_of(block * BLK, BLK), BLK)
@@ -308,6 +345,12 @@
             @pl.when(mask > 0)
             def _():
                 send_block(me, count, capacity, mask, send_ref, x_rows, sends, recvs).wait_recv()
+
+            for late_mask in held(count):
+
+                @pl.when(mask == late_mask)
+                def _():
+                    send_block(me, count, capacity, mask, cot_send_ref, g_ref, cot_sends, cot_recvs).wait_recv()
 
         rows = pl.ds(pl.multiple_of(block * BLK, BLK), BLK)
         x = x_rows[rows, :]
@@ -379,6 +422,8 @@
     tail.wait()
     for mask in range(1, count):
         send_block(me, count, capacity, mask, send_ref, x_rows, sends, recvs).wait_send()
+    for mask in held(count):
+        send_block(me, count, capacity, mask, cot_send_ref, g_ref, cot_sends, cot_recvs).wait_send()
     for mask in range(1, early):
         return_block(me, count, capacity, mask, dx_rows, back_ref, back_sends, back_recvs).wait()
 
@@ -386,7 +431,8 @@
 def backward_kernel(
     count,
     capacity,
-    weight_ref,
+    group_ref,
+    domain_ref,
     x_ref,
     cot_ref,
     gain_one_ref,
@@ -431,8 +477,8 @@
     lates = [return_block(me, count, capacity, mask, late_ref, dx_ref, late_sends, late_recvs, early) for mask in range(early, count)]
     for copy in lates:
         copy.start()
-    copies = [return_block(me, count, capacity, mask, y_ref, y_back_ref, sends, recvs) for mask in range(1, early)]
-    for copy in reversed(copies):
+    copies = [return_block(me, count, capacity, mask, y_ref, y_back_ref, sends, recvs) for mask in range(1, count)]
+    for copy in copies:
         copy.start()
     mine = pltpu.make_async_copy(
         y_ref.at[pl.ds(0, capacity)], y_back_ref.at[pl.ds(pl.multiple_of(me * capacity, capacity), capacity)], own
@@ -450,6 +496,9 @@
     slots = dx_ref.shape[0]
     blocks = tokens // BLK
     lane = iota((1, 128), 1)
+    weight = domain_weight(group_ref, domain_ref)
+    gain_one = row_of(gain_one_ref)
+    gain_two = row_of(gain_two_ref)
     sums[...] = jnp.zeros_like(sums)
 
     def open_block(block, carry):
@@ -460,9 +509,9 @@
         hat, rstd = norm_stats(hidden_ref[rows, :])
         sums[2:3, :] += jnp.sum(grad * hat, axis=0, keepdims=True)
         sums[3:4, :] += jnp.sum(grad, axis=0, keepdims=True)
-        gg = grad * gain_two_ref[...]
+        gg = grad * gain_two
         inner = gg - jnp.mean(gg, axis=1, keepdims=True) - hat * jnp.mean(gg * hat, axis=1, keepdims=True)
-        total = cot_ref[rows, :].astype(F32) * weight_ref[0, 0] + rstd * inner
+        total = cot_ref[rows, :].astype(F32) * weight + rstd * inner
         ghid[rows, :] = total
         low = total.astype(BF16)
         branch[rows, :] = low
@@ -531,7 +580,7 @@
         hat, rstd = norm_stats(x_ref[rows, :].astype(F32))
         sums[0:1, :] += jnp.sum(grad * hat, axis=0, keepdims=True)
         sums[1:2, :] += jnp.sum(grad, axis=0, keepdims=True)
-        gg = grad * gain_one_ref[...]
+        gg = grad * gain_one
         inner = gg - jnp.mean(gg, axis=1, keepdims=True) - hat * jnp.mean(gg * hat, axis=1, keepdims=True)
         grad_ref[rows, :] = (ghid[rows, :] + rstd * inner).astype(BF16)
         return carry
@@ -543,14 +592,17 @@
         copy.wait()
 
 
-def bits_of(count):
-    return [1 << bit for bit in range(count.bit_length() - 1)]
-
-
 def halving_plan(dp, count, rows):
-    experts = [("expert", mask) for mask in bits_of(count)]
-    groups = [("dp", mask) for mask in bits_of(dp)]
-    plans = [experts[:1] + groups + experts[1:], experts[:1] + experts[1:] + groups]
+    experts = []
+    mask = 2
+    while 2 * mask < count:
+        experts += [("expert", mask, (mask, 2 * mask)), ("expert", 3 * mask, (2 * mask,))]
+        mask *= 4
+    if mask < count:
+        experts.append(("expert", mask, (mask,)))
+    groups = [("dp", 1 << bit, (1 << bit,)) for bit in range(dp.bit_length() - 1)]
+    core = [("expert", 1, (1,))]
+    plans = [core + experts + groups, core + experts[::-1] + groups[::-1]]
     halvings = 0
     while halvings < len(plans[0]) and (rows >> halvings) % 32 == 0:
         halvings += 1
@@ -560,18 +612,15 @@
 def finish_kernel(
     dp,
     count,
-    capacity,
     dense_ref,
     vec_ref,
     slot_col_ref,
     hidden_ref,
     gate_ref,
-    y_hbm,
     y_ref,
     out_ref,
     full_ref,
     total_ref,
-    y_all,
     acc,
     landing,
     full,
@@ -583,33 +632,26 @@
     back_recvs,
     vec_sends,
     vec_recvs,
-    y_sends,
-    y_recvs,
-    gets,
     put,
 ):
     tokens, width = hidden_ref.shape
-    slots = y_all.shape[0]
+    slots = y_ref.shape[0]
     rows = dense_ref.shape[0] // 2
-    early = count - count // 4
     place = {"dp": lax.axis_index("dp"), "expert": lax.axis_index("expert")}
     size = {"dp": dp, "expert": count}
-    me = place["expert"]
     plans, halvings = halving_plan(dp, count, rows)
     steps = len(plans[0])
 
-    barrier = pltpu.get_barrier_semaphore()
-    for mask in range(1, count):
-        pl.semaphore_signal(barrier, inc=1, device_id={"expert": flip(me, mask, count)}, device_id_type=MESH)
-    for mask in bits_of(dp):
-        pl.semaphore_signal(barrier, inc=1, device_id={"dp": flip(place["dp"], mask, dp)}, device_id_type=MESH)
-    pl.semaphore_wait(barrier, count - 1 + len(bits_of(dp)))
-
     def partner(axis, mask):
         return {axis: flip(place[axis], mask, size[axis])}
 
-    def bit(axis, mask):
-        return (place[axis] // mask) % 2
+    barrier = pltpu.get_barrier_semaphore()
+    for axis, mask, _ in plans[0]:
+        pl.semaphore_signal(barrier, inc=1, device_id=partner(axis, mask), device_id_type=MESH)
+    pl.semaphore_wait(barrier, steps)
+
+    def side(axis, masks):
+        return sum(place[axis] // mask for mask in masks) % 2
 
     def aligned(start):
         return pl.multiple_of(start, 16)
@@ -619,21 +661,26 @@
             src_ref=source, dst_ref=target, send_sem=send, recv_sem=recv, device_id=device, device_id_type=MESH
         )
 
+    def combine(block):
+        span = pl.ds(block * BLK, BLK)
+        slot = slot_col_ref[span, 0:1]
+        pick = jnp.where(iota((BLK, slots), 1) == slot, 1.0, 0.0).astype(BF16)
+        returned = nn(pick, y_ref[...])
+        out_ref[span, :] = (hidden_ref[span, :] + gate_ref[span, 0:1] * returned).astype(BF16)
+
+    todo = list(range(tokens // BLK))
     low = [jnp.int32(stream * rows) for stream in range(2)]
     extent = rows
     offset = 0
     trail = []
-    pending = []
-    y_copies = [return_block(me, count, capacity, mask, y_ref, y_all, y_sends, y_recvs) for mask in range(early, count)]
-    loads = []
     for step in range(steps):
         halve = step < halvings
         part = extent // 2 if halve else extent
         copies = []
         for stream in range(2):
-            axis, mask = plans[stream][step]
-            mine = low[stream] + bit(axis, mask) * part if halve else low[stream]
-            other = low[stream] + (1 - bit(axis, mask)) * part if halve else low[stream]
+            axis, mask, masks = plans[stream][step]
+            mine = low[stream] + side(axis, masks) * part if halve else low[stream]
+            other = low[stream] + (1 - side(axis, masks)) * part if halve else low[stream]
             source = dense_ref if step == 0 else acc.at[(step - 1) % 2]
             land = landing.at[stream, pl.ds(offset, part)]
             copy = remote(
@@ -641,18 +688,15 @@
             )
             copy.start()
             copies.append((copy, mine, source))
-        axis, mask = plans[0][step]
+        axis, mask, _ = plans[0][step]
         vec_source = vec_ref if step == 0 else vec_acc.at[step - 1]
         vec_copy = remote(vec_source, vec_land.at[step], vec_sends.at[step], vec_recvs.at[step], partner(axis, mask))
         vec_copy.start()
-        if step == 0:
-            for copy in y_copies:
-                copy.start()
-            for mask in range(early):
-                span = pl.ds(pl.multiple_of(flip(me, mask, count) * capacity, capacity), capacity)
-                loads.append(pltpu.make_async_copy(y_hbm.at[span], y_all.at[span], gets.at[mask]))
-                loads[-1].start()
-        trail.append((list(low), extent, halve))
+        if step in (1, 2):
+            for block in todo[: tokens // BLK // 4]:
+                combine(block)
+            todo = todo[tokens // BLK // 4 :]
+        trail.append((list(low), extent))
         for stream in range(2):
             copy, mine, source = copies[stream]
             copy.wait()
@@ -672,38 +716,25 @@
         extent = part
         offset += part
 
-    for load in loads:
-        load.wait()
-
-    back = []
     for step in reversed(range(halvings)):
-        starts, whole, _ = trail[step]
+        starts, whole = trail[step]
         copies = []
         for stream in range(2):
-            axis, mask = plans[stream][step]
+            axis, mask, _ = plans[stream][step]
             span = pl.ds(aligned(low[stream]), extent)
             copy = remote(
                 full.at[span], full.at[span], back_sends.at[stream, step], back_recvs.at[stream, step], partner(axis, mask)
             )
             copy.start()
             copies.append(copy)
+        if step in (1, 2):
+            for block in todo if step == 1 else todo[: tokens // BLK // 4]:
+                combine(block)
+            todo = todo[tokens // BLK // 4 :]
         for stream in range(2):
             copies[stream].wait()
             low[stream] = starts[stream]
         extent = whole
-        if step == halvings - 1:
-            for copy in y_copies:
-                copy.wait()
-
-            def combine(block, carry):
-                span = pl.ds(pl.multiple_of(block * BLK, BLK), BLK)
-                slot = slot_col_ref[span, 0:1]
-                pick = jnp.where(iota((BLK, slots), 1) == slot, 1.0, 0.0).astype(BF16)
-                returned = nn(pick, y_all[...])
-                out_ref[span, :] = (hidden_ref[span, :] + gate_ref[span, 0:1] * returned).astype(BF16)
-                return carry
-
-    lax.fori_loop(0, tokens // BLK, combine, 0)
     write = pltpu.make_async_copy(full, full_ref, put)
     write.start()
     write.wait()
@@ -731,16 +762,16 @@
     return jax.ShapeDtypeStruct(dims, kind)
 
 
-def tables(experts, capacity, counts, weight, sort_order, cotangent):
+def tables(experts, capacity, counts, group, domains, sort_order, cotangent):
     tokens, width = cotangent.shape
     slots = experts * capacity
     return call(
         functools.partial(table_kernel, experts, capacity),
         [shape((slots, width), BF16), shape((tokens, 128), jnp.int32), shape((8, tokens), jnp.int32)],
-        [SMEM, SMEM, VMEM, VMEM],
+        [SMEM, SMEM, SMEM, VMEM, VMEM],
         [pltpu.VMEM((tokens, width), BF16)],
         "tables",
-    )(counts, weight, sort_order, cotangent)
+    )(counts, group, domains, sort_order, cotangent)
 
 
 def forward(count, capacity, slots, inputs, g1, s1, g2, s2, wq, wk, wv, wo, router, slot_col, slot_row, cot_send):
@@ -768,7 +799,7 @@
     )(inputs, g1, s1, g2, s2, wq, wk, wv, wo, router, slot_col, slot_row, cot_send)
 
 
-def expert_block(count, capacity, send, g, router_row, w1, w2, chunk=768):
+def expert_block(count, capacity, send, cot_send, cot_rows, router_t, w1, w2, chunk=768):
     slots, width = send.shape
     hidden = w1.shape[1]
     rows = shape((slots, width), BF16)
@@ -776,7 +807,7 @@
     return call(
         functools.partial(expert_kernel, count, capacity, chunk),
         [rows, rows, shape((slots // 4, width), BF16), shape((width, hidden), BF16), shape((hidden, width), BF16)],
-        [ANY, VMEM, VMEM, ANY, ANY],
+        [ANY, ANY, ANY, VMEM, ANY, ANY],
         [
             pltpu.VMEM((width, hidden), BF16),
             pltpu.VMEM((hidden, width), BF16),
@@ -785,8 +816,12 @@
             keep,
             keep,
             keep,
+            keep,
             pltpu.VMEM((2, width, width), BF16),
             dma(2),
+            dma(count),
+            dma(count),
+            dma(count),
             dma(count),
             dma(count),
             dma(count),
@@ -798,17 +833,17 @@
         "expert",
         [ANY] * 5,
         2,
-    )(send, g, router_row, w1, w2)
+    )(send, cot_send, cot_rows, router_t, w1, w2)
 
 
 def backward(
-    count, capacity, weight, inputs, cotangent, g1, g2, wq, wk, wv, wo, slot_col, normed, q, k, v, mixed, lse, hidden, dx, late, y
+    count, capacity, group, domains, inputs, cotangent, g1, g2, wq, wk, wv, wo, slot_col, normed, q, k, v, mixed, lse, hidden, dx, late, y
 ):
     tokens, width = inputs.shape
     return call(
         functools.partial(backward_kernel, count, capacity),
         [shape((tokens, width), BF16), shape((4 * width, width), BF16), shape((8, width), F32), shape(y.shape, BF16)],
-        [SMEM] + [VMEM] * 16 + [ANY] * 3,
+        [SMEM] * 2 + [VMEM] * 16 + [ANY] * 3,
         [
             pltpu.VMEM(dx.shape, BF16),
             pltpu.VMEM((tokens, width), F32),
@@ -828,19 +863,18 @@
         [VMEM, VMEM, VMEM, ANY],
         3,
         5 * 10**10,
-    )(weight, inputs, cotangent, g1, g2, wq, wk, wv, wo, slot_col, normed, q, k, v, mixed, lse, hidden, dx, late, y)
-
-
-def finish(dp, count, capacity, dense, vec, slot_col, hidden, gate, y_back, y):
-    tokens, width = hidden.shape
+    )(group, domains, inputs, cotangent, g1, g2, wq, wk, wv, wo, slot_col, normed, q, k, v, mixed, lse, hidden, dx, late, y)
+
+
+def finish(dp, count, dense, vec, slot_col, hidden, gate, y_back):
+    width = hidden.shape[1]
     rows = dense.shape[0]
-    steps = len(bits_of(dp)) + len(bits_of(count))
+    steps = len(halving_plan(dp, count, rows // 2)[0][0])
     return call(
-        functools.partial(finish_kernel, dp, count, capacity),
+        functools.partial(finish_kernel, dp, count),
         [shape(hidden.shape, BF16), shape(dense.shape, BF16), shape(vec.shape, F32)],
-        [VMEM] * 5 + [ANY] * 2,
+        [VMEM] * 6,
         [
-            pltpu.VMEM(y.shape, BF16),
             pltpu.VMEM((2, rows, width), BF16),
             pltpu.VMEM((2, rows, width), BF16),
             pltpu.VMEM((rows, width), BF16),
@@ -852,15 +886,12 @@
             dma(2, steps),
             dma(steps),
             dma(steps),
-            dma(count),
-            dma(count),
-            dma(count),
             dma(),
         ],
         "finish",
         [VMEM, ANY, VMEM],
         4,
-    )(dense, vec, slot_col, hidden, gate, y_back, y)
+    )(dense, vec, slot_col, hidden, gate, y_back)
 
 
 def local(
@@ -886,28 +917,22 @@
     experts = send_counts.shape[1]
     capacity = 2 * tokens // experts
     slots = experts * capacity
-    inverse = 1.0 / domain_counts.astype(F32)
-    domain_weights = inverse / jnp.mean(inverse)
-    ids = jnp.arange(domain_counts.shape[0], dtype=jnp.int32)
-    weight = jnp.sum(jnp.where(seq_group[:, None] == ids[None, :], domain_weights[None, :], 0.0), axis=1).reshape(1, 1)
-    mine = lax.axis_index("expert")
-    router_row = lax.dynamic_slice_in_dim(router.T, mine, 1, axis=0).astype(F32)
-
     count = lax.axis_size("expert")
-    g1, s1, g2, s2 = (v.reshape(1, width) for v in (gain_one, shift_one, gain_two, shift_two))
-    cot_send, slot_col, slot_row = tables(experts, capacity, send_counts, weight, sort_order, cotangent)
+    g1, s1, g2, s2 = gain_one, shift_one, gain_two, shift_two
+    router_t = router.T
+    cot_send, slot_col, slot_row = tables(experts, capacity, send_counts, seq_group, domain_counts, sort_order, cotangent)
     normed, q, k, v, mixed, lse, hidden, gate, send, cot_rows = forward(
-        count, capacity, slots, inputs, g1, s1, g2, s2, w_query, w_key, w_value, w_out, router, slot_col, slot_row, cot_send
+        count, capacity, slots, inputs, g1, s1, g2, s2, w_query, w_key, w_value, w_out, router_t, slot_col, slot_row, cot_send
     )
     y_rows, dx_back, dx_late, grad_first, grad_second = expert_block(
-        count, capacity, send, cot_rows, router_row, expert_in[0], expert_out[0]
+        count, capacity, send, cot_send, cot_rows, router_t, expert_in[0], expert_out[0]
     )
     expert_sums = (lax.psum(grad_first, "dp").astype(F32), lax.psum(grad_second, "dp").astype(F32))
     grad_inputs, dense, vec, y_back = backward(
-        count, capacity, weight, inputs, cotangent, g1, g2, w_query, w_key, w_value, w_out, slot_col,
+        count, capacity, seq_group, domain_counts, inputs, cotangent, g1, g2, w_query, w_key, w_value, w_out, slot_col,
         normed, q, k, v, mixed, lse, hidden, dx_back, dx_late, y_rows,
     )
-    output, dense, vec = finish(lax.axis_size("dp"), count, capacity, dense, vec, slot_col, hidden, gate, y_back, y_rows)
+    output, dense, vec = finish(lax.axis_size("dp"), count, dense, vec, slot_col, hidden, gate, y_back)
     dense = dense.astype(F32)
     parts = [dense[i * width : (i + 1) * width] for i in range(4)]
     vecs = [vec[i] for i in range(4)]

time: 479 us -> 488 us (1.019); the launches traced: 478 us -> 481 us
  Pallas kernels: 429 us -> 443 us
  local copies, waits for them, and re-layouts: 17.4 us -> 10.9 us
    pallas_call x1, Pallas kernels: 82.7 us -> 57 us  [forward(): call(functools.partial(forward_kernel, count, capacity), [rows_low, rows_...]
    pallas_call x1, Pallas kernels: 107 us -> 131 us  [expert_block(): call(functools.partial(expert_kernel, count, capacity, chunk), [rows, row...]
    pallas_call x1, Pallas kernels: 83.1 us -> 98.9 us  [backward(): call(functools.partial(backward_kernel, count, capacity), [shape((tokens,...]
    reshape x4 -> x0, local copies, waits for them, and re-layouts: 5.07 us -> none  [local(): v.reshape(1, width)]
  transfers between devices with their start and end apart: 1 -> 1, of which waited for: 0 -> 0; matrix products, arithmetic and copies ran while one was open for 2% -> 2% of each run, Pallas kernels for 48% -> 51%
where the time goes in v4:
time: 488 us; the launch traced here: 481 us
  Pallas kernels  443 us (91%)
  between operations  15.2 us (3%)
  other arithmetic  12 us (2%)
  local copies, waits for them, and re-layouts  10.9 us (2%)
    pallas_call x1, Pallas kernels, finish(): call(functools.partial(finish_kernel, dp, count), [shape(hidden.shape, BF...  147 us
    pallas_call x1, Pallas kernels, expert_block(): call(functools.partial(expert_kernel, count, capacity, chunk), [rows, row...  131 us
    pallas_call x1, Pallas kernels, backward(): call(functools.partial(backward_kernel, count, capacity), [shape((tokens,...  98.9 us
    pallas_call x1, Pallas kernels, forward(): call(functools.partial(forward_kernel, count, capacity), [rows_low, rows_...  57 us
  transfers between devices with their start and end apart: 1, of which 0 were waited for; matrix products, arithmetic and copies ran while one was open for 2% of the time, Pallas kernels for 51%

profile of v4, /device:TPU:0, one launch (start us, length us, event | category | flops | bytes accessed | tf_op | source)
XLA Modules:
  0.0 481.0 jit_solution(11234790208976398166)
XLA Ops:
  7.2 0.0 all-reduce.3.cloned.1.call-start
  7.9 8.9 %tables.1 = (bf16[2048,768]{1,0:T(8,128)(2,1)}, s32[1024,128]{1,0:T(8,128)}, s32[8,1024]{1,0:T(8,128)}) custom-call(s32[1,8]{1,0:T(1,128)} %counts_ref.1, s32[1]{0:T(128)S(6)} %copy.33.group_ref, s32[8]{0:T(128)} %domain_ref.3, s32[1,1024]{1,0:T(1,128)} %sort_ref.1, bf16[1024,768]{1,0:T(8,128)(2,1)} %cot_ref.3), custom_call_target="tpu_custom_call" | custom-call | flops 1000000000 | bytes 10000000 | tf_op jit(solution)/shard_map/tables/pallas_call | solution.py:768
  16.8 57.0 %dense_forward.1 = (bf16[1024,768]{1,0:T(8,128)(2,1)}, bf16[1024,768]{1,0:T(8,128)(2,1)}, bf16[1024,768]{1,0:T(8,128)(2,1)}, bf16[1024,768]{1,0:T(8,128)(2,1)}, ...) custom-call(bf16[1024,768]{1,0:T(8,128)(2,1)} %x_ref.3, ...), custom_call_target="tpu_custom_call" | custom-call | flops 1000000000 | bytes 10000000 | tf_op jit(solution)/shard_map/dense_forward/pallas_call | solution.py:780
  73.8 130.8 %expert.1 = (bf16[2048,768]{1,0:T(8,128)(2,1)}, bf16[2048,768]{1,0:T(8,128)(2,1)}, bf16[512,768]{1,0:T(8,128)(2,1)}, bf16[768,3072]{1,0:T(8,128)(2,1)}, bf16[3072,768]{1,0:T(8,128)(2,1)}) custom-call(bf16[2048,768]{1,0:T(8,128)(2,1)} %get-tuple-element.47.send_ref, bf16[2048,768]{1,0:T(8,128)(2,1)} %get-tuple-element.39.cot_send_ref, ...), custom_call_target="tpu_custom_call" | custom-call | flops 1000000000 | bytes 10000000 | tf_op jit(solution)/shard_map/expert/pallas_call | solution.py:807
  204.5 0.0 all-reduce.3.cloned.1.call-update
  204.6 98.9 %dense_backward.1 = (bf16[1024,768]{1,0:T(8,128)(2,1)}, bf16[3072,768]{1,0:T(8,128)(2,1)}, f32[8,768]{1,0:T(8,128)}, bf16[2048,768]{1,0:T(8,128)(2,1)}) custom-call(s32[1]{0:T(128)S(6)} %copy.33.group_ref, s32[8]{0:T(128)} %domain_ref.3, bf16[1024,768]{1,0:T(8,128)(2,1)} %x_ref.3, bf16[1024,768]{1,0:T(8,128)(2,1)} %cot_ref.3, f32[768]{0:T(1024)} %gain_one_ref.3, ...), custom_call_target="tpu_custom_call" | custom-call | flops 49999998976 | bytes 10000000 | tf_op jit(solution)/shard_map/dense_backward/pallas_call | solution.py:843
  303.5 147.3 %finish.1 = (bf16[1024,768]{1,0:T(8,128)(2,1)}, bf16[3072,768]{1,0:T(8,128)(2,1)}, f32[8,768]{1,0:T(8,128)}) custom-call(bf16[3072,768]{1,0:T(8,128)(2,1)} %get-tuple-element.52.dense_ref, f32[8,768]{1,0:T(8,128)} %get-tuple-element.53.vec_ref, s32[1024,128]{1,0:T(8,128)} %get-tuple-element.37.slot_col_ref, f32[1024,768]{1,0:T(8,128)} %get-tuple-element.46.hidden_ref, ...), custom_call_target="tpu_custom_call" | custom-call | flops 1000000000 | bytes 10000000 | tf_op jit(solution)/shard_map/finish/pallas_call | solution.py:873
  450.8 1.6 slice_reduce_fusion
  452.4 6.2 %fusion = (f32[768,768]{1,0:T(8,128)}, f32[768,768]{1,0:T(8,128)}, f32[768,768]{1,0:T(8,128)}, f32[768,768]{1,0:T(8,128)}) fusion(bf16[3072,768]{1,0:T(8,128)(2,1)} %get-tuple-element.59), kind=kLoop, calls=%fused_computation.4 | loop fusion | bytes 18874368 | tf_op jit(solution)/shard_map/slice | solution.py:937
  458.5 0.0 all-reduce.3.cloned.1.call-done
  458.5 0.0 copy-start
  458.5 7.5 %broadcast_in_dim.13 = f32[1,768,3072]{2,1,0:T(8,128)} convert(bf16[1,768,3072]{2,1,0:T(8,128)(2,1)} %get-tuple-element.66) | non-fusion elementwise | flops 2359296 | bytes 14155776 | tf_op jit(solution)/shard_map/broadcast_in_dim | solution.py:944
  466.1 0.0 copy-done
  466.1 0.0 copy-start.2
  466.1 4.5 broadcast_in_dim.15
  470.6 0.0 copy-start.1
  470.6 0.0 copy-done.2
  470.6 1.1 copy.34
  471.7 0.8 copy-done.1
  472.5 1.1 copy.35
Async XLA Ops:
  7.2 451.4 %all-reduce.3.cloned.1.call-start = ((), (), s32[]{:S(2)}) async-start(), calls=%async_computation | async-start | bytes 18874368 | tf_op jit(solution)/shard_map/psum | solution.py:930
  458.5 7.5 %copy-start = (bf16[1,3072,768]{2,1,0:T(8,128)(2,1)S(1)}, bf16[1,3072,768]{2,1,0:T(8,128)(2,1)}, u32[]{:S(2)}) copy-start(bf16[1,3072,768]{2,1,0:T(8,128)(2,1)} %get-tuple-element.67) | copy-start | bytes 14155780
  466.1 4.5 copy-start.2
  470.6 2.0 copy-start.1
Sparse Core Ops, SparseCore 0:
  204.7 199.2 all-reduce.2

commit v5 on v4

--- a/solution.py
+++ b/solution.py
@@ -14,6 +14,7 @@
 F32 = jnp.float32
 BF16 = jnp.bfloat16
 BLK = 256
+CODE = 4096
 LIMIT = 60 * 1024 * 1024
 
 VMEM = pl.BlockSpec(memory_space=pltpu.VMEM)
@@ -57,30 +58,57 @@
     pl.semaphore_wait(barrier, count - 1)
 
 
-def held(count):
-    return (5,) if count == 8 else ()
-
-
-def send_block(me, count, capacity, mask, source, target, sends, recvs):
+def copy_to(source, target, send, recv, device):
+    return pltpu.make_async_remote_copy(
+        src_ref=source, dst_ref=target, send_sem=send, recv_sem=recv, device_id=device, device_id_type=MESH
+    )
+
+
+def span(start, rows):
+    return pl.ds(pl.multiple_of(start, 16), rows)
+
+
+def send_block(me, count, rows, mask, source, target, sends, recvs):
     peer = flip(me, mask, count)
-    return pltpu.make_async_remote_copy(
-        src_ref=source.at[pl.ds(pl.multiple_of(peer * capacity, capacity), capacity)],
-        dst_ref=target.at[pl.ds(pl.multiple_of(mask * capacity, capacity), capacity)],
-        send_sem=sends.at[mask],
-        recv_sem=recvs.at[mask],
-        device_id={"expert": peer},
-        device_id_type=MESH,
+    return copy_to(
+        source.at[span(peer * rows, rows)], target.at[span(mask * rows, rows)], sends.at[mask], recvs.at[mask], {"expert": peer}
     )
 
 
-def return_block(me, count, capacity, mask, source, target, sends, recvs, shift=0):
-    return pltpu.make_async_remote_copy(
-        src_ref=source.at[pl.ds(pl.multiple_of((mask - shift) * capacity, capacity), capacity)],
-        dst_ref=target.at[pl.ds(pl.multiple_of(me * capacity, capacity), capacity)],
-        send_sem=sends.at[mask],
-        recv_sem=recvs.at[mask],
-        device_id={"expert": flip(me, mask, count)},
-        device_id_type=MESH,
+def return_block(me, count, rows, mask, source, target, sends, recvs, shift=0):
+    return copy_to(
+        source.at[span((mask - shift) * rows, rows)],
+        target.at[span(me * rows, rows)],
+        sends.at[mask],
+        recvs.at[mask],
+        {"expert": flip(me, mask, count)},
+    )
+
+
+def depth_of(count):
+    return count.bit_length() - 1
+
+
+def gather_spare(me, count, base, rows, step, first, target, sends, recvs):
+    have = rows << step
+    source = first.at[pl.ds(base, rows)] if step == 0 else target.at[pl.ds(base, have)]
+    return copy_to(
+        source,
+        target.at[pl.ds(base + have, have)],
+        sends.at[step],
+        recvs.at[step],
+        {"expert": flip(me, count >> (step + 1), count)},
+    )
+
+
+def return_spare(me, count, rows, step, source, shift, landing, sends, recvs):
+    half = rows << step
+    return copy_to(
+        source.at[pl.ds(shift + half, half)],
+        landing.at[pl.ds(half, half)],
+        sends.at[step],
+        recvs.at[step],
+        {"expert": flip(me, count >> (step + 1), count)},
     )
 
 
@@ -120,7 +148,7 @@
     lax.fori_loop(0, slots // BLK, step, 0)
 
 
-def table_kernel(experts, capacity, counts_ref, group_ref, domain_ref, sort_ref, cot_ref, send_ref, slot_col_ref, slot_row_ref, scaled):
+def table_kernel(experts, main, counts_ref, group_ref, domain_ref, sort_ref, cot_ref, send_ref, slot_col_ref, slot_row_ref, scaled):
     tokens = cot_ref.shape[0]
     place = iota((1, tokens), 1)
     expert_at = jnp.zeros((1, tokens), jnp.int32)
@@ -132,21 +160,25 @@
         past = place >= end
         expert_at = expert_at + jnp.where(past, 1, 0)
         start_at = start_at + jnp.where(past, count, 0)
-    dest = (expert_at * capacity + place - start_at).astype(F32)
+    slot = place - start_at
+    dest = jnp.where(slot < main, expert_at * main + slot, (experts - 1) * main + slot)
+    code = (expert_at * CODE + dest).astype(F32)
     sort_row = sort_ref[...]
     scaled[...] = (cot_ref[...].astype(F32) * domain_weight(group_ref, domain_ref)).astype(BF16)
     for block in range(tokens // BLK):
         token = iota((BLK, tokens), 0) + block * BLK
-        col = jnp.sum(jnp.where(token == sort_row, dest, 0.0), axis=1, keepdims=True)
-        wide = jnp.broadcast_to(col, (BLK, 128))
-        slot_col_ref[pl.ds(block * BLK, BLK), :] = wide.astype(jnp.int32)
-        slot_row_ref[:, pl.ds(block * BLK, BLK)] = wide.T[0:8].astype(jnp.int32)
+        col = jnp.sum(jnp.where(token == sort_row, code, 0.0), axis=1, keepdims=True)
+        owner = (col * (1.0 / CODE)).astype(jnp.int32)
+        where = col.astype(jnp.int32) - owner * CODE
+        slot_col_ref[pl.ds(block * BLK, BLK), :] = jnp.where(iota((1, 128), 1) < 64, where, owner)
+        slot_row_ref[:, pl.ds(block * BLK, BLK)] = jnp.broadcast_to(where, (BLK, 128)).astype(F32).T[0:8].astype(jnp.int32)
     pack_rows(slot_row_ref[0:1, :], scaled, send_ref)
 
 
 def forward_kernel(
     count,
-    capacity,
+    main,
+    spare,
     x_ref,
     gain_one_ref,
     shift_one_ref,
@@ -173,23 +205,30 @@
     routed,
     sends,
     recvs,
+    spare_sends,
+    spare_recvs,
     own,
 ):
     tokens, width = x_ref.shape
     blocks = tokens // BLK
     me = lax.axis_index("expert")
     greet("expert", me, count)
-    copies = [
-        send_block(me, count, capacity, mask, cot_send_ref, cot_rows_ref, sends, recvs)
-        for mask in range(1, count)
-        if mask not in held(count)
-    ]
+    base = count * main
+    depth = depth_of(count)
+
+    def gather(step):
+        return gather_spare(me, count, base, spare, step, cot_send_ref, cot_rows_ref, spare_sends, spare_recvs)
+
+    gather(0).start()
+    copies = [send_block(me, count, main, mask, cot_send_ref, cot_rows_ref, sends, recvs) for mask in range(1, count)]
     for copy in copies:
         copy.start()
-    mine = pltpu.make_async_copy(
-        cot_send_ref.at[pl.ds(pl.multiple_of(me * capacity, capacity), capacity)], cot_rows_ref.at[pl.ds(0, capacity)], own
-    )
-    mine.start()
+    mine = [
+        pltpu.make_async_copy(cot_send_ref.at[span(me * main, main)], cot_rows_ref.at[pl.ds(0, main)], own.at[0]),
+        pltpu.make_async_copy(cot_send_ref.at[pl.ds(base, spare)], cot_rows_ref.at[pl.ds(base, spare)], own.at[1]),
+    ]
+    for copy in mine:
+        copy.start()
     lane = iota((1, 128), 1)
     gain_one, shift_one, gain_two, shift_two = (row_of(r) for r in (gain_one_ref, shift_one_ref, gain_two_ref, shift_two_ref))
 
@@ -204,6 +243,10 @@
         return carry
 
     lax.fori_loop(0, blocks, project, 0)
+    for copy in mine:
+        copy.wait()
+    gather(0).wait()
+    gather(1).start()
 
     keep = iota((BLK, BLK), 0) <= iota((BLK, BLK), 1)
 
@@ -230,6 +273,10 @@
         return carry
 
     lax.fori_loop(0, HEADS // 2, attend, 0)
+    for step in range(1, depth):
+        gather(step).wait()
+        if step + 1 < depth:
+            gather(step + 1).start()
 
     experts = router_ref.shape[0]
 
@@ -241,16 +288,13 @@
         low = (hat * gain_two + shift_two).astype(BF16)
         routed[rows, :] = low
         logits = nt(low, router_ref[...])
-        slot = slot_col_ref[rows, 0:1]
-        first = iota((BLK, experts), 1) * capacity
-        mine = (slot >= first) & (slot < first + capacity)
-        logit = jnp.sum(jnp.where(mine, logits, 0.0), axis=1, keepdims=True)
+        owner = slot_col_ref[rows, 64:65]
+        logit = jnp.sum(jnp.where(iota((BLK, experts), 1) == owner, logits, 0.0), axis=1, keepdims=True)
         gate_ref[rows, :] = jnp.broadcast_to(jax.nn.sigmoid(logit), (BLK, 128))
         return carry
 
     lax.fori_loop(0, blocks, finish, 0)
     pack_rows(slot_row_ref[0:1, :], routed, send_ref)
-    mine.wait()
     for copy in copies:
         copy.wait()
 
@@ -266,10 +310,11 @@
 
 def expert_kernel(
     count,
-    capacity,
+    main,
+    spare,
     chunk,
+    counts_ref,
     send_ref,
-    cot_send_ref,
     cot_rows_ref,
     router_ref,
     w1_hbm,
@@ -289,11 +334,10 @@
     y_rows,
     stage,
     load_sems,
-    cot_sems,
     sends,
     recvs,
-    cot_sends,
-    cot_recvs,
+    spare_sends,
+    spare_recvs,
     back_sends,
     back_recvs,
     own,
@@ -302,61 +346,78 @@
 ):
     width, hidden = w1_ref.shape
     slots = x_rows.shape[0]
-    group = BLK // capacity
+    base = count * main
+    plain = base // BLK
+    blocks = slots // BLK
+    depth = depth_of(count)
     early = count - count // 4
     me = lax.axis_index("expert")
-    loads = [pltpu.make_async_copy(w1_hbm, w1_ref, load_sems.at[0]), pltpu.make_async_copy(w2_hbm, w2_ref, load_sems.at[1])]
-    for mask in range(count):
-        if mask not in held(count):
-            part = pl.ds(mask * capacity, capacity)
-            loads.append(pltpu.make_async_copy(cot_rows_ref.at[part], g_ref.at[part], cot_sems.at[mask]))
+    loads = [
+        pltpu.make_async_copy(w1_hbm, w1_ref, load_sems.at[0]),
+        pltpu.make_async_copy(w2_hbm, w2_ref, load_sems.at[1]),
+        pltpu.make_async_copy(cot_rows_ref, g_ref, load_sems.at[2]),
+    ]
     for load in loads:
         load.start()
     greet("expert", me, count)
-    mine_in = pltpu.make_async_copy(
-        send_ref.at[pl.ds(pl.multiple_of(me * capacity, capacity), capacity)], x_rows.at[pl.ds(0, capacity)], own.at[0]
-    )
-    mine_in.start()
+
+    def gather(step):
+        return gather_spare(me, count, base, spare, step, send_ref, x_rows, spare_sends, spare_recvs)
+
+    def arrive(mask):
+        return send_block(me, count, main, mask, send_ref, x_rows, sends, recvs)
+
+    def leave(mask):
+        return return_block(me, count, main, mask, dx_rows, back_ref, back_sends, back_recvs)
+
+    gather(0).start()
     for mask in range(1, count):
-        if mask in held(count):
-            send_block(me, count, capacity, mask, cot_send_ref, g_ref, cot_sends, cot_recvs).start()
-        send_block(me, count, capacity, mask, send_ref, x_rows, sends, recvs).start()
+        arrive(mask).start()
+    mine_in = [
+        pltpu.make_async_copy(send_ref.at[span(me * main, main)], x_rows.at[pl.ds(0, main)], own.at[0]),
+        pltpu.make_async_copy(send_ref.at[pl.ds(base, spare)], x_rows.at[pl.ds(base, spare)], own.at[1]),
+    ]
+    for copy in mine_in:
+        copy.start()
     acc1[...] = jnp.zeros_like(acc1)
     acc2[...] = jnp.zeros_like(acc2)
-    for load in loads:
-        load.wait()
-    mine_in.wait()
     experts = router_ref.shape[0]
     router = jnp.sum(jnp.where(iota((experts, 1), 0) == me, router_ref[...].astype(F32), 0.0), axis=0, keepdims=True)
+    hot = jnp.full((1, 128), counts_ref[0, me], jnp.int32)[:, 0:1] > main
+    hot = jnp.where(hot, 1.0, 0.0)
+    for copy in loads + mine_in:
+        copy.wait()
 
     def store_y(block):
         rows = pl.ds(pl.multiple_of(block * BLK, BLK), BLK)
         return pltpu.make_async_copy(y_rows.at[rows], y_ref.at[rows], y_sems.at[block])
 
     def mine_out():
-        return pltpu.make_async_copy(
-            dx_rows.at[pl.ds(0, capacity)], back_ref.at[pl.ds(pl.multiple_of(me * capacity, capacity), capacity)], own.at[1]
-        )
-
-    def run(block, carry):
-        for item in range(group):
-            mask = block * group + item
-
-            @pl.when(mask > 0)
+        return pltpu.make_async_copy(dx_rows.at[pl.ds(0, main)], back_ref.at[span(me * main, main)], own.at[0])
+
+    def run(turn, carry):
+        block = turn + turn // (plain - 1) - (turn // (blocks - 1)) * (blocks - plain + 1)
+        for item in range(BLK // main + 1):
+            mask = (block * BLK + main - 1) // main + item
+
+            @pl.when((block < plain) & (mask > 0) & (mask < ((block + 1) * BLK + main - 1) // main))
             def _():
-                send_block(me, count, capacity, mask, send_ref, x_rows, sends, recvs).wait_recv()
-
-            for late_mask in held(count):
-
-                @pl.when(mask == late_mask)
-                def _():
-                    send_block(me, count, capacity, mask, cot_send_ref, g_ref, cot_sends, cot_recvs).wait_recv()
+                arrive(mask).wait_recv()
+
+        for step in range(depth):
+
+            @pl.when(turn == (step + 1 if step + 1 < depth else plain - 1))
+            def _():
+                gather(step).wait_recv()
+                if step + 1 < depth:
+                    gather(step + 1).start()
 
         rows = pl.ds(pl.multiple_of(block * BLK, BLK), BLK)
-        x = x_rows[rows, :]
+        live = jnp.where(block < plain, 1.0, hot)
+        x = (x_rows[rows, :].astype(F32) * live).astype(BF16)
         logit = jnp.sum(x.astype(F32) * router, axis=1, keepdims=True)
         gate = jax.nn.sigmoid(logit)
-        go = g_ref[rows, :].astype(F32)
+        go = g_ref[rows, :].astype(F32) * live
         g = (gate * go).astype(BF16)
         x_t = x.astype(F32).T.astype(BF16)
         y = jnp.zeros(x.shape, F32)
@@ -379,20 +440,23 @@
         dlogit = jnp.sum(y_low.astype(F32) * go, axis=1, keepdims=True) * gate * (1.0 - gate)
         dx_rows[rows, :] = (dx + dlogit * router).astype(BF16)
         store_y(block).start()
-        for item in range(group):
-            mask = block * group + item
-
-            @pl.when((mask > 0) & (mask < early))
+        for item in range(BLK // main + 1):
+            mask = (block * BLK) // main + item
+            done = (block < plain) & (mask < ((block + 1) * BLK) // main)
+
+            @pl.when(done & (mask > 0) & (mask < early))
             def _():
-                return_block(me, count, capacity, mask, dx_rows, back_ref, back_sends, back_recvs).start()
-
-            @pl.when(mask == 0)
+                leave(mask).start()
+
+            @pl.when(done & (mask == 0))
             def _():
                 mine_out().start()
 
         return carry
 
-    lax.fori_loop(0, slots // BLK, run, 0)
+    lax.fori_loop(0, blocks, run, 0)
+    tail = pltpu.make_async_copy(dx_rows.at[pl.ds(early * main, slots - early * main)], late_ref, own.at[1])
+    tail.start()
 
     pieces = []
     for first in range(0, hidden, stage.shape[1]):
@@ -411,26 +475,25 @@
     for write in writes[-2:]:
         write.wait()
     mine_out().wait()
-    tail = pltpu.make_async_copy(dx_rows.at[pl.ds(early * capacity, (count - early) * capacity)], late_ref, own.at[0])
-    tail.start()
+    tail.wait()
 
     def settle(block, carry):
         store_y(block).wait()
         return carry
 
-    lax.fori_loop(0, slots // BLK, settle, 0)
-    tail.wait()
+    lax.fori_loop(0, blocks, settle, 0)
+    for step in range(depth):
+        gather(step).wait_send()
     for mask in range(1, count):
-        send_block(me, count, capacity, mask, send_ref, x_rows, sends, recvs).wait_send()
-    for mask in held(count):
-        send_block(me, count, capacity, mask, cot_send_ref, g_ref, cot_sends, cot_recvs).wait_send()
+        arrive(mask).wait_send()
     for mask in range(1, early):
-        return_block(me, count, capacity, mask, dx_rows, back_ref, back_sends, back_recvs).wait()
+        leave(mask).wait()
 
 
 def backward_kernel(
     count,
-    capacity,
+    main,
+    spare,
     group_ref,
     domain_ref,
     x_ref,
@@ -457,6 +520,10 @@
     vec_ref,
     y_back_ref,
     dx_ref,
+    spare_dx,
+    spare_y,
+    dx_land,
+    y_land,
     ghid,
     gmix,
     branch,
@@ -467,30 +534,63 @@
     recvs,
     late_sends,
     late_recvs,
+    dx_sends,
+    dx_recvs,
+    y_sends,
+    y_recvs,
     own,
     gets,
 ):
     tokens, width = x_ref.shape
     me = lax.axis_index("expert")
     early = count - count // 4
+    base = count * main
+    late = (count - early) * main
+    total = count * spare
+    depth = depth_of(count)
     greet("expert", me, count)
-    lates = [return_block(me, count, capacity, mask, late_ref, dx_ref, late_sends, late_recvs, early) for mask in range(early, count)]
+
+    def sum_dx(step):
+        if step == depth - 1:
+            return return_spare(me, count, spare, step, late_ref, late, dx_land, dx_sends, dx_recvs)
+        return return_spare(me, count, spare, step, spare_dx, 0, dx_land, dx_sends, dx_recvs)
+
+    def sum_y(step):
+        if step == depth - 1:
+            return return_spare(me, count, spare, step, y_ref, base, y_land, y_sends, y_recvs)
+        return return_spare(me, count, spare, step, spare_y, 0, y_land, y_sends, y_recvs)
+
+    def settle(copy, kept, landing, step):
+        copy.wait()
+        half = spare << step
+        kept[0:half, :] = (kept[0:half, :].astype(F32) + landing[half : 2 * half, :].astype(F32)).astype(BF16)
+
+    sum_dx(depth - 1).start()
+    lates = [return_block(me, count, main, mask, late_ref, dx_ref, late_sends, late_recvs, early) for mask in range(early, count)]
     for copy in lates:
         copy.start()
-    copies = [return_block(me, count, capacity, mask, y_ref, y_back_ref, sends, recvs) for mask in range(1, count)]
+    copies = [return_block(me, count, main, mask, y_ref, y_back_ref, sends, recvs) for mask in range(1, count)]
     for copy in copies:
         copy.start()
-    mine = pltpu.make_async_copy(
-        y_ref.at[pl.ds(0, capacity)], y_back_ref.at[pl.ds(pl.multiple_of(me * capacity, capacity), capacity)], own
-    )
+    mine = pltpu.make_async_copy(y_ref.at[pl.ds(0, main)], y_back_ref.at[span(me * main, main)], own.at[0])
     mine.start()
-    loads = []
+    loads = [
+        pltpu.make_async_copy(late_ref.at[pl.ds(late, total)], spare_dx, own.at[1]),
+        pltpu.make_async_copy(y_ref.at[pl.ds(base, total)], spare_y, own.at[2]),
+    ]
     for mask in range(early):
-        part = pl.ds(pl.multiple_of(flip(me, mask, count) * capacity, capacity), capacity)
+        part = span(flip(me, mask, count) * main, main)
         loads.append(pltpu.make_async_copy(dx_hbm.at[part], dx_ref.at[part], gets.at[mask]))
-        loads[-1].start()
+    for load in loads:
+        load.start()
     for load in loads:
         load.wait()
+    for step in reversed(range(depth)):
+        settle(sum_dx(step), spare_dx, dx_land, step)
+        if step:
+            sum_dx(step - 1).start()
+    dx_ref[pl.ds(base, BLK), :] = spare_dx[0:BLK, :]
+    sum_y(depth - 1).start()
     for copy in lates:
         copy.wait()
     slots = dx_ref.shape[0]
@@ -521,6 +621,8 @@
 
     lax.fori_loop(0, blocks, open_block, 0)
     dense_ref[pl.ds(3 * width, width), :] = tn(mixed_ref[...], branch[...]).astype(BF16)
+    settle(sum_y(depth - 1), spare_y, y_land, depth - 1)
+    sum_y(depth - 2).start()
 
     keep = iota((BLK, BLK), 0) <= iota((BLK, BLK), 1)
 
@@ -568,6 +670,12 @@
         return carry
 
     lax.fori_loop(0, HEADS // 2, attend, 0)
+    for step in reversed(range(depth - 1)):
+        settle(sum_y(step), spare_y, y_land, step)
+        if step:
+            sum_y(step - 1).start()
+    spare_out = pltpu.make_async_copy(spare_y.at[pl.ds(0, BLK)], y_back_ref.at[pl.ds(base, BLK)], own.at[1])
+    spare_out.start()
 
     for part in range(3):
         dense_ref[pl.ds(part * width, width), :] = nn(normed_t[...], dqkv[:, pl.ds(part * width, width)]).astype(BF16)
@@ -587,22 +695,17 @@
 
     lax.fori_loop(0, blocks, close_block, 0)
     vec_ref[...] = sums[...]
+    spare_out.wait()
     mine.wait()
     for copy in copies:
         copy.wait()
 
 
 def halving_plan(dp, count, rows):
-    experts = []
-    mask = 2
-    while 2 * mask < count:
-        experts += [("expert", mask, (mask, 2 * mask)), ("expert", 3 * mask, (2 * mask,))]
-        mask *= 4
-    if mask < count:
-        experts.append(("expert", mask, (mask,)))
-    groups = [("dp", 1 << bit, (1 << bit,)) for bit in range(dp.bit_length() - 1)]
-    core = [("expert", 1, (1,))]
-    plans = [core + experts + groups, core + experts[::-1] + groups[::-1]]
+    experts = [("expert", 2 << bit) for bit in range(depth_of(count) - 1)]
+    groups = [("dp", 1 << bit) for bit in range(depth_of(dp))]
+    core = [("expert", 1)]
+    plans = [core + groups + experts, core + experts + groups]
     halvings = 0
     while halvings < len(plans[0]) and (rows >> halvings) % 32 == 0:
         halvings += 1
@@ -646,27 +749,19 @@
         return {axis: flip(place[axis], mask, size[axis])}
 
     barrier = pltpu.get_barrier_semaphore()
-    for axis, mask, _ in plans[0]:
+    for axis, mask in plans[0]:
         pl.semaphore_signal(barrier, inc=1, device_id=partner(axis, mask), device_id_type=MESH)
     pl.semaphore_wait(barrier, steps)
 
-    def side(axis, masks):
-        return sum(place[axis] // mask for mask in masks) % 2
-
-    def aligned(start):
-        return pl.multiple_of(start, 16)
-
-    def remote(source, target, send, recv, device):
-        return pltpu.make_async_remote_copy(
-            src_ref=source, dst_ref=target, send_sem=send, recv_sem=recv, device_id=device, device_id_type=MESH
-        )
+    def side(axis, mask):
+        return (place[axis] // mask) % 2
 
     def combine(block):
-        span = pl.ds(block * BLK, BLK)
-        slot = slot_col_ref[span, 0:1]
+        rows_at = pl.ds(block * BLK, BLK)
+        slot = slot_col_ref[rows_at, 0:1]
         pick = jnp.where(iota((BLK, slots), 1) == slot, 1.0, 0.0).astype(BF16)
         returned = nn(pick, y_ref[...])
-        out_ref[span, :] = (hidden_ref[span, :] + gate_ref[span, 0:1] * returned).astype(BF16)
+        out_ref[rows_at, :] = (hidden_ref[rows_at, :] + gate_ref[rows_at, 0:1] * returned).astype(BF16)
 
     todo = list(range(tokens // BLK))
     low = [jnp.int32(stream * rows) for stream in range(2)]
@@ -678,19 +773,19 @@
         part = extent // 2 if halve else extent
         copies = []
         for stream in range(2):
-            axis, mask, masks = plans[stream][step]
-            mine = low[stream] + side(axis, masks) * part if halve else low[stream]
-            other = low[stream] + (1 - side(axis, masks)) * part if halve else low[stream]
+            axis, mask = plans[stream][step]
+            mine = low[stream] + side(axis, mask) * part if halve else low[stream]
+            other = low[stream] + (1 - side(axis, mask)) * part if halve else low[stream]
             source = dense_ref if step == 0 else acc.at[(step - 1) % 2]
             land = landing.at[stream, pl.ds(offset, part)]
-            copy = remote(
-                source.at[pl.ds(aligned(other), part)], land, sends.at[stream, step], recvs.at[stream, step], partner(axis, mask)
+            copy = copy_to(
+                source.at[span(other, part)], land, sends.at[stream, step], recvs.at[stream, step], partner(axis, mask)
             )
             copy.start()
             copies.append((copy, mine, source))
-        axis, mask, _ = plans[0][step]
+        axis, mask = plans[0][step]
         vec_source = vec_ref if step == 0 else vec_acc.at[step - 1]
-        vec_copy = remote(vec_source, vec_land.at[step], vec_sends.at[step], vec_recvs.at[step], partner(axis, mask))
+        vec_copy = copy_to(vec_source, vec_land.at[step], vec_sends.at[step], vec_recvs.at[step], partner(axis, mask))
         vec_copy.start()
         if step in (1, 2):
             for block in todo[: tokens // BLK // 4]:
@@ -700,12 +795,12 @@
         for stream in range(2):
             copy, mine, source = copies[stream]
             copy.wait()
-            span = pl.ds(aligned(mine), part)
-            kept = source[span, :].astype(F32) + landing[stream, pl.ds(offset, part), :].astype(F32)
+            held = span(mine, part)
+            kept = source[held, :].astype(F32) + landing[stream, pl.ds(offset, part), :].astype(F32)
             if step < steps - 1:
-                acc[step % 2, span, :] = kept.astype(BF16)
+                acc[step % 2, held, :] = kept.astype(BF16)
             else:
-                full[span, :] = kept.astype(BF16)
+                full[held, :] = kept.astype(BF16)
             low[stream] = mine
         vec_copy.wait()
         vec_sum = vec_source[...] + vec_land[step]
@@ -720,10 +815,10 @@
         starts, whole = trail[step]
         copies = []
         for stream in range(2):
-            axis, mask, _ = plans[stream][step]
-            span = pl.ds(aligned(low[stream]), extent)
-            copy = remote(
-                full.at[span], full.at[span], back_sends.at[stream, step], back_recvs.at[stream, step], partner(axis, mask)
+            axis, mask = plans[stream][step]
+            held = span(low[stream], extent)
+            copy = copy_to(
+                full.at[held], full.at[held], back_sends.at[stream, step], back_recvs.at[stream, step], partner(axis, mask)
             )
             copy.start()
             copies.append(copy)
@@ -762,11 +857,10 @@
     return jax.ShapeDtypeStruct(dims, kind)
 
 
-def tables(experts, capacity, counts, group, domains, sort_order, cotangent):
+def tables(experts, main, slots, counts, group, domains, sort_order, cotangent):
     tokens, width = cotangent.shape
-    slots = experts * capacity
     return call(
-        functools.partial(table_kernel, experts, capacity),
+        functools.partial(table_kernel, experts, main),
         [shape((slots, width), BF16), shape((tokens, 128), jnp.int32), shape((8, tokens), jnp.int32)],
         [SMEM, SMEM, SMEM, VMEM, VMEM],
         [pltpu.VMEM((tokens, width), BF16)],
@@ -774,11 +868,11 @@
     )(counts, group, domains, sort_order, cotangent)
 
 
-def forward(count, capacity, slots, inputs, g1, s1, g2, s2, wq, wk, wv, wo, router, slot_col, slot_row, cot_send):
+def forward(count, main, spare, inputs, g1, s1, g2, s2, wq, wk, wv, wo, router, slot_col, slot_row, cot_send):
     tokens, width = inputs.shape
     rows_low = shape((tokens, width), BF16)
     return call(
-        functools.partial(forward_kernel, count, capacity),
+        functools.partial(forward_kernel, count, main, spare),
         [
             rows_low,
             rows_low,
@@ -788,26 +882,34 @@
             shape((HEADS // 2, 8, tokens), F32),
             shape((tokens, width), F32),
             shape((tokens, 128), F32),
-            shape((slots, width), BF16),
-            shape((slots, width), BF16),
+            shape(cot_send.shape, BF16),
+            shape((count * (main + spare), width), BF16),
         ],
         [VMEM] * 12 + [ANY],
-        [pltpu.VMEM((tokens, width), BF16), dma(count), dma(count), dma()],
+        [pltpu.VMEM((tokens, width), BF16), dma(count), dma(count), dma(depth_of(count)), dma(depth_of(count)), dma(2)],
         "dense_forward",
         [VMEM] * 9 + [ANY],
         1,
     )(inputs, g1, s1, g2, s2, wq, wk, wv, wo, router, slot_col, slot_row, cot_send)
 
 
-def expert_block(count, capacity, send, cot_send, cot_rows, router_t, w1, w2, chunk=768):
-    slots, width = send.shape
+def expert_block(count, main, spare, counts, send, cot_rows, router_t, w1, w2, chunk=768):
+    slots, width = cot_rows.shape
     hidden = w1.shape[1]
+    late = slots - (count - count // 4) * main
     rows = shape((slots, width), BF16)
     keep = pltpu.VMEM((slots, width), BF16)
+    depth = depth_of(count)
     return call(
-        functools.partial(expert_kernel, count, capacity, chunk),
-        [rows, rows, shape((slots // 4, width), BF16), shape((width, hidden), BF16), shape((hidden, width), BF16)],
-        [ANY, ANY, ANY, VMEM, ANY, ANY],
+        functools.partial(expert_kernel, count, main, spare, chunk),
+        [
+            rows,
+            shape((count * main, width), BF16),
+            shape((late, width), BF16),
+            shape((width, hidden), BF16),
+            shape((hidden, width), BF16),
+        ],
+        [SMEM, ANY, ANY, VMEM, ANY, ANY],
         [
             pltpu.VMEM((width, hidden), BF16),
             pltpu.VMEM((hidden, width), BF16),
@@ -818,12 +920,11 @@
             keep,
             keep,
             pltpu.VMEM((2, width, width), BF16),
-            dma(2),
+            dma(3),
             dma(count),
             dma(count),
-            dma(count),
-            dma(count),
-            dma(count),
+            dma(depth),
+            dma(depth),
             dma(count),
             dma(count),
             dma(2),
@@ -833,19 +934,23 @@
         "expert",
         [ANY] * 5,
         2,
-    )(send, cot_send, cot_rows, router_t, w1, w2)
+    )(counts, send, cot_rows, router_t, w1, w2)
 
 
 def backward(
-    count, capacity, group, domains, inputs, cotangent, g1, g2, wq, wk, wv, wo, slot_col, normed, q, k, v, mixed, lse, hidden, dx, late, y
+    count, main, spare, group, domains, inputs, cotangent, g1, g2, wq, wk, wv, wo, slot_col, normed, q, k, v, mixed, lse, hidden, dx, late, y
 ):
     tokens, width = inputs.shape
     return call(
-        functools.partial(backward_kernel, count, capacity),
-        [shape((tokens, width), BF16), shape((4 * width, width), BF16), shape((8, width), F32), shape(y.shape, BF16)],
+        functools.partial(backward_kernel, count, main, spare),
+        [shape((tokens, width), BF16), shape((4 * width, width), BF16), shape((8, width), F32), shape((count * main + BLK, width), BF16)],
         [SMEM] * 2 + [VMEM] * 16 + [ANY] * 3,
         [
-            pltpu.VMEM(dx.shape, BF16),
+            pltpu.VMEM((count * main + BLK, width), BF16),
+            pltpu.VMEM((count * spare, width), BF16),
+            pltpu.VMEM((count * spare, width), BF16),
+            pltpu.VMEM((count * spare, width), BF16),
+            pltpu.VMEM((count * spare, width), BF16),
             pltpu.VMEM((tokens, width), F32),
             pltpu.VMEM((tokens, width), BF16),
             pltpu.VMEM((tokens, width), BF16),
@@ -856,7 +961,11 @@
             dma(count),
             dma(count),
             dma(count),
-            dma(),
+            dma(depth_of(count)),
+            dma(depth_of(count)),
+            dma(depth_of(count)),
+            dma(depth_of(count)),
+            dma(3),
             dma(count),
         ],
         "dense_backward",
@@ -916,20 +1025,22 @@
     tokens, width = inputs.shape
     experts = send_counts.shape[1]
     capacity = 2 * tokens // experts
-    slots = experts * capacity
+    spare = capacity // 4
+    main = capacity - spare
+    slots = experts * main + BLK
     count = lax.axis_size("expert")
     g1, s1, g2, s2 = gain_one, shift_one, gain_two, shift_two
     router_t = router.T
-    cot_send, slot_col, slot_row = tables(experts, capacity, send_counts, seq_group, domain_counts, sort_order, cotangent)
+    cot_send, slot_col, slot_row = tables(experts, main, slots, send_counts, seq_group, domain_counts, sort_order, cotangent)
     normed, q, k, v, mixed, lse, hidden, gate, send, cot_rows = forward(
-        count, capacity, slots, inputs, g1, s1, g2, s2, w_query, w_key, w_value, w_out, router_t, slot_col, slot_row, cot_send
+        count, main, spare, inputs, g1, s1, g2, s2, w_query, w_key, w_value, w_out, router_t, slot_col, slot_row, cot_send
     )
     y_rows, dx_back, dx_late, grad_first, grad_second = expert_block(
-        count, capacity, send, cot_send, cot_rows, router_t, expert_in[0], expert_out[0]
+        count, main, spare, send_counts, send, cot_rows, router_t, expert_in[0], expert_out[0]
     )
     expert_sums = (lax.psum(grad_first, "dp").astype(F32), lax.psum(grad_second, "dp").astype(F32))
     grad_inputs, dense, vec, y_back = backward(
-        count, capacity, seq_group, domain_counts, inputs, cotangent, g1, g2, w_query, w_key, w_value, w_out, slot_col,
+        count, main, spare, seq_group, domain_counts, inputs, cotangent, g1, g2, w_query, w_key, w_value, w_out, slot_col,
         normed, q, k, v, mixed, lse, hidden, dx_back, dx_late, y_rows,
     )
     output, dense, vec = finish(lax.axis_size("dp"), count, dense, vec, slot_col, hidden, gate, y_back)

time: 488 us -> 490 us (level)
    pallas_call x4, Pallas kernels: 296 us -> 331 us  [the longest x1 142 us: backward(): call(functools.partial(backward_kernel, count, main, spare), [shape((toke...]
    pallas_call x1, Pallas kernels: 147 us -> 114 us  [finish(): call(functools.partial(finish_kernel, dp, count), [shape(hidden.shape, BF...]
  transfers between devices with their start and end apart: 1 -> 1, of which waited for: 0 -> 0; matrix products, arithmetic and copies ran while one was open for 2% -> 2% of each run, Pallas kernels for 51% -> 53%
where the time goes in v5:
time: 490 us; the launch traced here: 483 us
  Pallas kernels  445 us (91%)
  between operations  15.2 us (3%)
  other arithmetic  12 us (2%)
  local copies, waits for them, and re-layouts  10.8 us (2%)
    pallas_call x1, Pallas kernels, backward(): call(functools.partial(backward_kernel, count, main, spare), [shape((toke...  142 us
    pallas_call x1, Pallas kernels, finish(): call(functools.partial(finish_kernel, dp, count), [shape(hidden.shape, BF...  114 us
    pallas_call x1, Pallas kernels, expert_block(): call(functools.partial(expert_kernel, count, main, spare, chunk), [rows,...  110 us
    pallas_call x1, Pallas kernels, forward(): call(functools.partial(forward_kernel, count, main, spare), [rows_low, ro...  70 us
  transfers between devices with their start and end apart: 1, of which 0 were waited for; matrix products, arithmetic and copies ran while one was open for 2% of the time, Pallas kernels for 53%

profile of v5, /device:TPU:0, one launch (start us, length us, event | category | flops | bytes accessed | tf_op | source)
XLA Modules:
  0.0 482.7 jit_solution(18428532176182338005)
XLA Ops:
  7.2 0.0 all-reduce.3.cloned.1.call-start
  7.9 8.2 %tables.1 = (bf16[1792,768]{1,0:T(8,128)(2,1)}, s32[1024,128]{1,0:T(8,128)}, s32[8,1024]{1,0:T(8,128)}) custom-call(s32[1,8]{1,0:T(1,128)} %counts_ref.3, s32[1]{0:T(128)S(6)} %copy.33.group_ref, s32[8]{0:T(128)} %domain_ref.3, s32[1,1024]{1,0:T(1,128)} %sort_ref.1, bf16[1024,768]{1,0:T(8,128)(2,1)} %cot_ref.3), custom_call_target="tpu_custom_call" | custom-call | flops 1000000000 | bytes 10000000 | tf_op jit(solution)/shard_map/tables/pallas_call | solution.py:862
  16.1 70.0 %dense_forward.1 = (bf16[1024,768]{1,0:T(8,128)(2,1)}, bf16[1024,768]{1,0:T(8,128)(2,1)}, bf16[1024,768]{1,0:T(8,128)(2,1)}, bf16[1024,768]{1,0:T(8,128)(2,1)}, ...) custom-call(bf16[1024,768]{1,0:T(8,128)(2,1)} %x_ref.3, ...), custom_call_target="tpu_custom_call" | custom-call | flops 1000000000 | bytes 10000000 | tf_op jit(solution)/shard_map/dense_forward/pallas_call | solution.py:874
  86.1 110.1 %expert.1 = (bf16[2048,768]{1,0:T(8,128)(2,1)}, bf16[1536,768]{1,0:T(8,128)(2,1)}, bf16[896,768]{1,0:T(8,128)(2,1)}, bf16[768,3072]{1,0:T(8,128)(2,1)}, bf16[3072,768]{1,0:T(8,128)(2,1)}) custom-call(s32[1,8]{1,0:T(1,128)} %counts_ref.3, bf16[1792,768]{1,0:T(8,128)(2,1)} %get-tuple-element.47.send_ref, bf16[2048,768]{1,0:T(8,128)(2,1)} %get-tuple-element.48.cot_rows_ref, ...), custom_call_target="tpu_custom_call" | custom-call | flops 1000000000 | bytes 10000000 | tf_op jit(solution)/shard_map/expert/pallas_call | solution.py:903
  196.2 0.0 all-reduce.3.cloned.1.call-update
  196.3 142.5 %dense_backward.1 = (bf16[1024,768]{1,0:T(8,128)(2,1)}, bf16[3072,768]{1,0:T(8,128)(2,1)}, f32[8,768]{1,0:T(8,128)}, bf16[1792,768]{1,0:T(8,128)(2,1)}) custom-call(s32[1]{0:T(128)S(6)} %copy.33.group_ref, s32[8]{0:T(128)} %domain_ref.3, bf16[1024,768]{1,0:T(8,128)(2,1)} %x_ref.3, bf16[1024,768]{1,0:T(8,128)(2,1)} %cot_ref.3, f32[768]{0:T(1024)} %gain_one_ref.3, ...), custom_call_target="tpu_custom_call" | custom-call | flops 49999998976 | bytes 10000000 | tf_op jit(solution)/shard_map/dense_backward/pallas_call | solution.py:944
  338.8 113.8 %finish.1 = (bf16[1024,768]{1,0:T(8,128)(2,1)}, bf16[3072,768]{1,0:T(8,128)(2,1)}, f32[8,768]{1,0:T(8,128)}) custom-call(bf16[3072,768]{1,0:T(8,128)(2,1)} %get-tuple-element.52.dense_ref, f32[8,768]{1,0:T(8,128)} %get-tuple-element.53.vec_ref, s32[1024,128]{1,0:T(8,128)} %get-tuple-element.37.slot_col_ref, f32[1024,768]{1,0:T(8,128)} %get-tuple-element.46.hidden_ref, ...), custom_call_target="tpu_custom_call" | custom-call | flops 1000000000 | bytes 10000000 | tf_op jit(solution)/shard_map/finish/pallas_call | solution.py:982
  452.6 1.5 slice_reduce_fusion
  454.1 6.2 %fusion = (f32[768,768]{1,0:T(8,128)}, f32[768,768]{1,0:T(8,128)}, f32[768,768]{1,0:T(8,128)}, f32[768,768]{1,0:T(8,128)}) fusion(bf16[3072,768]{1,0:T(8,128)(2,1)} %get-tuple-element.59), kind=kLoop, calls=%fused_computation.4 | loop fusion | bytes 18874368 | tf_op jit(solution)/shard_map/slice | solution.py:1048
  460.3 0.0 all-reduce.3.cloned.1.call-done
  460.3 0.0 copy-start
  460.3 7.5 %broadcast_in_dim.13 = f32[1,768,3072]{2,1,0:T(8,128)} convert(bf16[1,768,3072]{2,1,0:T(8,128)(2,1)} %get-tuple-element.66) | non-fusion elementwise | flops 2359296 | bytes 14155776 | tf_op jit(solution)/shard_map/broadcast_in_dim | solution.py:1055
  467.8 0.0 copy-done
  467.8 0.0 copy-start.2
  467.8 4.5 broadcast_in_dim.15
  472.3 0.0 copy-start.1
  472.3 0.0 copy-done.2
  472.3 1.1 copy.34
  473.5 0.8 copy-done.1
  474.3 1.1 copy.35
Async XLA Ops:
  7.2 453.1 %all-reduce.3.cloned.1.call-start = ((), (), s32[]{:S(2)}) async-start(), calls=%async_computation | async-start | bytes 18874368 | tf_op jit(solution)/shard_map/psum | solution.py:1041
  460.3 7.5 %copy-start = (bf16[1,3072,768]{2,1,0:T(8,128)(2,1)S(1)}, bf16[1,3072,768]{2,1,0:T(8,128)(2,1)}, u32[]{:S(2)}) copy-start(bf16[1,3072,768]{2,1,0:T(8,128)(2,1)} %get-tuple-element.67) | copy-start | bytes 14155780
  467.8 4.5 copy-start.2
  472.3 2.0 copy-start.1
Sparse Core Ops, SparseCore 0:
  196.4 204.1 all-reduce.2

commit v6 on v5

--- a/solution.py
+++ b/solution.py
@@ -214,13 +214,12 @@
     me = lax.axis_index("expert")
     greet("expert", me, count)
     base = count * main
-    depth = depth_of(count)
 
     def gather(step):
         return gather_spare(me, count, base, spare, step, cot_send_ref, cot_rows_ref, spare_sends, spare_recvs)
 
     gather(0).start()
-    copies = [send_block(me, count, main, mask, cot_send_ref, cot_rows_ref, sends, recvs) for mask in range(1, count)]
+    copies = [send_block(me, count, main, mask, cot_send_ref, cot_rows_ref, sends, recvs) for mask in range(1, count - 1)]
     for copy in copies:
         copy.start()
     mine = [
@@ -243,10 +242,6 @@
         return carry
 
     lax.fori_loop(0, blocks, project, 0)
-    for copy in mine:
-        copy.wait()
-    gather(0).wait()
-    gather(1).start()
 
     keep = iota((BLK, BLK), 0) <= iota((BLK, BLK), 1)
 
@@ -273,11 +268,6 @@
         return carry
 
     lax.fori_loop(0, HEADS // 2, attend, 0)
-    for step in range(1, depth):
-        gather(step).wait()
-        if step + 1 < depth:
-            gather(step + 1).start()
-
     experts = router_ref.shape[0]
 
     def finish(block, carry):
@@ -295,7 +285,9 @@
 
     lax.fori_loop(0, blocks, finish, 0)
     pack_rows(slot_row_ref[0:1, :], routed, send_ref)
-    for copy in copies:
+    for copy in mine:
+        copy.wait()
+    for copy in copies + [gather(0)]:
         copy.wait()
 
 
@@ -315,6 +307,7 @@
     chunk,
     counts_ref,
     send_ref,
+    cot_send_ref,
     cot_rows_ref,
     router_ref,
     w1_hbm,
@@ -338,6 +331,8 @@
     recvs,
     spare_sends,
     spare_recvs,
+    cot_sends,
+    cot_recvs,
     back_sends,
     back_recvs,
     own,
@@ -355,7 +350,8 @@
     loads = [
         pltpu.make_async_copy(w1_hbm, w1_ref, load_sems.at[0]),
         pltpu.make_async_copy(w2_hbm, w2_ref, load_sems.at[1]),
-        pltpu.make_async_copy(cot_rows_ref, g_ref, load_sems.at[2]),
+        pltpu.make_async_copy(cot_rows_ref.at[pl.ds(0, base - main)], g_ref.at[pl.ds(0, base - main)], load_sems.at[2]),
+        pltpu.make_async_copy(cot_rows_ref.at[pl.ds(base, 2 * spare)], g_ref.at[pl.ds(base, 2 * spare)], load_sems.at[3]),
     ]
     for load in loads:
         load.start()
@@ -370,9 +366,32 @@
     def leave(mask):
         return return_block(me, count, main, mask, dx_rows, back_ref, back_sends, back_recvs)
 
+    def gather_cot(step):
+        source = cot_rows_ref if step == 1 else g_ref
+        have = spare << step
+        return copy_to(
+            source.at[pl.ds(base, have)],
+            g_ref.at[pl.ds(base + have, have)],
+            cot_sends.at[step],
+            cot_recvs.at[step],
+            {"expert": flip(me, count >> (step + 1), count)},
+        )
+
+    def last_cot():
+        rows = span(flip(me, count - 1, count) * main, main)
+        return copy_to(
+            cot_send_ref.at[rows],
+            g_ref.at[pl.ds(base - main, main)],
+            cot_sends.at[0],
+            cot_recvs.at[0],
+            {"expert": flip(me, count - 1, count)},
+        )
+
+    gather_cot(1).start()
     gather(0).start()
     for mask in range(1, count):
         arrive(mask).start()
+    last_cot().start()
     mine_in = [
         pltpu.make_async_copy(send_ref.at[span(me * main, main)], x_rows.at[pl.ds(0, main)], own.at[0]),
         pltpu.make_async_copy(send_ref.at[pl.ds(base, spare)], x_rows.at[pl.ds(base, spare)], own.at[1]),
@@ -404,13 +423,21 @@
             def _():
                 arrive(mask).wait_recv()
 
+            @pl.when((block == plain - 1) & (mask == count - 1))
+            def _():
+                last_cot().wait_recv()
+
         for step in range(depth):
 
-            @pl.when(turn == (step + 1 if step + 1 < depth else plain - 1))
+            @pl.when(turn == (max(step + 1, plain - depth + step) if step else 1))
             def _():
                 gather(step).wait_recv()
+                if step:
+                    gather_cot(step).wait_recv()
                 if step + 1 < depth:
                     gather(step + 1).start()
+                    if step:
+                        gather_cot(step + 1).start()
 
         rows = pl.ds(pl.multiple_of(block * BLK, BLK), BLK)
         live = jnp.where(block < plain, 1.0, hot)
@@ -484,6 +511,9 @@
     lax.fori_loop(0, blocks, settle, 0)
     for step in range(depth):
         gather(step).wait_send()
+    for step in range(1, depth):
+        gather_cot(step).wait_send()
+    last_cot().wait_send()
     for mask in range(1, count):
         arrive(mask).wait_send()
     for mask in range(1, early):
@@ -496,10 +526,31 @@
     spare,
     group_ref,
     domain_ref,
+    x_hbm,
+    cot_hbm,
+    gain_one_ref,
+    gain_two_ref,
+    wq_hbm,
+    wk_hbm,
+    wv_hbm,
+    wo_hbm,
+    slot_col_hbm,
+    normed_hbm,
+    q_hbm,
+    k_hbm,
+    v_hbm,
+    mixed_hbm,
+    lse_hbm,
+    hidden_hbm,
+    dx_hbm,
+    late_ref,
+    y_ref,
+    grad_ref,
+    dense_ref,
+    vec_ref,
+    y_back_ref,
     x_ref,
     cot_ref,
-    gain_one_ref,
-    gain_two_ref,
     wq_ref,
     wk_ref,
     wv_ref,
@@ -512,13 +563,6 @@
     mixed_ref,
     lse_ref,
     hidden_ref,
-    dx_hbm,
-    late_ref,
-    y_ref,
-    grad_ref,
-    dense_ref,
-    vec_ref,
-    y_back_ref,
     dx_ref,
     spare_dx,
     spare_y,
@@ -540,6 +584,7 @@
     y_recvs,
     own,
     gets,
+    fills,
 ):
     tokens, width = x_ref.shape
     me = lax.axis_index("expert")
@@ -548,6 +593,25 @@
     late = (count - early) * main
     total = count * spare
     depth = depth_of(count)
+    operands = [
+        (x_hbm, x_ref),
+        (cot_hbm, cot_ref),
+        (wq_hbm, wq_ref),
+        (wk_hbm, wk_ref),
+        (wv_hbm, wv_ref),
+        (wo_hbm, wo_ref),
+        (slot_col_hbm, slot_col_ref),
+        (normed_hbm, normed_ref),
+        (q_hbm, q_ref),
+        (k_hbm, k_ref),
+        (v_hbm, v_ref),
+        (mixed_hbm, mixed_ref),
+        (lse_hbm, lse_ref),
+        (hidden_hbm, hidden_ref),
+    ]
+    operands = [pltpu.make_async_copy(source, target, fills.at[i]) for i, (source, target) in enumerate(operands)]
+    for copy in operands:
+        copy.start()
     greet("expert", me, count)
 
     def sum_dx(step):
@@ -570,8 +634,6 @@
     for copy in lates:
         copy.start()
     copies = [return_block(me, count, main, mask, y_ref, y_back_ref, sends, recvs) for mask in range(1, count)]
-    for copy in copies:
-        copy.start()
     mine = pltpu.make_async_copy(y_ref.at[pl.ds(0, main)], y_back_ref.at[span(me * main, main)], own.at[0])
     mine.start()
     loads = [
@@ -590,8 +652,12 @@
         if step:
             sum_dx(step - 1).start()
     dx_ref[pl.ds(base, BLK), :] = spare_dx[0:BLK, :]
+    for copy in lates:
+        copy.wait()
     sum_y(depth - 1).start()
-    for copy in lates:
+    for copy in copies:
+        copy.start()
+    for copy in operands:
         copy.wait()
     slots = dx_ref.shape[0]
     blocks = tokens // BLK
@@ -670,12 +736,6 @@
         return carry
 
     lax.fori_loop(0, HEADS // 2, attend, 0)
-    for step in reversed(range(depth - 1)):
-        settle(sum_y(step), spare_y, y_land, step)
-        if step:
-            sum_y(step - 1).start()
-    spare_out = pltpu.make_async_copy(spare_y.at[pl.ds(0, BLK)], y_back_ref.at[pl.ds(base, BLK)], own.at[1])
-    spare_out.start()
 
     for part in range(3):
         dense_ref[pl.ds(part * width, width), :] = nn(normed_t[...], dqkv[:, pl.ds(part * width, width)]).astype(BF16)
@@ -695,6 +755,12 @@
 
     lax.fori_loop(0, blocks, close_block, 0)
     vec_ref[...] = sums[...]
+    for step in reversed(range(depth - 1)):
+        settle(sum_y(step), spare_y, y_land, step)
+        if step:
+            sum_y(step - 1).start()
+    spare_out = pltpu.make_async_copy(spare_y.at[pl.ds(0, BLK)], y_back_ref.at[pl.ds(base, BLK)], own.at[1])
+    spare_out.start()
     spare_out.wait()
     mine.wait()
     for copy in copies:
@@ -893,7 +959,7 @@
     )(inputs, g1, s1, g2, s2, wq, wk, wv, wo, router, slot_col, slot_row, cot_send)
 
 
-def expert_block(count, main, spare, counts, send, cot_rows, router_t, w1, w2, chunk=768):
+def expert_block(count, main, spare, counts, send, cot_send, cot_rows, router_t, w1, w2, chunk=768):
     slots, width = cot_rows.shape
     hidden = w1.shape[1]
     late = slots - (count - count // 4) * main
@@ -909,7 +975,7 @@
             shape((width, hidden), BF16),
             shape((hidden, width), BF16),
         ],
-        [SMEM, ANY, ANY, VMEM, ANY, ANY],
+        [SMEM, ANY, ANY, ANY, VMEM, ANY, ANY],
         [
             pltpu.VMEM((width, hidden), BF16),
             pltpu.VMEM((hidden, width), BF16),
@@ -920,9 +986,11 @@
             keep,
             keep,
             pltpu.VMEM((2, width, width), BF16),
-            dma(3),
+            dma(4),
             dma(count),
             dma(count),
+            dma(depth),
+            dma(depth),
             dma(depth),
             dma(depth),
             dma(count),
@@ -934,7 +1002,7 @@
         "expert",
         [ANY] * 5,
         2,
-    )(counts, send, cot_rows, router_t, w1, w2)
+    )(counts, send, cot_send, cot_rows, router_t, w1, w2)
 
 
 def backward(
@@ -944,8 +1012,9 @@
     return call(
         functools.partial(backward_kernel, count, main, spare),
         [shape((tokens, width), BF16), shape((4 * width, width), BF16), shape((8, width), F32), shape((count * main + BLK, width), BF16)],
-        [SMEM] * 2 + [VMEM] * 16 + [ANY] * 3,
-        [
+        [SMEM] * 2 + [ANY] * 2 + [VMEM] * 2 + [ANY] * 15,
+        [pltpu.VMEM(v.shape, v.dtype) for v in (inputs, cotangent, wq, wk, wv, wo, slot_col, normed, q, k, v, mixed, lse, hidden)]
+        + [
             pltpu.VMEM((count * main + BLK, width), BF16),
             pltpu.VMEM((count * spare, width), BF16),
             pltpu.VMEM((count * spare, width), BF16),
@@ -967,6 +1036,7 @@
             dma(depth_of(count)),
             dma(3),
             dma(count),
+            dma(14),
         ],
         "dense_backward",
         [VMEM, VMEM, VMEM, ANY],
@@ -1036,7 +1106,7 @@
         count, main, spare, inputs, g1, s1, g2, s2, w_query, w_key, w_value, w_out, router_t, slot_col, slot_row, cot_send
     )
     y_rows, dx_back, dx_late, grad_first, grad_second = expert_block(
-        count, main, spare, send_counts, send, cot_rows, router_t, expert_in[0], expert_out[0]
+        count, main, spare, send_counts, send, cot_send, cot_rows, router_t, expert_in[0], expert_out[0]
     )
     expert_sums = (lax.psum(grad_first, "dp").astype(F32), lax.psum(grad_second, "dp").astype(F32))
     grad_inputs, dense, vec, y_back = backward(

time: 490 us -> 437 us (0.89)
  Pallas kernels: 445 us -> 392 us
    pallas_call x1, Pallas kernels: 142 us -> 94.4 us  [backward(): call(functools.partial(backward_kernel, count, main, spare), [shape((toke...]
    pallas_call x1, Pallas kernels: 70 us -> 51.1 us  [forward(): call(functools.partial(forward_kernel, count, main, spare), [rows_low, ro...]
    pallas_call x1, Pallas kernels: 114 us -> 130 us  [finish(): call(functools.partial(finish_kernel, dp, count), [shape(hidden.shape, BF...]
  transfers between devices with their start and end apart: 1 -> 1, of which waited for: 0 -> 0; matrix products, arithmetic and copies ran while one was open for 2% -> 2% of each run, Pallas kernels for 53% -> 52%
where the time goes in v6:
time: 437 us; the launch traced here: 430 us
  Pallas kernels  392 us (90%)
  between operations  15.2 us (3%)
  other arithmetic  12 us (3%)
  local copies, waits for them, and re-layouts  10.8 us (2%)
    pallas_call x1, Pallas kernels, finish(): call(functools.partial(finish_kernel, dp, count), [shape(hidden.shape, BF...  130 us
    pallas_call x1, Pallas kernels, expert_block(): call(functools.partial(expert_kernel, count, main, spare, chunk), [rows,...  109 us
    pallas_call x1, Pallas kernels, backward(): call(functools.partial(backward_kernel, count, main, spare), [shape((toke...  94.4 us
    pallas_call x1, Pallas kernels, forward(): call(functools.partial(forward_kernel, count, main, spare), [rows_low, ro...  51.1 us
  transfers between devices with their start and end apart: 1, of which 0 were waited for; matrix products, arithmetic and copies ran while one was open for 2% of the time, Pallas kernels for 52%

profile of v6, /device:TPU:0, one launch (start us, length us, event | category | flops | bytes accessed | tf_op | source)
XLA Modules:
  0.0 430.3 jit_solution(4705998363706546981)
XLA Ops:
  7.2 0.0 all-reduce.3.cloned.1.call-start
  7.9 8.2 %tables.1 = (bf16[1792,768]{1,0:T(8,128)(2,1)}, s32[1024,128]{1,0:T(8,128)}, s32[8,1024]{1,0:T(8,128)}) custom-call(s32[1,8]{1,0:T(1,128)} %counts_ref.3, s32[1]{0:T(128)S(6)} %copy.33.group_ref, s32[8]{0:T(128)} %domain_ref.3, s32[1,1024]{1,0:T(1,128)} %sort_ref.1, bf16[1024,768]{1,0:T(8,128)(2,1)} %cot_hbm.1), custom_call_target="tpu_custom_call" | custom-call | flops 1000000000 | bytes 10000000 | tf_op jit(solution)/shard_map/tables/pallas_call | solution.py:928
  16.1 51.1 %dense_forward.1 = (bf16[1024,768]{1,0:T(8,128)(2,1)}, bf16[1024,768]{1,0:T(8,128)(2,1)}, bf16[1024,768]{1,0:T(8,128)(2,1)}, bf16[1024,768]{1,0:T(8,128)(2,1)}, ...) custom-call(bf16[1024,768]{1,0:T(8,128)(2,1)} %x_hbm.1, ...), custom_call_target="tpu_custom_call" | custom-call | flops 1000000000 | bytes 10000000 | tf_op jit(solution)/shard_map/dense_forward/pallas_call | solution.py:940
  67.3 108.6 %expert.1 = (bf16[2048,768]{1,0:T(8,128)(2,1)}, bf16[1536,768]{1,0:T(8,128)(2,1)}, bf16[896,768]{1,0:T(8,128)(2,1)}, bf16[768,3072]{1,0:T(8,128)(2,1)}, bf16[3072,768]{1,0:T(8,128)(2,1)}) custom-call(s32[1,8]{1,0:T(1,128)} %counts_ref.3, bf16[1792,768]{1,0:T(8,128)(2,1)} %get-tuple-element.47.send_ref, bf16[1792,768]{1,0:T(8,128)(2,1)} %get-tuple-element.39.cot_send_ref, ...), custom_call_target="tpu_custom_call" | custom-call | flops 1000000000 | bytes 10000000 | tf_op jit(solution)/shard_map/expert/pallas_call | solution.py:969
  175.8 0.0 all-reduce.3.cloned.1.call-update
  175.9 94.4 %dense_backward.1 = (bf16[1024,768]{1,0:T(8,128)(2,1)}, bf16[3072,768]{1,0:T(8,128)(2,1)}, f32[8,768]{1,0:T(8,128)}, bf16[1792,768]{1,0:T(8,128)(2,1)}) custom-call(s32[1]{0:T(128)S(6)} %copy.33.group_ref, s32[8]{0:T(128)} %domain_ref.3, bf16[1024,768]{1,0:T(8,128)(2,1)} %x_hbm.1, bf16[1024,768]{1,0:T(8,128)(2,1)} %cot_hbm.1, f32[768]{0:T(1024)} %gain_one_ref.3, ...), custom_call_target="tpu_custom_call" | custom-call | flops 49999998976 | bytes 10000000 | tf_op jit(solution)/shard_map/dense_backward/pallas_call | solution.py:1012
  270.3 129.9 %finish.1 = (bf16[1024,768]{1,0:T(8,128)(2,1)}, bf16[3072,768]{1,0:T(8,128)(2,1)}, f32[8,768]{1,0:T(8,128)}) custom-call(bf16[3072,768]{1,0:T(8,128)(2,1)} %get-tuple-element.52.dense_ref, f32[8,768]{1,0:T(8,128)} %get-tuple-element.53.vec_ref, s32[1024,128]{1,0:T(8,128)} %get-tuple-element.37.slot_col_ref.slot_col_hbm, ...), custom_call_target="tpu_custom_call" | custom-call | flops 1000000000 | bytes 10000000 | tf_op jit(solution)/shard_map/finish/pallas_call | solution.py:1052
  400.2 1.5 slice_reduce_fusion
  401.7 6.2 %fusion = (f32[768,768]{1,0:T(8,128)}, f32[768,768]{1,0:T(8,128)}, f32[768,768]{1,0:T(8,128)}, f32[768,768]{1,0:T(8,128)}) fusion(bf16[3072,768]{1,0:T(8,128)(2,1)} %get-tuple-element.59), kind=kLoop, calls=%fused_computation.4 | loop fusion | bytes 18874368 | tf_op jit(solution)/shard_map/slice | solution.py:1118
  407.9 0.0 all-reduce.3.cloned.1.call-done
  407.9 0.0 copy-start
  407.9 7.5 %broadcast_in_dim.13 = f32[1,768,3072]{2,1,0:T(8,128)} convert(bf16[1,768,3072]{2,1,0:T(8,128)(2,1)} %get-tuple-element.66) | non-fusion elementwise | flops 2359296 | bytes 14155776 | tf_op jit(solution)/shard_map/broadcast_in_dim | solution.py:1125
  415.4 0.0 copy-done
  415.4 0.0 copy-start.2
  415.4 4.5 %broadcast_in_dim.15 = f32[1,3072,768]{2,1,0:T(8,128)} convert(bf16[1,3072,768]{2,1,0:T(8,128)(2,1)S(1)} %copy-done) | non-fusion elementwise | flops 2359296 | bytes 14155776 | tf_op jit(solution)/shard_map/broadcast_in_dim | solution.py:1126
  419.9 0.0 copy-start.1
  419.9 0.0 copy-done.2
  419.9 1.1 copy.34
  421.1 0.8 copy-done.1
  421.9 1.1 copy.35
Async XLA Ops:
  7.2 400.7 %all-reduce.3.cloned.1.call-start = ((), (), s32[]{:S(2)}) async-start(), calls=%async_computation | async-start | bytes 18874368 | tf_op jit(solution)/shard_map/psum | solution.py:1111
  407.9 7.5 %copy-start = (bf16[1,3072,768]{2,1,0:T(8,128)(2,1)S(1)}, bf16[1,3072,768]{2,1,0:T(8,128)(2,1)}, u32[]{:S(2)}) copy-start(bf16[1,3072,768]{2,1,0:T(8,128)(2,1)} %get-tuple-element.67) | copy-start | bytes 14155780
  415.4 4.5 %copy-start.2 = (bf16[1024,768]{1,0:T(8,128)(2,1)S(1)}, bf16[1024,768]{1,0:T(8,128)(2,1)}, u32[]{:S(2)}) copy-start(bf16[1024,768]{1,0:T(8,128)(2,1)} %get-tuple-element.84) | copy-start | bytes 4718596
  419.9 2.0 copy-start.1
Sparse Core Ops, SparseCore 0:
  176.0 219.5 all-reduce.2

commit v7 on v6

--- a/solution.py
+++ b/solution.py
@@ -83,6 +83,20 @@
         recvs.at[mask],
         {"expert": flip(me, mask, count)},
     )
+
+
+def dp_sides():
+    index = lax.axis_index("dp")
+    return index, (index % 2, (index // 2) % 2)
+
+
+def sum_rows(target, other, rows):
+    def step(block, carry):
+        part = pl.ds(pl.multiple_of(block * BLK, BLK), BLK)
+        target[part, :] = (target[part, :].astype(F32) + other[part, :].astype(F32)).astype(BF16)
+        return carry
+
+    lax.fori_loop(0, rows // BLK, step, 0)
 
 
 def depth_of(count):
@@ -315,8 +329,7 @@
     y_ref,
     back_ref,
     late_ref,
-    gw1_ref,
-    gw2_ref,
+    grads_ref,
     w1_ref,
     w2_ref,
     acc1,
@@ -486,10 +499,10 @@
     tail.start()
 
     pieces = []
-    for first in range(0, hidden, stage.shape[1]):
-        pieces.append((acc1.at[:, pl.ds(first, stage.shape[1])], gw1_ref.at[:, pl.ds(first, stage.shape[1])]))
-    for first in range(0, hidden, stage.shape[1]):
-        pieces.append((acc2.at[pl.ds(first, stage.shape[1]), :], gw2_ref.at[pl.ds(first, stage.shape[1]), :]))
+    for first in range(0, hidden, width):
+        pieces.append((acc1.at[:, pl.ds(first, width)], grads_ref.at[pl.ds(first, width)]))
+    for first in range(0, hidden, width):
+        pieces.append((acc2.at[pl.ds(first, width), :], grads_ref.at[pl.ds(hidden + first, width)]))
     writes = []
     for index, (piece, target) in enumerate(pieces):
         slot = index % 2
@@ -521,6 +534,7 @@
 
 
 def backward_kernel(
+    dp,
     count,
     main,
     spare,
@@ -545,10 +559,12 @@
     dx_hbm,
     late_ref,
     y_ref,
+    grads_hbm,
     grad_ref,
     dense_ref,
     vec_ref,
     y_back_ref,
+    piece_ref,
     x_ref,
     cot_ref,
     wq_ref,
@@ -568,6 +584,9 @@
     spare_y,
     dx_land,
     y_land,
+    kept,
+    land_one,
+    land_two,
     ghid,
     gmix,
     branch,
@@ -585,6 +604,9 @@
     own,
     gets,
     fills,
+    scatter_sends,
+    scatter_recvs,
+    keeps,
 ):
     tokens, width = x_ref.shape
     me = lax.axis_index("expert")
@@ -612,7 +634,47 @@
     operands = [pltpu.make_async_copy(source, target, fills.at[i]) for i, (source, target) in enumerate(operands)]
     for copy in operands:
         copy.start()
-    greet("expert", me, count)
+    barrier = pltpu.get_barrier_semaphore()
+    place, bits = dp_sides()
+    for mask in range(1, count):
+        pl.semaphore_signal(barrier, inc=1, device_id={"expert": flip(me, mask, count)}, device_id_type=MESH)
+    for mask in (1, 2):
+        pl.semaphore_signal(barrier, inc=1, device_id={"dp": flip(place, mask, dp)}, device_id_type=MESH)
+    pl.semaphore_wait(barrier, count + 1)
+    portion = grads_hbm.shape[0] // 4
+    quarter = portion // 2
+
+    def scatter_one(stream):
+        start = 2 * portion * stream + (1 - bits[stream]) * portion
+        device = {"dp": flip(place, 1 << stream, dp)}
+        return copy_to(
+            grads_hbm.at[span(start, portion)], land_one.at[stream], scatter_sends.at[0, stream], scatter_recvs.at[0, stream], device
+        )
+
+    def keep_one(stream):
+        start = 2 * portion * stream + bits[stream] * portion
+        return pltpu.make_async_copy(grads_hbm.at[span(start, portion)], kept.at[stream], keeps.at[stream])
+
+    def scatter_two(stream):
+        start = (1 - bits[1 - stream]) * quarter
+        device = {"dp": flip(place, 2 >> stream, dp)}
+        return copy_to(
+            kept.at[stream, span(start, quarter)],
+            land_two.at[stream],
+            scatter_sends.at[1, stream],
+            scatter_recvs.at[1, stream],
+            device,
+        )
+
+    def store_piece(stream):
+        start = bits[1 - stream] * quarter
+        return pltpu.make_async_copy(
+            kept.at[stream, span(start, quarter)], piece_ref.at[pl.ds(stream * quarter, quarter)], keeps.at[stream]
+        )
+
+    for stream in range(2):
+        scatter_one(stream).start()
+        keep_one(stream).start()
 
     def sum_dx(step):
         if step == depth - 1:
@@ -624,10 +686,10 @@
             return return_spare(me, count, spare, step, y_ref, base, y_land, y_sends, y_recvs)
         return return_spare(me, count, spare, step, spare_y, 0, y_land, y_sends, y_recvs)
 
-    def settle(copy, kept, landing, step):
+    def settle(copy, own_rows, landing, step):
         copy.wait()
-        half = spare << step
-        kept[0:half, :] = (kept[0:half, :].astype(F32) + landing[half : 2 * half, :].astype(F32)).astype(BF16)
+        rows = spare << step
+        own_rows[0:rows, :] = (own_rows[0:rows, :].astype(F32) + landing[rows : 2 * rows, :].astype(F32)).astype(BF16)
 
     sum_dx(depth - 1).start()
     lates = [return_block(me, count, main, mask, late_ref, dx_ref, late_sends, late_recvs, early) for mask in range(early, count)]
@@ -693,6 +755,14 @@
     keep = iota((BLK, BLK), 0) <= iota((BLK, BLK), 1)
 
     def attend(pair, carry):
+        @pl.when(pair == HEADS // 4)
+        def _():
+            for stream in range(2):
+                keep_one(stream).wait()
+                scatter_one(stream).wait()
+                sum_rows(kept.at[stream], land_one.at[stream], portion)
+                scatter_two(stream).start()
+
         base = pl.multiple_of(pair * 128, 128)
         cols = pl.ds(base, 128)
         q_pair = q_ref[:, cols]
@@ -755,6 +825,11 @@
 
     lax.fori_loop(0, blocks, close_block, 0)
     vec_ref[...] = sums[...]
+    for stream in range(2):
+        scatter_two(stream).wait()
+        start = bits[1 - stream] * quarter
+        sum_rows(kept.at[stream, span(start, quarter)], land_two.at[stream], quarter)
+        store_piece(stream).start()
     for step in reversed(range(depth - 1)):
         settle(sum_y(step), spare_y, y_land, step)
         if step:
@@ -762,16 +837,22 @@
     spare_out = pltpu.make_async_copy(spare_y.at[pl.ds(0, BLK)], y_back_ref.at[pl.ds(base, BLK)], own.at[1])
     spare_out.start()
     spare_out.wait()
+    for stream in range(2):
+        store_piece(stream).wait()
     mine.wait()
     for copy in copies:
         copy.wait()
+
+
+STREAMS = 3
+CHUNKS = 4
 
 
 def halving_plan(dp, count, rows):
     experts = [("expert", 2 << bit) for bit in range(depth_of(count) - 1)]
     groups = [("dp", 1 << bit) for bit in range(depth_of(dp))]
     core = [("expert", 1)]
-    plans = [core + groups + experts, core + experts + groups]
+    plans = [core + groups + experts, core + groups[::-1] + experts, core + experts + groups]
     halvings = 0
     while halvings < len(plans[0]) and (rows >> halvings) % 32 == 0:
         halvings += 1
@@ -787,9 +868,11 @@
     hidden_ref,
     gate_ref,
     y_ref,
+    piece_ref,
     out_ref,
     full_ref,
     total_ref,
+    grads_ref,
     acc,
     landing,
     full,
@@ -802,10 +885,13 @@
     vec_sends,
     vec_recvs,
     put,
+    unit_sends,
+    unit_recvs,
+    own,
 ):
     tokens, width = hidden_ref.shape
     slots = y_ref.shape[0]
-    rows = dense_ref.shape[0] // 2
+    rows = dense_ref.shape[0] // STREAMS
     place = {"dp": lax.axis_index("dp"), "expert": lax.axis_index("expert")}
     size = {"dp": dp, "expert": count}
     plans, halvings = halving_plan(dp, count, rows)
@@ -821,6 +907,47 @@
 
     def side(axis, mask):
         return (place[axis] // mask) % 2
+
+    _, bits = dp_sides()
+    quarter = piece_ref.shape[0] // 2
+    chunk = quarter // CHUNKS
+    starts = [
+        4 * quarter * stream + bits[stream] * 2 * quarter + bits[1 - stream] * quarter for stream in range(2)
+    ]
+    others = [
+        4 * quarter * stream + bits[stream] * 2 * quarter + (1 - bits[1 - stream]) * quarter for stream in range(2)
+    ]
+
+    def unit(index, stream):
+        kind, part = index // CHUNKS, index % CHUNKS
+        near, far = partner("dp", 1 << stream), partner("dp", 2 >> stream)
+        if kind == 2:
+            source = target = grads_ref.at[span(others[stream] + part * chunk, chunk)]
+        else:
+            source = piece_ref.at[pl.ds(stream * quarter + part * chunk, chunk)]
+            target = grads_ref.at[span(starts[stream] + part * chunk, chunk)]
+        return copy_to(
+            source, target, unit_sends.at[index, stream], unit_recvs.at[index, stream], far if kind == 0 else near
+        )
+
+    pending = list(range(3 * CHUNKS))
+
+    def advance(number):
+        for _ in range(min(number, len(pending))):
+            index = pending.pop(0)
+            for stream in range(2):
+                if index >= 2 * CHUNKS:
+                    unit(index - 2 * CHUNKS, stream).wait_recv()
+                unit(index, stream).start()
+
+    mine = [
+        pltpu.make_async_copy(
+            piece_ref.at[pl.ds(stream * quarter, quarter)], grads_ref.at[span(starts[stream], quarter)], own.at[stream]
+        )
+        for stream in range(2)
+    ]
+    for copy in mine:
+        copy.start()
 
     def combine(block):
         rows_at = pl.ds(block * BLK, BLK)
@@ -830,7 +957,7 @@
         out_ref[rows_at, :] = (hidden_ref[rows_at, :] + gate_ref[rows_at, 0:1] * returned).astype(BF16)
 
     todo = list(range(tokens // BLK))
-    low = [jnp.int32(stream * rows) for stream in range(2)]
+    low = [jnp.int32(stream * rows) for stream in range(STREAMS)]
     extent = rows
     offset = 0
     trail = []
@@ -838,9 +965,9 @@
         halve = step < halvings
         part = extent // 2 if halve else extent
         copies = []
-        for stream in range(2):
+        for stream in range(STREAMS):
             axis, mask = plans[stream][step]
-            mine = low[stream] + side(axis, mask) * part if halve else low[stream]
+            kept = low[stream] + side(axis, mask) * part if halve else low[stream]
             other = low[stream] + (1 - side(axis, mask)) * part if halve else low[stream]
             source = dense_ref if step == 0 else acc.at[(step - 1) % 2]
             land = landing.at[stream, pl.ds(offset, part)]
@@ -848,26 +975,27 @@
                 source.at[span(other, part)], land, sends.at[stream, step], recvs.at[stream, step], partner(axis, mask)
             )
             copy.start()
-            copies.append((copy, mine, source))
+            copies.append((copy, kept, source))
         axis, mask = plans[0][step]
         vec_source = vec_ref if step == 0 else vec_acc.at[step - 1]
         vec_copy = copy_to(vec_source, vec_land.at[step], vec_sends.at[step], vec_recvs.at[step], partner(axis, mask))
         vec_copy.start()
+        advance(1)
         if step in (1, 2):
             for block in todo[: tokens // BLK // 4]:
                 combine(block)
             todo = todo[tokens // BLK // 4 :]
         trail.append((list(low), extent))
-        for stream in range(2):
-            copy, mine, source = copies[stream]
+        for stream in range(STREAMS):
+            copy, kept, source = copies[stream]
             copy.wait()
-            held = span(mine, part)
-            kept = source[held, :].astype(F32) + landing[stream, pl.ds(offset, part), :].astype(F32)
+            held = span(kept, part)
+            value = source[held, :].astype(F32) + landing[stream, pl.ds(offset, part), :].astype(F32)
             if step < steps - 1:
-                acc[step % 2, held, :] = kept.astype(BF16)
+                acc[step % 2, held, :] = value.astype(BF16)
             else:
-                full[held, :] = kept.astype(BF16)
-            low[stream] = mine
+                full[held, :] = value.astype(BF16)
+            low[stream] = kept
         vec_copy.wait()
         vec_sum = vec_source[...] + vec_land[step]
         if step < steps - 1:
@@ -878,9 +1006,9 @@
         offset += part
 
     for step in reversed(range(halvings)):
-        starts, whole = trail[step]
+        origins, whole = trail[step]
         copies = []
-        for stream in range(2):
+        for stream in range(STREAMS):
             axis, mask = plans[stream][step]
             held = span(low[stream], extent)
             copy = copy_to(
@@ -888,17 +1016,53 @@
             )
             copy.start()
             copies.append(copy)
+        advance(2)
         if step in (1, 2):
             for block in todo if step == 1 else todo[: tokens // BLK // 4]:
                 combine(block)
             todo = todo[tokens // BLK // 4 :]
-        for stream in range(2):
+        for stream in range(STREAMS):
             copies[stream].wait()
-            low[stream] = starts[stream]
+            low[stream] = origins[stream]
         extent = whole
+    advance(len(pending))
     write = pltpu.make_async_copy(full, full_ref, put)
     write.start()
-    write.wait()
+    for index in range(3 * CHUNKS):
+        for stream in range(2):
+            if index >= CHUNKS:
+                unit(index, stream).wait_recv()
+            unit(index, stream).wait_send()
+    for copy in mine + [write]:
+        copy.wait()
+
+
+def widen_kernel(hidden, dense_hbm, grads_hbm, total_ref, *rest):
+    outs, vecs, (low, high, gets, puts) = rest[:6], rest[6:10], rest[10:]
+    width = dense_hbm.shape[1]
+    jobs = []
+    for block in range(hidden // width):
+        part = pl.ds(block * width, width)
+        jobs.append((grads_hbm.at[part], outs[4].at[:, part]))
+        jobs.append((grads_hbm.at[pl.ds(hidden + block * width, width)], outs[5].at[part, :]))
+    for index in range(4):
+        jobs.append((dense_hbm.at[pl.ds(index * width, width)], outs[index]))
+    loads = [pltpu.make_async_copy(source, low.at[i], gets.at[i]) for i, (source, _) in enumerate(jobs)]
+    for load in loads:
+        load.start()
+    for index, vec in enumerate(vecs):
+        vec[...] = total_ref[index : index + 1, :].reshape(width)
+    slots = high.shape[0]
+    stores = []
+    for index, (_, target) in enumerate(jobs):
+        loads[index].wait()
+        if index >= slots:
+            stores[index - slots].wait()
+        high[index % slots] = low[index].astype(F32)
+        stores.append(pltpu.make_async_copy(high.at[index % slots], target, puts.at[index % slots]))
+        stores[-1].start()
+    for store in stores[-slots:]:
+        store.wait()
 
 
 def call(kernel, outs, in_specs, scratch, name, out_specs=None, collective=None, flops=10**9):
@@ -972,8 +1136,7 @@
             rows,
             shape((count * main, width), BF16),
             shape((late, width), BF16),
-            shape((width, hidden), BF16),
-            shape((hidden, width), BF16),
+            shape((2 * hidden, width), BF16),
         ],
         [SMEM, ANY, ANY, ANY, VMEM, ANY, ANY],
         [
@@ -1000,19 +1163,21 @@
             dma(2),
         ],
         "expert",
-        [ANY] * 5,
+        [ANY] * 4,
         2,
     )(counts, send, cot_send, cot_rows, router_t, w1, w2)
 
 
 def backward(
-    count, main, spare, group, domains, inputs, cotangent, g1, g2, wq, wk, wv, wo, slot_col, normed, q, k, v, mixed, lse, hidden, dx, late, y
+    dp, count, main, spare, group, domains, inputs, cotangent, g1, g2, wq, wk, wv, wo, slot_col,
+    normed, q, k, v, mixed, lse, hidden, dx, late, y, grads,
 ):
     tokens, width = inputs.shape
+    half = grads.shape[0] // 4
     return call(
-        functools.partial(backward_kernel, count, main, spare),
-        [shape((tokens, width), BF16), shape((4 * width, width), BF16), shape((8, width), F32), shape((count * main + BLK, width), BF16)],
-        [SMEM] * 2 + [ANY] * 2 + [VMEM] * 2 + [ANY] * 15,
+        functools.partial(backward_kernel, dp, count, main, spare),
+        [shape((tokens, width), BF16), shape((4 * width, width), BF16), shape((8, width), F32), shape((count * main + BLK, width), BF16), shape((half, width), BF16)],
+        [SMEM] * 2 + [ANY] * 2 + [VMEM] * 2 + [ANY] * 16,
         [pltpu.VMEM(v.shape, v.dtype) for v in (inputs, cotangent, wq, wk, wv, wo, slot_col, normed, q, k, v, mixed, lse, hidden)]
         + [
             pltpu.VMEM((count * main + BLK, width), BF16),
@@ -1020,6 +1185,9 @@
             pltpu.VMEM((count * spare, width), BF16),
             pltpu.VMEM((count * spare, width), BF16),
             pltpu.VMEM((count * spare, width), BF16),
+            pltpu.VMEM((2, half, width), BF16),
+            pltpu.VMEM((2, half, width), BF16),
+            pltpu.VMEM((2, half // 2, width), BF16),
             pltpu.VMEM((tokens, width), F32),
             pltpu.VMEM((tokens, width), BF16),
             pltpu.VMEM((tokens, width), BF16),
@@ -1037,40 +1205,65 @@
             dma(3),
             dma(count),
             dma(14),
+            dma(2, 2),
+            dma(2, 2),
+            dma(2),
         ],
         "dense_backward",
-        [VMEM, VMEM, VMEM, ANY],
+        [VMEM, VMEM, VMEM, ANY, ANY],
         3,
         5 * 10**10,
-    )(group, domains, inputs, cotangent, g1, g2, wq, wk, wv, wo, slot_col, normed, q, k, v, mixed, lse, hidden, dx, late, y)
-
-
-def finish(dp, count, dense, vec, slot_col, hidden, gate, y_back):
+    )(group, domains, inputs, cotangent, g1, g2, wq, wk, wv, wo, slot_col, normed, q, k, v, mixed, lse, hidden, dx, late, y, grads)
+
+
+def finish(dp, count, dense, vec, slot_col, hidden, gate, y_back, piece):
     width = hidden.shape[1]
     rows = dense.shape[0]
-    steps = len(halving_plan(dp, count, rows // 2)[0][0])
+    steps = len(halving_plan(dp, count, rows // STREAMS)[0][0])
     return call(
         functools.partial(finish_kernel, dp, count),
-        [shape(hidden.shape, BF16), shape(dense.shape, BF16), shape(vec.shape, F32)],
-        [VMEM] * 6,
+        [shape(hidden.shape, BF16), shape(dense.shape, BF16), shape(vec.shape, F32), shape((4 * piece.shape[0], width), BF16)],
+        [VMEM] * 6 + [ANY],
         [
             pltpu.VMEM((2, rows, width), BF16),
-            pltpu.VMEM((2, rows, width), BF16),
+            pltpu.VMEM((STREAMS, rows // STREAMS + 64, width), BF16),
             pltpu.VMEM((rows, width), BF16),
             pltpu.VMEM((steps,) + vec.shape, F32),
             pltpu.VMEM((steps,) + vec.shape, F32),
-            dma(2, steps),
-            dma(2, steps),
-            dma(2, steps),
-            dma(2, steps),
+            dma(STREAMS, steps),
+            dma(STREAMS, steps),
+            dma(STREAMS, steps),
+            dma(STREAMS, steps),
             dma(steps),
             dma(steps),
             dma(),
+            dma(3 * CHUNKS, 2),
+            dma(3 * CHUNKS, 2),
+            dma(2),
         ],
         "finish",
-        [VMEM, ANY, VMEM],
+        [VMEM, ANY, VMEM, ANY],
         4,
-    )(dense, vec, slot_col, hidden, gate, y_back)
+    )(dense, vec, slot_col, hidden, gate, y_back, piece)
+
+
+def widen(hidden, dense, grads, total):
+    width = dense.shape[1]
+    square = shape((width, width), F32)
+    jobs = 2 * (hidden // width) + 4
+    return call(
+        functools.partial(widen_kernel, hidden),
+        [square] * 4 + [shape((width, hidden), F32), shape((hidden, width), F32)] + [shape((width,), F32)] * 4,
+        [ANY, ANY, VMEM],
+        [
+            pltpu.VMEM((jobs, width, width), BF16),
+            pltpu.VMEM((6, width, width), F32),
+            dma(jobs),
+            dma(6),
+        ],
+        "widen",
+        [ANY] * 6 + [VMEM] * 4,
+    )(dense, grads, total)
 
 
 def local(
@@ -1105,26 +1298,17 @@
     normed, q, k, v, mixed, lse, hidden, gate, send, cot_rows = forward(
         count, main, spare, inputs, g1, s1, g2, s2, w_query, w_key, w_value, w_out, router_t, slot_col, slot_row, cot_send
     )
-    y_rows, dx_back, dx_late, grad_first, grad_second = expert_block(
+    y_rows, dx_back, dx_late, grads = expert_block(
         count, main, spare, send_counts, send, cot_send, cot_rows, router_t, expert_in[0], expert_out[0]
     )
-    expert_sums = (lax.psum(grad_first, "dp").astype(F32), lax.psum(grad_second, "dp").astype(F32))
-    grad_inputs, dense, vec, y_back = backward(
-        count, main, spare, seq_group, domain_counts, inputs, cotangent, g1, g2, w_query, w_key, w_value, w_out, slot_col,
-        normed, q, k, v, mixed, lse, hidden, dx_back, dx_late, y_rows,
+    dp = lax.axis_size("dp")
+    grad_inputs, dense, vec, y_back, piece = backward(
+        dp, count, main, spare, seq_group, domain_counts, inputs, cotangent, g1, g2, w_query, w_key, w_value, w_out, slot_col,
+        normed, q, k, v, mixed, lse, hidden, dx_back, dx_late, y_rows, grads,
     )
-    output, dense, vec = finish(lax.axis_size("dp"), count, dense, vec, slot_col, hidden, gate, y_back)
-    dense = dense.astype(F32)
-    parts = [dense[i * width : (i + 1) * width] for i in range(4)]
-    vecs = [vec[i] for i in range(4)]
-    return (
-        output,
-        grad_inputs,
-        *vecs,
-        *parts,
-        expert_sums[0][None],
-        expert_sums[1][None],
-    )
+    output, dense, vec, grads = finish(dp, count, dense, vec, slot_col, hidden, gate, y_back, piece)
+    wq, wk, wv, wo, first, second, gain_a, shift_a, gain_b, shift_b = widen(expert_in.shape[2], dense, grads, vec)
+    return (output, grad_inputs, gain_a, shift_a, gain_b, shift_b, wq, wk, wv, wo, first[None], second[None])
 
 
 def solution(mesh):

time: 437 us -> 406 us (0.929)
  between operations: 15.2 us -> 1.79 us
  other arithmetic: 12 us -> 0 us
  local copies, waits for them, and re-layouts: 10.8 us -> 3.1 us
    pallas_call x1 -> x2, Pallas kernels: 94.4 us -> 111 us  [the longest x1 95.6 us: backward(): call(functools.partial(backward_kernel, dp, count, main, spare), [shape((...]
    pallas_call x1, Pallas kernels: 130 us -> 116 us  [finish(): call(functools.partial(finish_kernel, dp, count), [shape(hidden.shape, BF...]
    broadcast_in_dim x2 -> x0, other arithmetic: 12 us -> none  [the longest x1 7.52 us: local(): expert_sums[0][None]]
    slice x2 -> x0, local copies, waits for them, and re-layouts: 7.7 us -> none  [the longest x1 6.18 us: local(): parts = [dense[i * width:(i + 1) * width] for i in range(4)]]
  transfers between devices with their start and end apart: 1 -> 0, of which waited for: 0 -> 0; matrix products, arithmetic and copies ran while one was open for 2% -> 0% of each run, Pallas kernels for 52% -> 0%
where the time goes in v7:
time: 406 us; the launch traced here: 399 us
  Pallas kernels  394 us (97%)
    pallas_call x1, Pallas kernels, finish(): call(functools.partial(finish_kernel, dp, count), [shape(hidden.shape, BF...  116 us
    pallas_call x1, Pallas kernels, expert_block(): call(functools.partial(expert_kernel, count, main, spare, chunk), [rows,...  108 us
    pallas_call x1, Pallas kernels, backward(): call(functools.partial(backward_kernel, dp, count, main, spare), [shape((...  95.6 us
    pallas_call x1, Pallas kernels, forward(): call(functools.partial(forward_kernel, count, main, spare), [rows_low, ro...  51 us
    pallas_call x1, Pallas kernels, widen(): call(functools.partial(widen_kernel, hidden), [square] * 4 + [shape((widt...  15 us
    pallas_call x1, Pallas kernels, tables(): call(functools.partial(table_kernel, experts, main), [shape((slots, width...  8.25 us

profile of v7, /device:TPU:0, one launch (start us, length us, event | category | flops | bytes accessed | tf_op | source)
XLA Modules:
  0.0 399.4 jit_solution(964865208497759673)
XLA Ops:
  1.3 8.2 %tables.1 = (bf16[1792,768]{1,0:T(8,128)(2,1)}, s32[1024,128]{1,0:T(8,128)}, s32[8,1024]{1,0:T(8,128)}) custom-call(s32[1,8]{1,0:T(1,128)} %counts_ref.3, s32[1]{0:T(128)S(6)} %copy.31.group_ref, s32[8]{0:T(128)} %domain_ref.3, s32[1,1024]{1,0:T(1,128)} %sort_ref.1, bf16[1024,768]{1,0:T(8,128)(2,1)} %cot_hbm.1), custom_call_target="tpu_custom_call" | custom-call | flops 1000000000 | bytes 10000000 | tf_op jit(solution)/shard_map/tables/pallas_call | solution.py:1092
  9.5 51.0 %dense_forward.1 = (bf16[1024,768]{1,0:T(8,128)(2,1)}, bf16[1024,768]{1,0:T(8,128)(2,1)}, bf16[1024,768]{1,0:T(8,128)(2,1)}, bf16[1024,768]{1,0:T(8,128)(2,1)}, ...) custom-call(bf16[1024,768]{1,0:T(8,128)(2,1)} %x_hbm.1, ...), custom_call_target="tpu_custom_call" | custom-call | flops 1000000000 | bytes 10000000 | tf_op jit(solution)/shard_map/dense_forward/pallas_call | solution.py:1104
  60.5 108.5 %expert.1 = (bf16[2048,768]{1,0:T(8,128)(2,1)}, bf16[1536,768]{1,0:T(8,128)(2,1)}, bf16[896,768]{1,0:T(8,128)(2,1)}, bf16[6144,768]{1,0:T(8,128)(2,1)}) custom-call(s32[1,8]{1,0:T(1,128)} %counts_ref.3, bf16[1792,768]{1,0:T(8,128)(2,1)} %get-tuple-element.58.send_ref, bf16[1792,768]{1,0:T(8,128)(2,1)} %get-tuple-element.50.cot_send_ref, ...), custom_call_target="tpu_custom_call" | custom-call | flops 1000000000 | bytes 10000000 | tf_op jit(solution)/shard_map/expert/pallas_call | solution.py:1133
  169.0 95.6 %dense_backward.1 = (bf16[1024,768]{1,0:T(8,128)(2,1)}, bf16[3072,768]{1,0:T(8,128)(2,1)}, f32[8,768]{1,0:T(8,128)}, bf16[1792,768]{1,0:T(8,128)(2,1)}, bf16[1536,768]{1,0:T(8,128)(2,1)}) custom-call(s32[1]{0:T(128)S(6)} %copy.31.group_ref, s32[8]{0:T(128)} %domain_ref.3, bf16[1024,768]{1,0:T(8,128)(2,1)} %x_hbm.1, bf16[1024,768]{1,0:T(8,128)(2,1)} %cot_hbm.1, ...), custom_call_target="tpu_custom_call" | custom-call | flops 49999998976 | bytes 10000000 | tf_op jit(solution)/shard_map/dense_backward/pallas_call | solution.py:1177
  264.6 116.2 %finish.1 = (bf16[1024,768]{1,0:T(8,128)(2,1)}, bf16[3072,768]{1,0:T(8,128)(2,1)}, f32[8,768]{1,0:T(8,128)}, bf16[6144,768]{1,0:T(8,128)(2,1)}) custom-call(bf16[3072,768]{1,0:T(8,128)(2,1)} %get-tuple-element.64.dense_ref, f32[8,768]{1,0:T(8,128)} %get-tuple-element.65.vec_ref, s32[1024,128]{1,0:T(8,128)} %get-tuple-element.48.slot_col_ref.slot_col_hbm, ...), custom_call_target="tpu_custom_call" | custom-call | flops 1000000000 | bytes 10000000 | tf_op jit(solution)/shard_map/finish/pallas_call | solution.py:1223
  380.8 0.0 copy-start.1
  380.8 15.0 %widen.1 = (f32[768,768]{1,0:T(8,128)}, f32[768,768]{1,0:T(8,128)}, f32[768,768]{1,0:T(8,128)}, f32[768,768]{1,0:T(8,128)}, f32[768,3072]{1,0:T(8,128)}, /*index...) custom-call(bf16[3072,768]{1,0:T(8,128)(2,1)} %get-tuple-element.71.dense_hbm, ...), custom_call_target="tpu_custom_call" | custom-call | flops 1000000000 | bytes 10000000 | tf_op jit(solution)/shard_map/widen/pallas_call | solution.py:1254
  395.8 0.0 copy-start
  395.8 0.0 copy-done.1
  395.8 1.1 copy.32
  397.0 0.8 copy-done
  397.8 1.1 copy.33
Async XLA Ops:
  380.8 15.0 %copy-start.1 = (bf16[1024,768]{1,0:T(8,128)(2,1)S(1)}, bf16[1024,768]{1,0:T(8,128)(2,1)}, u32[]{:S(2)}) copy-start(bf16[1024,768]{1,0:T(8,128)(2,1)} %get-tuple-element.96) | copy-start | bytes 4718596
  395.8 2.0 copy-start

commit v8 on v7

--- a/solution.py
+++ b/solution.py
@@ -15,7 +15,7 @@
 BF16 = jnp.bfloat16
 BLK = 256
 CODE = 4096
-LIMIT = 60 * 1024 * 1024
+LIMIT = 63 * 1024 * 1024
 
 VMEM = pl.BlockSpec(memory_space=pltpu.VMEM)
 SMEM = pl.BlockSpec(memory_space=pltpu.SMEM)
@@ -85,9 +85,21 @@
     )
 
 
+def last_returns(count):
+    return count // 8
+
+
 def dp_sides():
     index = lax.axis_index("dp")
     return index, (index % 2, (index // 2) % 2)
+
+
+def each_rows(rows, step, size=64):
+    def body(block, carry):
+        step(pl.ds(pl.multiple_of(block * size, size), size))
+        return carry
+
+    lax.fori_loop(0, rows // size, body, 0)
 
 
 def sum_rows(target, other, rows):
@@ -211,12 +223,14 @@
     k_ref,
     v_ref,
     mixed_ref,
-    lse_ref,
     hidden_ref,
     gate_ref,
     send_ref,
     cot_rows_ref,
+    probs_hbm,
     routed,
+    probs,
+    prob_sems,
     sends,
     recvs,
     spare_sends,
@@ -259,7 +273,14 @@
 
     keep = iota((BLK, BLK), 0) <= iota((BLK, BLK), 1)
 
+    def keep_probs(pair):
+        return pltpu.make_async_copy(probs.at[pair % 2], probs_hbm.at[pair], prob_sems.at[pair % 2])
+
     def attend(pair, carry):
+        @pl.when(pair >= 2)
+        def _():
+            keep_probs(pair - 2).wait()
+
         cols = pl.ds(pl.multiple_of(pair * 128, 128), 128)
         k_pair = k_ref[:, cols]
         v_t = v_ref[:, cols].astype(F32).T.astype(BF16)
@@ -275,10 +296,11 @@
                 peak = jnp.max(scores, axis=0, keepdims=True)
                 exps = jnp.exp(scores - peak)
                 total = jnp.sum(exps, axis=0, keepdims=True)
-                out = nn(v_t[half * 64 : half * 64 + 64, :span], exps.astype(BF16))
-                outs.append(out * (1.0 / total))
-                lse_ref[pair, half : half + 1, pl.ds(block * BLK, BLK)] = peak + jnp.log(total)
+                attention = (exps * (1.0 / total)).astype(BF16)
+                probs[pair % 2, half, pl.ds(block * (block + 1) // 2 * BLK, (block + 1) * BLK), :] = attention
+                outs.append(nn(v_t[half * 64 : half * 64 + 64, :span], attention))
             mixed_ref[pl.ds(block * BLK, BLK), cols] = jnp.concatenate(outs, axis=0).T.astype(BF16)
+        keep_probs(pair).start()
         return carry
 
     lax.fori_loop(0, HEADS // 2, attend, 0)
@@ -299,18 +321,17 @@
 
     lax.fori_loop(0, blocks, finish, 0)
     pack_rows(slot_row_ref[0:1, :], routed, send_ref)
-    for copy in mine:
+    for copy in mine + [keep_probs(HEADS // 2 - 2), keep_probs(HEADS // 2 - 1)]:
         copy.wait()
     for copy in copies + [gather(0)]:
         copy.wait()
 
 
 def gelu_parts(v):
-    size = jnp.abs(v)
-    t = 1.0 / (1.0 + (0.3275911 * 0.7071067811865476) * size)
-    bell = jnp.exp(-0.5 * (v * v))
-    poly = ((((1.061405429 * t - 1.453152027) * t + 1.421413741) * t - 0.284496736) * t + 0.254829592) * t
-    tail = 0.5 * poly * bell
+    t = 1.0 / (1.0 + (0.3275911 * 0.7071067811865476) * jnp.abs(v))
+    bell = jnp.exp2((-0.5 * 1.4426950408889634) * (v * v))
+    poly = ((((0.5307027145 * t - 0.7265760135) * t + 0.7107068705) * t - 0.142248368) * t + 0.127414796) * t
+    tail = poly * bell
     return jnp.where(v >= 0.0, 1.0 - tail, tail), bell * 0.3989422804014327
 
 
@@ -411,8 +432,15 @@
     ]
     for copy in mine_in:
         copy.start()
-    acc1[...] = jnp.zeros_like(acc1)
-    acc2[...] = jnp.zeros_like(acc2)
+
+    def clear_one(part):
+        acc1[part, :] = jnp.zeros((64, hidden), F32)
+
+    def clear_two(part):
+        acc2[part, :] = jnp.zeros((64, width), F32)
+
+    each_rows(width, clear_one)
+    each_rows(hidden, clear_two)
     experts = router_ref.shape[0]
     router = jnp.sum(jnp.where(iota((experts, 1), 0) == me, router_ref[...].astype(F32), 0.0), axis=0, keepdims=True)
     hot = jnp.full((1, 128), counts_ref[0, me], jnp.int32)[:, 0:1] > main
@@ -508,7 +536,11 @@
         slot = index % 2
         if index >= 2:
             writes[index - 2].wait()
-        stage[slot] = piece[...].astype(BF16)
+
+        def narrow(part):
+            stage[slot, part, :] = piece[part, :].astype(BF16)
+
+        each_rows(width, narrow)
         write = pltpu.make_async_copy(stage.at[slot], target, stage_sems.at[slot])
         write.start()
         writes.append(write)
@@ -554,7 +586,7 @@
     k_hbm,
     v_hbm,
     mixed_hbm,
-    lse_hbm,
+    probs_hbm,
     hidden_hbm,
     dx_hbm,
     late_ref,
@@ -577,17 +609,16 @@
     k_ref,
     v_ref,
     mixed_ref,
-    lse_ref,
     hidden_ref,
     dx_ref,
     spare_dx,
     spare_y,
     dx_land,
     y_land,
+    probs,
     kept,
     land_one,
     land_two,
-    ghid,
     gmix,
     branch,
     normed_t,
@@ -607,6 +638,7 @@
     scatter_sends,
     scatter_recvs,
     keeps,
+    prob_sems,
 ):
     tokens, width = x_ref.shape
     me = lax.axis_index("expert")
@@ -628,7 +660,6 @@
         (k_hbm, k_ref),
         (v_hbm, v_ref),
         (mixed_hbm, mixed_ref),
-        (lse_hbm, lse_ref),
         (hidden_hbm, hidden_ref),
     ]
     operands = [pltpu.make_async_copy(source, target, fills.at[i]) for i, (source, target) in enumerate(operands)]
@@ -644,12 +675,27 @@
     portion = grads_hbm.shape[0] // 4
     quarter = portion // 2
 
-    def scatter_one(stream):
-        start = 2 * portion * stream + (1 - bits[stream]) * portion
+    def scatter_one(stream, second):
+        side = bits[1 - stream] if second else 1 - bits[1 - stream]
+        start = 2 * portion * stream + (1 - bits[stream]) * portion + side * quarter
         device = {"dp": flip(place, 1 << stream, dp)}
         return copy_to(
-            grads_hbm.at[span(start, portion)], land_one.at[stream], scatter_sends.at[0, stream], scatter_recvs.at[0, stream], device
+            grads_hbm.at[span(start, quarter)],
+            land_one.at[stream, span(side * quarter, quarter)],
+            scatter_sends.at[second, stream],
+            scatter_recvs.at[second, stream],
+            device,
         )
+
+    def add_one(stream, second):
+        side = bits[1 - stream] if second else 1 - bits[1 - stream]
+        scatter_one(stream, second).wait()
+
+        def step(rows):
+            held = span(side * quarter + rows.start, 64)
+            kept[stream, held, :] = (kept[stream, held, :].astype(F32) + land_one[stream, held, :].astype(F32)).astype(BF16)
+
+        each_rows(quarter, step)
 
     def keep_one(stream):
         start = 2 * portion * stream + bits[stream] * portion
@@ -661,8 +707,8 @@
         return copy_to(
             kept.at[stream, span(start, quarter)],
             land_two.at[stream],
-            scatter_sends.at[1, stream],
-            scatter_recvs.at[1, stream],
+            scatter_sends.at[2, stream],
+            scatter_recvs.at[2, stream],
             device,
         )
 
@@ -672,8 +718,14 @@
             kept.at[stream, span(start, quarter)], piece_ref.at[pl.ds(stream * quarter, quarter)], keeps.at[stream]
         )
 
+    def load_probs(pair):
+        return pltpu.make_async_copy(probs_hbm.at[pair], probs.at[pair % 2], prob_sems.at[pair % 2])
+
+    load_probs(0).start()
+    for part in range(2):
+        for stream in range(2):
+            scatter_one(stream, part).start()
     for stream in range(2):
-        scatter_one(stream).start()
         keep_one(stream).start()
 
     def sum_dx(step):
@@ -695,7 +747,9 @@
     lates = [return_block(me, count, main, mask, late_ref, dx_ref, late_sends, late_recvs, early) for mask in range(early, count)]
     for copy in lates:
         copy.start()
-    copies = [return_block(me, count, main, mask, y_ref, y_back_ref, sends, recvs) for mask in range(1, count)]
+    copies = [
+        return_block(me, count, main, mask, y_ref, y_back_ref, sends, recvs) for mask in range(1, count - last_returns(count))
+    ]
     mine = pltpu.make_async_copy(y_ref.at[pl.ds(0, main)], y_back_ref.at[span(me * main, main)], own.at[0])
     mine.start()
     loads = [
@@ -740,7 +794,7 @@
         gg = grad * gain_two
         inner = gg - jnp.mean(gg, axis=1, keepdims=True) - hat * jnp.mean(gg * hat, axis=1, keepdims=True)
         total = cot_ref[rows, :].astype(F32) * weight + rstd * inner
-        ghid[rows, :] = total
+        hidden_ref[rows, :] = total
         low = total.astype(BF16)
         branch[rows, :] = low
         gmix[rows, :] = nt(low, wo_ref[...]).astype(BF16)
@@ -752,17 +806,22 @@
     settle(sum_y(depth - 1), spare_y, y_land, depth - 1)
     sum_y(depth - 2).start()
 
-    keep = iota((BLK, BLK), 0) <= iota((BLK, BLK), 1)
+    for stream in range(2):
+        keep_one(stream).wait()
+        add_one(stream, 0)
+        scatter_two(stream).start()
 
     def attend(pair, carry):
-        @pl.when(pair == HEADS // 4)
+        @pl.when(pair + 1 < HEADS // 2)
+        def _():
+            load_probs(pair + 1).start()
+
+        @pl.when(pair == 4)
         def _():
             for stream in range(2):
-                keep_one(stream).wait()
-                scatter_one(stream).wait()
-                sum_rows(kept.at[stream], land_one.at[stream], portion)
-                scatter_two(stream).start()
-
+                add_one(stream, 1)
+
+        load_probs(pair).wait()
         base = pl.multiple_of(pair * 128, 128)
         cols = pl.ds(base, 128)
         q_pair = q_ref[:, cols]
@@ -771,7 +830,6 @@
         o_pair = gmix[:, cols]
         low = lane < 64
         q_head = [jnp.where(low, q_pair, 0), jnp.where(low, 0, q_pair)]
-        k_head = [jnp.where(low, k_pair, 0), jnp.where(low, 0, k_pair)]
         v_head = [jnp.where(low, v_pair, 0), jnp.where(low, 0, v_pair)]
         o_head = [jnp.where(low, o_pair, 0), jnp.where(low, 0, o_pair)]
         k_t = k_pair.astype(F32).T.astype(BF16)
@@ -783,13 +841,14 @@
             dk = None
             dv = None
             for half in range(2):
-                scores = nt(k_head[half][start : start + BLK], q_pair[start:])
-                diag = jnp.where(keep, scores[:, :BLK], -1000000000.0)
-                scores = jnp.concatenate([diag, scores[:, BLK:]], axis=1) if block < blocks - 1 else diag
-                probs = jnp.exp(scores - lse_ref[pair, half : half + 1, pl.ds(start, tokens - start)])
+                tiles = [
+                    probs[pair % 2, half, pl.ds((later * (later + 1) // 2 + block) * BLK, BLK), :]
+                    for later in range(block, blocks)
+                ]
+                attention = jnp.concatenate(tiles, axis=1) if block < blocks - 1 else tiles[0]
                 grad_p = nt(v_head[half][start : start + BLK], o_pair[start:])
-                grad_s = (probs * (grad_p - delta[half][:, start:])).astype(BF16)
-                dv_part = nn(probs.astype(BF16), o_head[half][start:])
+                grad_s = (attention.astype(F32) * (grad_p - delta[half][:, start:])).astype(BF16)
+                dv_part = nn(attention, o_head[half][start:])
                 dk_part = nn(grad_s, q_head[half][start:])
                 dv = dv_part if dv is None else dv + dv_part
                 dk = dk_part if dk is None else dk + dk_part
@@ -820,7 +879,7 @@
         sums[1:2, :] += jnp.sum(grad, axis=0, keepdims=True)
         gg = grad * gain_one
         inner = gg - jnp.mean(gg, axis=1, keepdims=True) - hat * jnp.mean(gg * hat, axis=1, keepdims=True)
-        grad_ref[rows, :] = (ghid[rows, :] + rstd * inner).astype(BF16)
+        grad_ref[rows, :] = (hidden_ref[rows, :] + rstd * inner).astype(BF16)
         return carry
 
     lax.fori_loop(0, blocks, close_block, 0)
@@ -867,12 +926,14 @@
     slot_col_ref,
     hidden_ref,
     gate_ref,
-    y_ref,
+    y_hbm,
+    y_rows_hbm,
     piece_ref,
     out_ref,
     full_ref,
     total_ref,
     grads_ref,
+    y_ref,
     acc,
     landing,
     full,
@@ -888,9 +949,14 @@
     unit_sends,
     unit_recvs,
     own,
+    y_sends,
+    y_recvs,
+    gets,
 ):
     tokens, width = hidden_ref.shape
     slots = y_ref.shape[0]
+    main = (slots - BLK) // count
+    early = count - last_returns(count)
     rows = dense_ref.shape[0] // STREAMS
     place = {"dp": lax.axis_index("dp"), "expert": lax.axis_index("expert")}
     size = {"dp": dp, "expert": count}
@@ -903,7 +969,17 @@
     barrier = pltpu.get_barrier_semaphore()
     for axis, mask in plans[0]:
         pl.semaphore_signal(barrier, inc=1, device_id=partner(axis, mask), device_id_type=MESH)
-    pl.semaphore_wait(barrier, steps)
+    for mask in range(early, count):
+        pl.semaphore_signal(barrier, inc=1, device_id=partner("expert", mask), device_id_type=MESH)
+    pl.semaphore_wait(barrier, steps + count - early)
+    me = place["expert"]
+    y_copies = [return_block(me, count, main, mask, y_rows_hbm, y_ref, y_sends, y_recvs) for mask in range(early, count)]
+    loads = [pltpu.make_async_copy(y_hbm.at[pl.ds(count * main, BLK)], y_ref.at[pl.ds(count * main, BLK)], gets.at[count])]
+    for mask in range(early):
+        part = span(flip(me, mask, count) * main, main)
+        loads.append(pltpu.make_async_copy(y_hbm.at[part], y_ref.at[part], gets.at[mask]))
+    for load in loads:
+        load.start()
 
     def side(axis, mask):
         return (place[axis] // mask) % 2
@@ -950,13 +1026,12 @@
         copy.start()
 
     def combine(block):
-        rows_at = pl.ds(block * BLK, BLK)
+        rows_at = pl.ds(pl.multiple_of(block * BLK, BLK), BLK)
         slot = slot_col_ref[rows_at, 0:1]
         pick = jnp.where(iota((BLK, slots), 1) == slot, 1.0, 0.0).astype(BF16)
         returned = nn(pick, y_ref[...])
         out_ref[rows_at, :] = (hidden_ref[rows_at, :] + gate_ref[rows_at, 0:1] * returned).astype(BF16)
 
-    todo = list(range(tokens // BLK))
     low = [jnp.int32(stream * rows) for stream in range(STREAMS)]
     extent = rows
     offset = 0
@@ -981,20 +1056,22 @@
         vec_copy = copy_to(vec_source, vec_land.at[step], vec_sends.at[step], vec_recvs.at[step], partner(axis, mask))
         vec_copy.start()
         advance(1)
-        if step in (1, 2):
-            for block in todo[: tokens // BLK // 4]:
-                combine(block)
-            todo = todo[tokens // BLK // 4 :]
+        if step == 0:
+            for copy in y_copies:
+                copy.start()
         trail.append((list(low), extent))
         for stream in range(STREAMS):
             copy, kept, source = copies[stream]
             copy.wait()
-            held = span(kept, part)
-            value = source[held, :].astype(F32) + landing[stream, pl.ds(offset, part), :].astype(F32)
-            if step < steps - 1:
-                acc[step % 2, held, :] = value.astype(BF16)
-            else:
-                full[held, :] = value.astype(BF16)
+            target = acc.at[step % 2] if step < steps - 1 else full
+            grain = min(part, 64)
+
+            def add(rows_at):
+                held = span(kept + rows_at.start, grain)
+                value = source[held, :].astype(F32) + landing[stream, span(offset + rows_at.start, grain), :].astype(F32)
+                target[held, :] = value.astype(BF16)
+
+            each_rows(part, add, grain)
             low[stream] = kept
         vec_copy.wait()
         vec_sum = vec_source[...] + vec_land[step]
@@ -1017,10 +1094,15 @@
             copy.start()
             copies.append(copy)
         advance(2)
-        if step in (1, 2):
-            for block in todo if step == 1 else todo[: tokens // BLK // 4]:
+        if step == 1:
+            for copy in loads + y_copies:
+                copy.wait()
+
+            def combine_block(block, carry):
                 combine(block)
-            todo = todo[tokens // BLK // 4 :]
+                return carry
+
+            lax.fori_loop(0, tokens // BLK, combine_block, 0)
         for stream in range(STREAMS):
             copies[stream].wait()
             low[stream] = origins[stream]
@@ -1058,7 +1140,11 @@
         loads[index].wait()
         if index >= slots:
             stores[index - slots].wait()
-        high[index % slots] = low[index].astype(F32)
+
+        def step(part):
+            high[index % slots, part, :] = low[index, part, :].astype(F32)
+
+        each_rows(width, step)
         stores.append(pltpu.make_async_copy(high.at[index % slots], target, puts.at[index % slots]))
         stores[-1].start()
     for store in stores[-slots:]:
@@ -1100,6 +1186,8 @@
 
 def forward(count, main, spare, inputs, g1, s1, g2, s2, wq, wk, wv, wo, router, slot_col, slot_row, cot_send):
     tokens, width = inputs.shape
+    blocks = tokens // BLK
+    prob_block = (2, blocks * (blocks + 1) // 2 * BLK, BLK)
     rows_low = shape((tokens, width), BF16)
     return call(
         functools.partial(forward_kernel, count, main, spare),
@@ -1109,16 +1197,25 @@
             rows_low,
             rows_low,
             rows_low,
-            shape((HEADS // 2, 8, tokens), F32),
             shape((tokens, width), F32),
             shape((tokens, 128), F32),
             shape(cot_send.shape, BF16),
             shape((count * (main + spare), width), BF16),
+            shape((HEADS // 2,) + prob_block, BF16),
         ],
         [VMEM] * 12 + [ANY],
-        [pltpu.VMEM((tokens, width), BF16), dma(count), dma(count), dma(depth_of(count)), dma(depth_of(count)), dma(2)],
+        [
+            pltpu.VMEM((tokens, width), BF16),
+            pltpu.VMEM((2,) + prob_block, BF16),
+            dma(2),
+            dma(count),
+            dma(count),
+            dma(depth_of(count)),
+            dma(depth_of(count)),
+            dma(2),
+        ],
         "dense_forward",
-        [VMEM] * 9 + [ANY],
+        [VMEM] * 8 + [ANY] * 2,
         1,
     )(inputs, g1, s1, g2, s2, wq, wk, wv, wo, router, slot_col, slot_row, cot_send)
 
@@ -1170,7 +1267,7 @@
 
 def backward(
     dp, count, main, spare, group, domains, inputs, cotangent, g1, g2, wq, wk, wv, wo, slot_col,
-    normed, q, k, v, mixed, lse, hidden, dx, late, y, grads,
+    normed, q, k, v, mixed, probs, hidden, dx, late, y, grads,
 ):
     tokens, width = inputs.shape
     half = grads.shape[0] // 4
@@ -1178,17 +1275,17 @@
         functools.partial(backward_kernel, dp, count, main, spare),
         [shape((tokens, width), BF16), shape((4 * width, width), BF16), shape((8, width), F32), shape((count * main + BLK, width), BF16), shape((half, width), BF16)],
         [SMEM] * 2 + [ANY] * 2 + [VMEM] * 2 + [ANY] * 16,
-        [pltpu.VMEM(v.shape, v.dtype) for v in (inputs, cotangent, wq, wk, wv, wo, slot_col, normed, q, k, v, mixed, lse, hidden)]
+        [pltpu.VMEM(v.shape, v.dtype) for v in (inputs, cotangent, wq, wk, wv, wo, slot_col, normed, q, k, v, mixed, hidden)]
         + [
             pltpu.VMEM((count * main + BLK, width), BF16),
             pltpu.VMEM((count * spare, width), BF16),
             pltpu.VMEM((count * spare, width), BF16),
             pltpu.VMEM((count * spare, width), BF16),
             pltpu.VMEM((count * spare, width), BF16),
+            pltpu.VMEM((2,) + probs.shape[1:], BF16),
             pltpu.VMEM((2, half, width), BF16),
             pltpu.VMEM((2, half, width), BF16),
             pltpu.VMEM((2, half // 2, width), BF16),
-            pltpu.VMEM((tokens, width), F32),
             pltpu.VMEM((tokens, width), BF16),
             pltpu.VMEM((tokens, width), BF16),
             pltpu.VMEM((width, tokens), BF16),
@@ -1204,27 +1301,29 @@
             dma(depth_of(count)),
             dma(3),
             dma(count),
-            dma(14),
-            dma(2, 2),
-            dma(2, 2),
+            dma(13),
+            dma(3, 2),
+            dma(3, 2),
+            dma(2),
             dma(2),
         ],
         "dense_backward",
         [VMEM, VMEM, VMEM, ANY, ANY],
         3,
         5 * 10**10,
-    )(group, domains, inputs, cotangent, g1, g2, wq, wk, wv, wo, slot_col, normed, q, k, v, mixed, lse, hidden, dx, late, y, grads)
-
-
-def finish(dp, count, dense, vec, slot_col, hidden, gate, y_back, piece):
+    )(group, domains, inputs, cotangent, g1, g2, wq, wk, wv, wo, slot_col, normed, q, k, v, mixed, probs, hidden, dx, late, y, grads)
+
+
+def finish(dp, count, dense, vec, slot_col, hidden, gate, y_back, y_rows, piece):
     width = hidden.shape[1]
     rows = dense.shape[0]
     steps = len(halving_plan(dp, count, rows // STREAMS)[0][0])
     return call(
         functools.partial(finish_kernel, dp, count),
         [shape(hidden.shape, BF16), shape(dense.shape, BF16), shape(vec.shape, F32), shape((4 * piece.shape[0], width), BF16)],
-        [VMEM] * 6 + [ANY],
+        [VMEM] * 5 + [ANY] * 3,
         [
+            pltpu.VMEM(y_back.shape, BF16),
             pltpu.VMEM((2, rows, width), BF16),
             pltpu.VMEM((STREAMS, rows // STREAMS + 64, width), BF16),
             pltpu.VMEM((rows, width), BF16),
@@ -1240,11 +1339,14 @@
             dma(3 * CHUNKS, 2),
             dma(3 * CHUNKS, 2),
             dma(2),
+            dma(count),
+            dma(count),
+            dma(count + 1),
         ],
         "finish",
         [VMEM, ANY, VMEM, ANY],
         4,
-    )(dense, vec, slot_col, hidden, gate, y_back, piece)
+    )(dense, vec, slot_col, hidden, gate, y_back, y_rows, piece)
 
 
 def widen(hidden, dense, grads, total):
@@ -1295,7 +1397,7 @@
     g1, s1, g2, s2 = gain_one, shift_one, gain_two, shift_two
     router_t = router.T
     cot_send, slot_col, slot_row = tables(experts, main, slots, send_counts, seq_group, domain_counts, sort_order, cotangent)
-    normed, q, k, v, mixed, lse, hidden, gate, send, cot_rows = forward(
+    normed, q, k, v, mixed, hidden, gate, send, cot_rows, probs = forward(
         count, main, spare, inputs, g1, s1, g2, s2, w_query, w_key, w_value, w_out, router_t, slot_col, slot_row, cot_send
     )
     y_rows, dx_back, dx_late, grads = expert_block(
@@ -1304,9 +1406,9 @@
     dp = lax.axis_size("dp")
     grad_inputs, dense, vec, y_back, piece = backward(
         dp, count, main, spare, seq_group, domain_counts, inputs, cotangent, g1, g2, w_query, w_key, w_value, w_out, slot_col,
-        normed, q, k, v, mixed, lse, hidden, dx_back, dx_late, y_rows, grads,
+        normed, q, k, v, mixed, probs, hidden, dx_back, dx_late, y_rows, grads,
     )
-    output, dense, vec, grads = finish(dp, count, dense, vec, slot_col, hidden, gate, y_back, piece)
+    output, dense, vec, grads = finish(dp, count, dense, vec, slot_col, hidden, gate, y_back, y_rows, piece)
     wq, wk, wv, wo, first, second, gain_a, shift_a, gain_b, shift_b = widen(expert_in.shape[2], dense, grads, vec)
     return (output, grad_inputs, gain_a, shift_a, gain_b, shift_b, wq, wk, wv, wo, first[None], second[None])
 

time: 406 us -> 396 us (0.975); the launches traced: 399 us -> 396 us
    pallas_call x1, Pallas kernels: 108 us -> 103 us  [expert_block(): call(functools.partial(expert_kernel, count, main, spare, chunk), [rows,...]
    pallas_call x1, Pallas kernels: 51 us -> 55.4 us  [forward(): call(functools.partial(forward_kernel, count, main, spare), [rows_low, ro...]
where the time goes in v8:
time: 396 us
  Pallas kernels  390 us (98%)
    pallas_call x1, Pallas kernels, finish(): call(functools.partial(finish_kernel, dp, count), [shape(hidden.shape, BF...  116 us
    pallas_call x1, Pallas kernels, expert_block(): call(functools.partial(expert_kernel, count, main, spare, chunk), [rows,...  103 us
    pallas_call x1, Pallas kernels, backward(): call(functools.partial(backward_kernel, dp, count, main, spare), [shape((...  92.4 us
    pallas_call x1, Pallas kernels, forward(): call(functools.partial(forward_kernel, count, main, spare), [rows_low, ro...  55.4 us
    pallas_call x1, Pallas kernels, widen(): call(functools.partial(widen_kernel, hidden), [square] * 4 + [shape((widt...  14.8 us
    pallas_call x1, Pallas kernels, tables(): call(functools.partial(table_kernel, experts, main), [shape((slots, width...  8.25 us

profile of v8, /device:TPU:0, one launch (start us, length us, event | category | flops | bytes accessed | tf_op | source)
XLA Modules:
  0.0 395.7 jit_solution(11202371545455053407)
XLA Ops:
  1.3 8.2 %tables.1 = (bf16[1792,768]{1,0:T(8,128)(2,1)}, s32[1024,128]{1,0:T(8,128)}, s32[8,1024]{1,0:T(8,128)}) custom-call(s32[1,8]{1,0:T(1,128)} %counts_ref.3, s32[1]{0:T(128)S(6)} %copy.31.group_ref, s32[8]{0:T(128)} %domain_ref.3, s32[1,1024]{1,0:T(1,128)} %sort_ref.1, bf16[1024,768]{1,0:T(8,128)(2,1)} %cot_hbm.1), custom_call_target="tpu_custom_call" | custom-call | flops 1000000000 | bytes 10000000 | tf_op jit(solution)/shard_map/tables/pallas_call | solution.py:1178
  9.5 55.4 %dense_forward.1 = (bf16[1024,768]{1,0:T(8,128)(2,1)}, bf16[1024,768]{1,0:T(8,128)(2,1)}, bf16[1024,768]{1,0:T(8,128)(2,1)}, bf16[1024,768]{1,0:T(8,128)(2,1)}, ...) custom-call(bf16[1024,768]{1,0:T(8,128)(2,1)} %x_hbm.1, ...), custom_call_target="tpu_custom_call" | custom-call | flops 1000000000 | bytes 10000000 | tf_op jit(solution)/shard_map/dense_forward/pallas_call | solution.py:1192
  65.0 103.4 %expert.1 = (bf16[2048,768]{1,0:T(8,128)(2,1)}, bf16[1536,768]{1,0:T(8,128)(2,1)}, bf16[896,768]{1,0:T(8,128)(2,1)}, bf16[6144,768]{1,0:T(8,128)(2,1)}) custom-call(s32[1,8]{1,0:T(1,128)} %counts_ref.3, bf16[1792,768]{1,0:T(8,128)(2,1)} %get-tuple-element.58.send_ref, bf16[1792,768]{1,0:T(8,128)(2,1)} %get-tuple-element.50.cot_send_ref, ...), custom_call_target="tpu_custom_call" | custom-call | flops 1000000000 | bytes 10000000 | tf_op jit(solution)/shard_map/expert/pallas_call | solution.py:1230
  168.4 92.4 %dense_backward.1 = (bf16[1024,768]{1,0:T(8,128)(2,1)}, bf16[3072,768]{1,0:T(8,128)(2,1)}, f32[8,768]{1,0:T(8,128)}, bf16[1792,768]{1,0:T(8,128)(2,1)}, bf16[1536,768]{1,0:T(8,128)(2,1)}) custom-call(s32[1]{0:T(128)S(6)} %copy.31.group_ref, s32[8]{0:T(128)} %domain_ref.3, bf16[1024,768]{1,0:T(8,128)(2,1)} %x_hbm.1, bf16[1024,768]{1,0:T(8,128)(2,1)} %cot_hbm.1, ...), custom_call_target="tpu_custom_call" | custom-call | flops 49999998976 | bytes 10000000 | tf_op jit(solution)/shard_map/dense_backward/pallas_call | solution.py:1274
  260.8 116.1 %finish.1 = (bf16[1024,768]{1,0:T(8,128)(2,1)}, bf16[3072,768]{1,0:T(8,128)(2,1)}, f32[8,768]{1,0:T(8,128)}, bf16[6144,768]{1,0:T(8,128)(2,1)}) custom-call(bf16[3072,768]{1,0:T(8,128)(2,1)} %get-tuple-element.64.dense_ref, f32[8,768]{1,0:T(8,128)} %get-tuple-element.65.vec_ref, s32[1024,128]{1,0:T(8,128)} %get-tuple-element.48.slot_col_ref.slot_col_hbm, ...), custom_call_target="tpu_custom_call" | custom-call | flops 1000000000 | bytes 10000000 | tf_op jit(solution)/shard_map/finish/pallas_call | solution.py:1321
  377.0 14.8 %widen.1 = (f32[768,768]{1,0:T(8,128)}, f32[768,768]{1,0:T(8,128)}, f32[768,768]{1,0:T(8,128)}, f32[768,768]{1,0:T(8,128)}, f32[768,3072]{1,0:T(8,128)}, /*index...) custom-call(bf16[3072,768]{1,0:T(8,128)(2,1)} %get-tuple-element.71.dense_hbm, ...), custom_call_target="tpu_custom_call" | custom-call | flops 1000000000 | bytes 10000000 | tf_op jit(solution)/shard_map/widen/pallas_call | solution.py:1356
  391.8 0.0 copy-start
  391.8 2.8 copy.32
  394.6 0.0 copy-done
  394.6 1.1 copy.33
Async XLA Ops:
  391.8 2.8 copy-start

commit v9 on v8

--- a/solution.py
+++ b/solution.py
@@ -210,10 +210,10 @@
     shift_one_ref,
     gain_two_ref,
     shift_two_ref,
-    wq_ref,
-    wk_ref,
-    wv_ref,
-    wo_ref,
+    wq_hbm,
+    wk_hbm,
+    wv_hbm,
+    wo_hbm,
     router_ref,
     slot_col_ref,
     slot_row_ref,
@@ -228,6 +228,10 @@
     send_ref,
     cot_rows_ref,
     probs_hbm,
+    wq_ref,
+    wk_ref,
+    wv_ref,
+    wo_ref,
     routed,
     probs,
     prob_sems,
@@ -236,10 +240,15 @@
     spare_sends,
     spare_recvs,
     own,
+    fills,
 ):
     tokens, width = x_ref.shape
     blocks = tokens // BLK
     me = lax.axis_index("expert")
+    weights = [(wq_hbm, wq_ref), (wk_hbm, wk_ref), (wv_hbm, wv_ref), (wo_hbm, wo_ref)]
+    weights = [pltpu.make_async_copy(source, target, fills.at[i]) for i, (source, target) in enumerate(weights)]
+    for copy in weights:
+        copy.start()
     greet("expert", me, count)
     base = count * main
 
@@ -269,6 +278,8 @@
         v_ref[rows, :] = nn(normed, wv_ref[...]).astype(BF16)
         return carry
 
+    for copy in weights:
+        copy.wait()
     lax.fori_loop(0, blocks, project, 0)
 
     keep = iota((BLK, BLK), 0) <= iota((BLK, BLK), 1)
@@ -470,7 +481,7 @@
 
         for step in range(depth):
 
-            @pl.when(turn == (max(step + 1, plain - depth + step) if step else 1))
+            @pl.when(turn == (max(step + 1, plain - depth + step + 1) if step else 1))
             def _():
                 gather(step).wait_recv()
                 if step:
@@ -593,7 +604,7 @@
     y_ref,
     grads_hbm,
     grad_ref,
-    dense_ref,
+    dense_hbm,
     vec_ref,
     y_back_ref,
     piece_ref,
@@ -610,6 +621,7 @@
     v_ref,
     mixed_ref,
     hidden_ref,
+    dense_ref,
     dx_ref,
     spare_dx,
     spare_y,
@@ -639,6 +651,7 @@
     scatter_recvs,
     keeps,
     prob_sems,
+    puts,
 ):
     tokens, width = x_ref.shape
     me = lax.axis_index("expert")
@@ -802,7 +815,12 @@
         return carry
 
     lax.fori_loop(0, blocks, open_block, 0)
+    def put_dense(part):
+        rows = pl.ds(part * width, width)
+        return pltpu.make_async_copy(dense_ref.at[rows], dense_hbm.at[rows], puts.at[part])
+
     dense_ref[pl.ds(3 * width, width), :] = tn(mixed_ref[...], branch[...]).astype(BF16)
+    put_dense(3).start()
     settle(sum_y(depth - 1), spare_y, y_land, depth - 1)
     sum_y(depth - 2).start()
 
@@ -868,6 +886,7 @@
 
     for part in range(3):
         dense_ref[pl.ds(part * width, width), :] = nn(normed_t[...], dqkv[:, pl.ds(part * width, width)]).astype(BF16)
+        put_dense(part).start()
 
     def close_block(block, carry):
         rows = pl.ds(pl.multiple_of(block * BLK, BLK), BLK)
@@ -898,6 +917,8 @@
     spare_out.wait()
     for stream in range(2):
         store_piece(stream).wait()
+    for part in range(4):
+        put_dense(part).wait()
     mine.wait()
     for copy in copies:
         copy.wait()
@@ -921,11 +942,11 @@
 def finish_kernel(
     dp,
     count,
-    dense_ref,
+    dense_hbm,
     vec_ref,
-    slot_col_ref,
-    hidden_ref,
-    gate_ref,
+    slot_col_hbm,
+    hidden_hbm,
+    gate_hbm,
     y_hbm,
     y_rows_hbm,
     piece_ref,
@@ -933,6 +954,10 @@
     full_ref,
     total_ref,
     grads_ref,
+    dense_ref,
+    slot_col_ref,
+    hidden_ref,
+    gate_ref,
     y_ref,
     acc,
     landing,
@@ -952,6 +977,7 @@
     y_sends,
     y_recvs,
     gets,
+    fills,
 ):
     tokens, width = hidden_ref.shape
     slots = y_ref.shape[0]
@@ -966,6 +992,10 @@
     def partner(axis, mask):
         return {axis: flip(place[axis], mask, size[axis])}
 
+    operands = [(dense_hbm, dense_ref), (slot_col_hbm, slot_col_ref), (hidden_hbm, hidden_ref), (gate_hbm, gate_ref)]
+    operands = [pltpu.make_async_copy(source, target, fills.at[i]) for i, (source, target) in enumerate(operands)]
+    for copy in operands:
+        copy.start()
     barrier = pltpu.get_barrier_semaphore()
     for axis, mask in plans[0]:
         pl.semaphore_signal(barrier, inc=1, device_id=partner(axis, mask), device_id_type=MESH)
@@ -1047,7 +1077,7 @@
             source = dense_ref if step == 0 else acc.at[(step - 1) % 2]
             land = landing.at[stream, pl.ds(offset, part)]
             copy = copy_to(
-                source.at[span(other, part)], land, sends.at[stream, step], recvs.at[stream, step], partner(axis, mask)
+                (dense_hbm if step == 0 else source).at[span(other, part)], land, sends.at[stream, step], recvs.at[stream, step], partner(axis, mask)
             )
             copy.start()
             copies.append((copy, kept, source))
@@ -1059,6 +1089,9 @@
         if step == 0:
             for copy in y_copies:
                 copy.start()
+        if step == 0:
+            for copy in operands:
+                copy.wait()
         trail.append((list(low), extent))
         for stream in range(STREAMS):
             copy, kept, source = copies[stream]
@@ -1119,8 +1152,11 @@
         copy.wait()
 
 
-def widen_kernel(hidden, dense_hbm, grads_hbm, total_ref, *rest):
-    outs, vecs, (low, high, gets, puts) = rest[:6], rest[6:10], rest[10:]
+AHEAD = 4
+
+
+def widen_kernel(hidden, dense_hbm, grads_hbm, total_ref, output_hbm, inputs_hbm, *rest):
+    outs, vecs, passed, (low, high, rows, gets, puts, moves) = rest[:6], rest[6:10], rest[10:12], rest[12:]
     width = dense_hbm.shape[1]
     jobs = []
     for block in range(hidden // width):
@@ -1130,14 +1166,25 @@
     for index in range(4):
         jobs.append((dense_hbm.at[pl.ds(index * width, width)], outs[index]))
     loads = [pltpu.make_async_copy(source, low.at[i], gets.at[i]) for i, (source, _) in enumerate(jobs)]
-    for load in loads:
+    for load in loads[:AHEAD]:
         load.start()
     for index, vec in enumerate(vecs):
         vec[...] = total_ref[index : index + 1, :].reshape(width)
+    taken = [pltpu.make_async_copy(source, rows.at[i], moves.at[i]) for i, source in enumerate((output_hbm, inputs_hbm))]
+    given = [pltpu.make_async_copy(rows.at[i], target, moves.at[i]) for i, target in enumerate(passed)]
     slots = high.shape[0]
     stores = []
     for index, (_, target) in enumerate(jobs):
         loads[index].wait()
+        if index + AHEAD < len(jobs):
+            loads[index + AHEAD].start()
+        if index == 1:
+            for copy in taken:
+                copy.start()
+        if index == 4:
+            for before, after in zip(taken, given):
+                before.wait()
+                after.start()
         if index >= slots:
             stores[index - slots].wait()
 
@@ -1147,8 +1194,8 @@
         each_rows(width, step)
         stores.append(pltpu.make_async_copy(high.at[index % slots], target, puts.at[index % slots]))
         stores[-1].start()
-    for store in stores[-slots:]:
-        store.wait()
+    for copy in stores[-slots:] + given:
+        copy.wait()
 
 
 def call(kernel, outs, in_specs, scratch, name, out_specs=None, collective=None, flops=10**9):
@@ -1203,8 +1250,9 @@
             shape((count * (main + spare), width), BF16),
             shape((HEADS // 2,) + prob_block, BF16),
         ],
-        [VMEM] * 12 + [ANY],
-        [
+        [VMEM] * 5 + [ANY] * 4 + [VMEM] * 3 + [ANY],
+        [pltpu.VMEM((width, width), BF16)] * 4
+        + [
             pltpu.VMEM((tokens, width), BF16),
             pltpu.VMEM((2,) + prob_block, BF16),
             dma(2),
@@ -1213,6 +1261,7 @@
             dma(depth_of(count)),
             dma(depth_of(count)),
             dma(2),
+            dma(4),
         ],
         "dense_forward",
         [VMEM] * 8 + [ANY] * 2,
@@ -1277,6 +1326,7 @@
         [SMEM] * 2 + [ANY] * 2 + [VMEM] * 2 + [ANY] * 16,
         [pltpu.VMEM(v.shape, v.dtype) for v in (inputs, cotangent, wq, wk, wv, wo, slot_col, normed, q, k, v, mixed, hidden)]
         + [
+            pltpu.VMEM((4 * width, width), BF16),
             pltpu.VMEM((count * main + BLK, width), BF16),
             pltpu.VMEM((count * spare, width), BF16),
             pltpu.VMEM((count * spare, width), BF16),
@@ -1306,9 +1356,10 @@
             dma(3, 2),
             dma(2),
             dma(2),
+            dma(4),
         ],
         "dense_backward",
-        [VMEM, VMEM, VMEM, ANY, ANY],
+        [VMEM, ANY, VMEM, ANY, ANY],
         3,
         5 * 10**10,
     )(group, domains, inputs, cotangent, g1, g2, wq, wk, wv, wo, slot_col, normed, q, k, v, mixed, probs, hidden, dx, late, y, grads)
@@ -1321,8 +1372,9 @@
     return call(
         functools.partial(finish_kernel, dp, count),
         [shape(hidden.shape, BF16), shape(dense.shape, BF16), shape(vec.shape, F32), shape((4 * piece.shape[0], width), BF16)],
-        [VMEM] * 5 + [ANY] * 3,
-        [
+        [ANY, VMEM] + [ANY] * 6,
+        [pltpu.VMEM(v.shape, v.dtype) for v in (dense, slot_col, hidden, gate)]
+        + [
             pltpu.VMEM(y_back.shape, BF16),
             pltpu.VMEM((2, rows, width), BF16),
             pltpu.VMEM((STREAMS, rows // STREAMS + 64, width), BF16),
@@ -1342,6 +1394,7 @@
             dma(count),
             dma(count),
             dma(count + 1),
+            dma(4),
         ],
         "finish",
         [VMEM, ANY, VMEM, ANY],
@@ -1349,23 +1402,29 @@
     )(dense, vec, slot_col, hidden, gate, y_back, y_rows, piece)
 
 
-def widen(hidden, dense, grads, total):
+def widen(hidden, dense, grads, total, output, grad_inputs):
     width = dense.shape[1]
     square = shape((width, width), F32)
     jobs = 2 * (hidden // width) + 4
+    rows = shape(output.shape, BF16)
     return call(
         functools.partial(widen_kernel, hidden),
-        [square] * 4 + [shape((width, hidden), F32), shape((hidden, width), F32)] + [shape((width,), F32)] * 4,
-        [ANY, ANY, VMEM],
+        [square] * 4
+        + [shape((width, hidden), F32), shape((hidden, width), F32)]
+        + [shape((width,), F32)] * 4
+        + [rows, rows],
+        [ANY, ANY, VMEM, ANY, ANY],
         [
             pltpu.VMEM((jobs, width, width), BF16),
             pltpu.VMEM((6, width, width), F32),
+            pltpu.VMEM((2,) + output.shape, BF16),
             dma(jobs),
             dma(6),
+            dma(2),
         ],
         "widen",
-        [ANY] * 6 + [VMEM] * 4,
-    )(dense, grads, total)
+        [ANY] * 6 + [VMEM] * 4 + [ANY] * 2,
+    )(dense, grads, total, output, grad_inputs)
 
 
 def local(
@@ -1409,7 +1468,9 @@
         normed, q, k, v, mixed, probs, hidden, dx_back, dx_late, y_rows, grads,
     )
     output, dense, vec, grads = finish(dp, count, dense, vec, slot_col, hidden, gate, y_back, y_rows, piece)
-    wq, wk, wv, wo, first, second, gain_a, shift_a, gain_b, shift_b = widen(expert_in.shape[2], dense, grads, vec)
+    wq, wk, wv, wo, first, second, gain_a, shift_a, gain_b, shift_b, output, grad_inputs = widen(
+        expert_in.shape[2], dense, grads, vec, output, grad_inputs
+    )
     return (output, grad_inputs, gain_a, shift_a, gain_b, shift_b, wq, wk, wv, wo, first[None], second[None])
 
 

time: 396 us -> 389 us (0.982)
  no operation moved by 1% of the time
where the time goes in v9:
time: 389 us
  Pallas kernels  387 us (99%)
    pallas_call x1, Pallas kernels, finish(): call(functools.partial(finish_kernel, dp, count), [shape(hidden.shape, BF...  115 us
    pallas_call x1, Pallas kernels, expert_block(): call(functools.partial(expert_kernel, count, main, spare, chunk), [rows,...  101 us
    pallas_call x1, Pallas kernels, backward(): call(functools.partial(backward_kernel, dp, count, main, spare), [shape((...  92 us
    pallas_call x1, Pallas kernels, forward(): call(functools.partial(forward_kernel, count, main, spare), [rows_low, ro...  54.1 us
    pallas_call x1, Pallas kernels, widen(): call(functools.partial(widen_kernel, hidden), [square] * 4 + [shape((widt...  17 us
    pallas_call x1, Pallas kernels, tables(): call(functools.partial(table_kernel, experts, main), [shape((slots, width...  8.25 us

profile of v9, /device:TPU:0, one launch (start us, length us, event | category | flops | bytes accessed | tf_op | source)
XLA Modules:
  0.0 388.7 jit_solution(3573356816053702379)
XLA Ops:
  1.3 8.2 %tables.1 = (bf16[1792,768]{1,0:T(8,128)(2,1)}, s32[1024,128]{1,0:T(8,128)}, s32[8,1024]{1,0:T(8,128)}) custom-call(s32[1,8]{1,0:T(1,128)} %counts_ref.3, s32[1]{0:T(128)S(6)} %copy.29.group_ref, s32[8]{0:T(128)} %domain_ref.3, s32[1,1024]{1,0:T(1,128)} %sort_ref.1, bf16[1024,768]{1,0:T(8,128)(2,1)} %cot_hbm.1), custom_call_target="tpu_custom_call" | custom-call | flops 1000000000 | bytes 10000000 | tf_op jit(solution)/shard_map/tables/pallas_call | solution.py:1225
  9.5 54.1 %dense_forward.1 = (bf16[1024,768]{1,0:T(8,128)(2,1)}, bf16[1024,768]{1,0:T(8,128)(2,1)}, bf16[1024,768]{1,0:T(8,128)(2,1)}, bf16[1024,768]{1,0:T(8,128)(2,1)}, ...) custom-call(bf16[1024,768]{1,0:T(8,128)(2,1)} %x_hbm.1, ...), custom_call_target="tpu_custom_call" | custom-call | flops 1000000000 | bytes 10000000 | tf_op jit(solution)/shard_map/dense_forward/pallas_call | solution.py:1239
  63.6 101.3 %expert.1 = (bf16[2048,768]{1,0:T(8,128)(2,1)}, bf16[1536,768]{1,0:T(8,128)(2,1)}, bf16[896,768]{1,0:T(8,128)(2,1)}, bf16[6144,768]{1,0:T(8,128)(2,1)}) custom-call(s32[1,8]{1,0:T(1,128)} %counts_ref.3, bf16[1792,768]{1,0:T(8,128)(2,1)} %get-tuple-element.60.send_ref, bf16[1792,768]{1,0:T(8,128)(2,1)} %get-tuple-element.52.cot_send_ref, ...), custom_call_target="tpu_custom_call" | custom-call | flops 1000000000 | bytes 10000000 | tf_op jit(solution)/shard_map/expert/pallas_call | solution.py:1279
  164.9 92.0 %dense_backward.1 = (bf16[1024,768]{1,0:T(8,128)(2,1)}, bf16[3072,768]{1,0:T(8,128)(2,1)}, f32[8,768]{1,0:T(8,128)}, bf16[1792,768]{1,0:T(8,128)(2,1)}, bf16[1536,768]{1,0:T(8,128)(2,1)}) custom-call(s32[1]{0:T(128)S(6)} %copy.29.group_ref, s32[8]{0:T(128)} %domain_ref.3, bf16[1024,768]{1,0:T(8,128)(2,1)} %x_hbm.1, bf16[1024,768]{1,0:T(8,128)(2,1)} %cot_hbm.1, ...), custom_call_target="tpu_custom_call" | custom-call | flops 49999998976 | bytes 10000000 | tf_op jit(solution)/shard_map/dense_backward/pallas_call | solution.py:1323
  257.0 114.5 %finish.1 = (bf16[1024,768]{1,0:T(8,128)(2,1)}, bf16[3072,768]{1,0:T(8,128)(2,1)}, f32[8,768]{1,0:T(8,128)}, bf16[6144,768]{1,0:T(8,128)(2,1)}) custom-call(bf16[3072,768]{1,0:T(8,128)(2,1)} %get-tuple-element.66.dense_hbm, f32[8,768]{1,0:T(8,128)} %get-tuple-element.67.vec_ref, s32[1024,128]{1,0:T(8,128)} %get-tuple-element.50.slot_col_ref.slot_col_hbm, ...), custom_call_target="tpu_custom_call" | custom-call | flops 1000000000 | bytes 10000000 | tf_op jit(solution)/shard_map/finish/pallas_call | solution.py:1372
  371.5 17.0 %widen.1 = (f32[768,768]{1,0:T(8,128)}, f32[768,768]{1,0:T(8,128)}, f32[768,768]{1,0:T(8,128)}, f32[768,768]{1,0:T(8,128)}, f32[768,3072]{1,0:T(8,128)}, /*index...) custom-call(bf16[3072,768]{1,0:T(8,128)(2,1)} %get-tuple-element.71., ...), custom_call_target="tpu_custom_call" | custom-call | flops 1000000000 | bytes 10000000 | tf_op jit(solution)/shard_map/widen/pallas_call | solution.py:1410

commit v10 on v9

--- a/solution.py
+++ b/solution.py
@@ -784,7 +784,7 @@
     for copy in lates:
         copy.wait()
     sum_y(depth - 1).start()
-    for copy in copies:
+    for copy in copies[count // 2 - 1 :] + copies[: count // 2 - 1]:
         copy.start()
     for copy in operands:
         copy.wait()
@@ -838,6 +838,11 @@
         def _():
             for stream in range(2):
                 add_one(stream, 1)
+
+        @pl.when(pair == 5)
+        def _():
+            settle(sum_y(depth - 2), spare_y, y_land, depth - 2)
+            sum_y(depth - 3).start()
 
         load_probs(pair).wait()
         base = pl.multiple_of(pair * 128, 128)
@@ -908,7 +913,7 @@
         start = bits[1 - stream] * quarter
         sum_rows(kept.at[stream, span(start, quarter)], land_two.at[stream], quarter)
         store_piece(stream).start()
-    for step in reversed(range(depth - 1)):
+    for step in reversed(range(depth - 2)):
         settle(sum_y(step), spare_y, y_land, step)
         if step:
             sum_y(step - 1).start()
@@ -1115,6 +1120,7 @@
         extent = part
         offset += part
 
+    writes = []
     for step in reversed(range(halvings)):
         origins, whole = trail[step]
         copies = []
@@ -1140,19 +1146,26 @@
             copies[stream].wait()
             low[stream] = origins[stream]
         extent = whole
+        if step == 1:
+            for stream in range(STREAMS):
+                held = span(low[stream], extent)
+                writes.append(pltpu.make_async_copy(full.at[held], full_ref.at[held], put.at[0, stream]))
+                writes[-1].start()
     advance(len(pending))
-    write = pltpu.make_async_copy(full, full_ref, put)
-    write.start()
+    for stream in range(STREAMS):
+        held = span(stream * rows + (1 - side("expert", 1)) * (rows // 2), rows // 2)
+        writes.append(pltpu.make_async_copy(full.at[held], full_ref.at[held], put.at[1, stream]))
+        writes[-1].start()
     for index in range(3 * CHUNKS):
         for stream in range(2):
             if index >= CHUNKS:
                 unit(index, stream).wait_recv()
             unit(index, stream).wait_send()
-    for copy in mine + [write]:
+    for copy in mine + writes:
         copy.wait()
 
 
-AHEAD = 4
+AHEAD = 6
 
 
 def widen_kernel(hidden, dense_hbm, grads_hbm, total_ref, output_hbm, inputs_hbm, *rest):
@@ -1387,7 +1400,7 @@
             dma(STREAMS, steps),
             dma(steps),
             dma(steps),
-            dma(),
+            dma(2, STREAMS),
             dma(3 * CHUNKS, 2),
             dma(3 * CHUNKS, 2),
             dma(2),

time: 389 us -> 386 us (level)
  no operation moved by 1% of the time
where the time goes in v10:
time: 386 us; the launch traced here: 385 us
  Pallas kernels  384 us (99%)
    pallas_call x1, Pallas kernels, finish(): call(functools.partial(finish_kernel, dp, count), [shape(hidden.shape, BF...  114 us
    pallas_call x1, Pallas kernels, expert_block(): call(functools.partial(expert_kernel, count, main, spare, chunk), [rows,...  101 us
    pallas_call x1, Pallas kernels, backward(): call(functools.partial(backward_kernel, dp, count, main, spare), [shape((...  89.1 us
    pallas_call x1, Pallas kernels, forward(): call(functools.partial(forward_kernel, count, main, spare), [rows_low, ro...  54.1 us
    pallas_call x1, Pallas kernels, widen(): call(functools.partial(widen_kernel, hidden), [square] * 4 + [shape((widt...  16.8 us
    pallas_call x1, Pallas kernels, tables(): call(functools.partial(table_kernel, experts, main), [shape((slots, width...  8.25 us

profile of v10, /device:TPU:0, one launch (start us, length us, event | category | flops | bytes accessed | tf_op | source)
XLA Modules:
  0.0 385.2 jit_solution(16242263303869774249)
XLA Ops:
  1.3 8.2 %tables.1 = (bf16[1792,768]{1,0:T(8,128)(2,1)}, s32[1024,128]{1,0:T(8,128)}, s32[8,1024]{1,0:T(8,128)}) custom-call(s32[1,8]{1,0:T(1,128)} %counts_ref.3, s32[1]{0:T(128)S(6)} %copy.29.group_ref, s32[8]{0:T(128)} %domain_ref.3, s32[1,1024]{1,0:T(1,128)} %sort_ref.1, bf16[1024,768]{1,0:T(8,128)(2,1)} %cot_hbm.1), custom_call_target="tpu_custom_call" | custom-call | flops 1000000000 | bytes 10000000 | tf_op jit(solution)/shard_map/tables/pallas_call | solution.py:1238
  9.5 54.1 %dense_forward.1 = (bf16[1024,768]{1,0:T(8,128)(2,1)}, bf16[1024,768]{1,0:T(8,128)(2,1)}, bf16[1024,768]{1,0:T(8,128)(2,1)}, bf16[1024,768]{1,0:T(8,128)(2,1)}, ...) custom-call(bf16[1024,768]{1,0:T(8,128)(2,1)} %x_hbm.1, ...), custom_call_target="tpu_custom_call" | custom-call | flops 1000000000 | bytes 10000000 | tf_op jit(solution)/shard_map/dense_forward/pallas_call | solution.py:1252
  63.6 101.3 %expert.1 = (bf16[2048,768]{1,0:T(8,128)(2,1)}, bf16[1536,768]{1,0:T(8,128)(2,1)}, bf16[896,768]{1,0:T(8,128)(2,1)}, bf16[6144,768]{1,0:T(8,128)(2,1)}) custom-call(s32[1,8]{1,0:T(1,128)} %counts_ref.3, bf16[1792,768]{1,0:T(8,128)(2,1)} %get-tuple-element.60.send_ref, bf16[1792,768]{1,0:T(8,128)(2,1)} %get-tuple-element.52.cot_send_ref, ...), custom_call_target="tpu_custom_call" | custom-call | flops 1000000000 | bytes 10000000 | tf_op jit(solution)/shard_map/expert/pallas_call | solution.py:1292
  164.9 89.1 %dense_backward.1 = (bf16[1024,768]{1,0:T(8,128)(2,1)}, bf16[3072,768]{1,0:T(8,128)(2,1)}, f32[8,768]{1,0:T(8,128)}, bf16[1792,768]{1,0:T(8,128)(2,1)}, bf16[1536,768]{1,0:T(8,128)(2,1)}) custom-call(s32[1]{0:T(128)S(6)} %copy.29.group_ref, s32[8]{0:T(128)} %domain_ref.3, bf16[1024,768]{1,0:T(8,128)(2,1)} %x_hbm.1, bf16[1024,768]{1,0:T(8,128)(2,1)} %cot_hbm.1, ...), custom_call_target="tpu_custom_call" | custom-call | flops 49999998976 | bytes 10000000 | tf_op jit(solution)/shard_map/dense_backward/pallas_call | solution.py:1336
  254.0 114.2 %finish.1 = (bf16[1024,768]{1,0:T(8,128)(2,1)}, bf16[3072,768]{1,0:T(8,128)(2,1)}, f32[8,768]{1,0:T(8,128)}, bf16[6144,768]{1,0:T(8,128)(2,1)}) custom-call(bf16[3072,768]{1,0:T(8,128)(2,1)} %get-tuple-element.66.dense_hbm, f32[8,768]{1,0:T(8,128)} %get-tuple-element.67.vec_ref, s32[1024,128]{1,0:T(8,128)} %get-tuple-element.50.slot_col_ref.slot_col_hbm, ...), custom_call_target="tpu_custom_call" | custom-call | flops 1000000000 | bytes 10000000 | tf_op jit(solution)/shard_map/finish/pallas_call | solution.py:1385
  368.2 16.8 %widen.1 = (f32[768,768]{1,0:T(8,128)}, f32[768,768]{1,0:T(8,128)}, f32[768,768]{1,0:T(8,128)}, f32[768,768]{1,0:T(8,128)}, f32[768,3072]{1,0:T(8,128)}, /*index...) custom-call(bf16[3072,768]{1,0:T(8,128)(2,1)} %get-tuple-element.71., ...), custom_call_target="tpu_custom_call" | custom-call | flops 1000000000 | bytes 10000000 | tf_op jit(solution)/shard_map/widen/pallas_call | solution.py:1423

commit v11 on v10

--- a/solution.py
+++ b/solution.py
@@ -171,7 +171,7 @@
         send_ref[pl.ds(base, BLK), :] = nn(pick, rows_ref[...]).astype(BF16)
         return carry
 
-    lax.fori_loop(0, slots // BLK, step, 0)
+    lax.fori_loop(0, slots // BLK, step, 0, unroll=True)
 
 
 def table_kernel(experts, main, counts_ref, group_ref, domain_ref, sort_ref, cot_ref, send_ref, slot_col_ref, slot_row_ref, scaled):
@@ -280,7 +280,7 @@
 
     for copy in weights:
         copy.wait()
-    lax.fori_loop(0, blocks, project, 0)
+    lax.fori_loop(0, blocks, project, 0, unroll=2)
 
     keep = iota((BLK, BLK), 0) <= iota((BLK, BLK), 1)
 
@@ -330,7 +330,7 @@
         gate_ref[rows, :] = jnp.broadcast_to(jax.nn.sigmoid(logit), (BLK, 128))
         return carry
 
-    lax.fori_loop(0, blocks, finish, 0)
+    lax.fori_loop(0, blocks, finish, 0, unroll=2)
     pack_rows(slot_row_ref[0:1, :], routed, send_ref)
     for copy in mine + [keep_probs(HEADS // 2 - 2), keep_probs(HEADS // 2 - 1)]:
         copy.wait()

time: 386 us -> 384 us (level)
  no operation moved by 1% of the time
where the time goes in v11:
time: 384 us
  Pallas kernels  382 us (99%)
    pallas_call x1, Pallas kernels, finish(): call(functools.partial(finish_kernel, dp, count), [shape(hidden.shape, BF...  114 us
    pallas_call x1, Pallas kernels, expert_block(): call(functools.partial(expert_kernel, count, main, spare, chunk), [rows,...  104 us
    pallas_call x1, Pallas kernels, backward(): call(functools.partial(backward_kernel, dp, count, main, spare), [shape((...  89.1 us
    pallas_call x1, Pallas kernels, forward(): call(functools.partial(forward_kernel, count, main, spare), [rows_low, ro...  51.7 us
    pallas_call x1, Pallas kernels, widen(): call(functools.partial(widen_kernel, hidden), [square] * 4 + [shape((widt...  16.8 us

profile of v11, /device:TPU:0, one launch (start us, length us, event | category | flops | bytes accessed | tf_op | source)
XLA Modules:
  0.0 383.8 jit_solution(15079558433326787097)
XLA Ops:
  1.3 6.8 %tables.1 = (bf16[1792,768]{1,0:T(8,128)(2,1)}, s32[1024,128]{1,0:T(8,128)}, s32[8,1024]{1,0:T(8,128)}) custom-call(s32[1,8]{1,0:T(1,128)} %counts_ref.3, s32[1]{0:T(128)S(6)} %copy.29.group_ref, s32[8]{0:T(128)} %domain_ref.3, s32[1,1024]{1,0:T(1,128)} %sort_ref.1, bf16[1024,768]{1,0:T(8,128)(2,1)} %cot_hbm.1), custom_call_target="tpu_custom_call" | custom-call | flops 1000000000 | bytes 10000000 | tf_op jit(solution)/shard_map/tables/pallas_call | solution.py:1238
  8.1 51.7 %dense_forward.1 = (bf16[1024,768]{1,0:T(8,128)(2,1)}, bf16[1024,768]{1,0:T(8,128)(2,1)}, bf16[1024,768]{1,0:T(8,128)(2,1)}, bf16[1024,768]{1,0:T(8,128)(2,1)}, ...) custom-call(bf16[1024,768]{1,0:T(8,128)(2,1)} %x_hbm.1, ...), custom_call_target="tpu_custom_call" | custom-call | flops 1000000000 | bytes 10000000 | tf_op jit(solution)/shard_map/dense_forward/pallas_call | solution.py:1252
  59.8 103.7 %expert.1 = (bf16[2048,768]{1,0:T(8,128)(2,1)}, bf16[1536,768]{1,0:T(8,128)(2,1)}, bf16[896,768]{1,0:T(8,128)(2,1)}, bf16[6144,768]{1,0:T(8,128)(2,1)}) custom-call(s32[1,8]{1,0:T(1,128)} %counts_ref.3, bf16[1792,768]{1,0:T(8,128)(2,1)} %get-tuple-element.60.send_ref, bf16[1792,768]{1,0:T(8,128)(2,1)} %get-tuple-element.52.cot_send_ref, ...), custom_call_target="tpu_custom_call" | custom-call | flops 1000000000 | bytes 10000000 | tf_op jit(solution)/shard_map/expert/pallas_call | solution.py:1292
  163.5 89.1 %dense_backward.1 = (bf16[1024,768]{1,0:T(8,128)(2,1)}, bf16[3072,768]{1,0:T(8,128)(2,1)}, f32[8,768]{1,0:T(8,128)}, bf16[1792,768]{1,0:T(8,128)(2,1)}, bf16[1536,768]{1,0:T(8,128)(2,1)}) custom-call(s32[1]{0:T(128)S(6)} %copy.29.group_ref, s32[8]{0:T(128)} %domain_ref.3, bf16[1024,768]{1,0:T(8,128)(2,1)} %x_hbm.1, bf16[1024,768]{1,0:T(8,128)(2,1)} %cot_hbm.1, ...), custom_call_target="tpu_custom_call" | custom-call | flops 49999998976 | bytes 10000000 | tf_op jit(solution)/shard_map/dense_backward/pallas_call | solution.py:1336
  252.6 114.2 %finish.1 = (bf16[1024,768]{1,0:T(8,128)(2,1)}, bf16[3072,768]{1,0:T(8,128)(2,1)}, f32[8,768]{1,0:T(8,128)}, bf16[6144,768]{1,0:T(8,128)(2,1)}) custom-call(bf16[3072,768]{1,0:T(8,128)(2,1)} %get-tuple-element.66.dense_hbm, f32[8,768]{1,0:T(8,128)} %get-tuple-element.67.vec_ref, s32[1024,128]{1,0:T(8,128)} %get-tuple-element.50.slot_col_ref.slot_col_hbm, ...), custom_call_target="tpu_custom_call" | custom-call | flops 1000000000 | bytes 10000000 | tf_op jit(solution)/shard_map/finish/pallas_call | solution.py:1385
  366.8 16.8 %widen.1 = (f32[768,768]{1,0:T(8,128)}, f32[768,768]{1,0:T(8,128)}, f32[768,768]{1,0:T(8,128)}, f32[768,768]{1,0:T(8,128)}, f32[768,3072]{1,0:T(8,128)}, /*index...) custom-call(bf16[3072,768]{1,0:T(8,128)(2,1)} %get-tuple-element.71., ...), custom_call_target="tpu_custom_call" | custom-call | flops 1000000000 | bytes 10000000 | tf_op jit(solution)/shard_map/widen/pallas_call | solution.py:1423

commit v12 on v11

--- a/solution.py
+++ b/solution.py
@@ -544,9 +544,9 @@
         pieces.append((acc2.at[pl.ds(first, width), :], grads_ref.at[pl.ds(hidden + first, width)]))
     writes = []
     for index, (piece, target) in enumerate(pieces):
-        slot = index % 2
-        if index >= 2:
-            writes[index - 2].wait()
+        slot = index % 4
+        if index >= 4:
+            writes[index - 4].wait()
 
         def narrow(part):
             stage[slot, part, :] = piece[part, :].astype(BF16)
@@ -555,7 +555,7 @@
         write = pltpu.make_async_copy(stage.at[slot], target, stage_sems.at[slot])
         write.start()
         writes.append(write)
-    for write in writes[-2:]:
+    for write in writes[-4:]:
         write.wait()
     mine_out().wait()
     tail.wait()
@@ -1307,7 +1307,7 @@
             keep,
             keep,
             keep,
-            pltpu.VMEM((2, width, width), BF16),
+            pltpu.VMEM((4, width, width), BF16),
             dma(4),
             dma(count),
             dma(count),
@@ -1319,7 +1319,7 @@
             dma(count),
             dma(2),
             dma(slots // BLK),
-            dma(2),
+            dma(4),
         ],
         "expert",
         [ANY] * 4,

time: 384 us -> 383 us (level)
  no operation moved by 1% of the time
where the time goes in v12:
time: 383 us; the launch traced here: 382 us
  Pallas kernels  381 us (99%)
    pallas_call x1, Pallas kernels, finish(): call(functools.partial(finish_kernel, dp, count), [shape(hidden.shape, BF...  114 us
    pallas_call x1, Pallas kernels, expert_block(): call(functools.partial(expert_kernel, count, main, spare, chunk), [rows,...  102 us
    pallas_call x1, Pallas kernels, backward(): call(functools.partial(backward_kernel, dp, count, main, spare), [shape((...  89.1 us
    pallas_call x1, Pallas kernels, forward(): call(functools.partial(forward_kernel, count, main, spare), [rows_low, ro...  51.7 us
    pallas_call x1, Pallas kernels, widen(): call(functools.partial(widen_kernel, hidden), [square] * 4 + [shape((widt...  16.8 us

profile of v12, /device:TPU:0, one launch (start us, length us, event | category | flops | bytes accessed | tf_op | source)
XLA Modules:
  0.0 382.2 jit_solution(14065473519458748061)
XLA Ops:
  1.3 6.8 %tables.1 = (bf16[1792,768]{1,0:T(8,128)(2,1)}, s32[1024,128]{1,0:T(8,128)}, s32[8,1024]{1,0:T(8,128)}) custom-call(s32[1,8]{1,0:T(1,128)} %counts_ref.3, s32[1]{0:T(128)S(6)} %copy.29.group_ref, s32[8]{0:T(128)} %domain_ref.3, s32[1,1024]{1,0:T(1,128)} %sort_ref.1, bf16[1024,768]{1,0:T(8,128)(2,1)} %cot_hbm.1), custom_call_target="tpu_custom_call" | custom-call | flops 1000000000 | bytes 10000000 | tf_op jit(solution)/shard_map/tables/pallas_call | solution.py:1238
  8.1 51.7 %dense_forward.1 = (bf16[1024,768]{1,0:T(8,128)(2,1)}, bf16[1024,768]{1,0:T(8,128)(2,1)}, bf16[1024,768]{1,0:T(8,128)(2,1)}, bf16[1024,768]{1,0:T(8,128)(2,1)}, ...) custom-call(bf16[1024,768]{1,0:T(8,128)(2,1)} %x_hbm.1, ...), custom_call_target="tpu_custom_call" | custom-call | flops 1000000000 | bytes 10000000 | tf_op jit(solution)/shard_map/dense_forward/pallas_call | solution.py:1252
  59.8 102.1 %expert.1 = (bf16[2048,768]{1,0:T(8,128)(2,1)}, bf16[1536,768]{1,0:T(8,128)(2,1)}, bf16[896,768]{1,0:T(8,128)(2,1)}, bf16[6144,768]{1,0:T(8,128)(2,1)}) custom-call(s32[1,8]{1,0:T(1,128)} %counts_ref.3, bf16[1792,768]{1,0:T(8,128)(2,1)} %get-tuple-element.60.send_ref, bf16[1792,768]{1,0:T(8,128)(2,1)} %get-tuple-element.52.cot_send_ref, ...), custom_call_target="tpu_custom_call" | custom-call | flops 1000000000 | bytes 10000000 | tf_op jit(solution)/shard_map/expert/pallas_call | solution.py:1292
  162.0 89.1 %dense_backward.1 = (bf16[1024,768]{1,0:T(8,128)(2,1)}, bf16[3072,768]{1,0:T(8,128)(2,1)}, f32[8,768]{1,0:T(8,128)}, bf16[1792,768]{1,0:T(8,128)(2,1)}, bf16[1536,768]{1,0:T(8,128)(2,1)}) custom-call(s32[1]{0:T(128)S(6)} %copy.29.group_ref, s32[8]{0:T(128)} %domain_ref.3, bf16[1024,768]{1,0:T(8,128)(2,1)} %x_hbm.1, bf16[1024,768]{1,0:T(8,128)(2,1)} %cot_hbm.1, ...), custom_call_target="tpu_custom_call" | custom-call | flops 49999998976 | bytes 10000000 | tf_op jit(solution)/shard_map/dense_backward/pallas_call | solution.py:1336
  251.0 114.2 %finish.1 = (bf16[1024,768]{1,0:T(8,128)(2,1)}, bf16[3072,768]{1,0:T(8,128)(2,1)}, f32[8,768]{1,0:T(8,128)}, bf16[6144,768]{1,0:T(8,128)(2,1)}) custom-call(bf16[3072,768]{1,0:T(8,128)(2,1)} %get-tuple-element.66.dense_hbm, f32[8,768]{1,0:T(8,128)} %get-tuple-element.67.vec_ref, s32[1024,128]{1,0:T(8,128)} %get-tuple-element.50.slot_col_ref.slot_col_hbm, ...), custom_call_target="tpu_custom_call" | custom-call | flops 1000000000 | bytes 10000000 | tf_op jit(solution)/shard_map/finish/pallas_call | solution.py:1385
  365.2 16.8 %widen.1 = (f32[768,768]{1,0:T(8,128)}, f32[768,768]{1,0:T(8,128)}, f32[768,768]{1,0:T(8,128)}, f32[768,768]{1,0:T(8,128)}, f32[768,3072]{1,0:T(8,128)}, /*index...) custom-call(bf16[3072,768]{1,0:T(8,128)(2,1)} %get-tuple-element.71., ...), custom_call_target="tpu_custom_call" | custom-call | flops 1000000000 | bytes 10000000 | tf_op jit(solution)/shard_map/widen/pallas_call | solution.py:1423
